TPU v7x, 32 devices: a whole 2x2x4 slice. The times are simulated.
32 devices in a mesh: dp: 8 (over z, y), fsdp: 4 (over x, core).
Axes of the slice: x: 2, y: 2, z: 4, core: 2. Of those that a mesh axis runs over, the one named last changes fastest.
Arguments:
- inputs: bfloat16 [16, 1024, 1024], P('dp', 'fsdp'), may hold values from -6 to 6
- teacher: bfloat16 [16, 1024, 1024], P('dp', 'fsdp'), may hold values from -16 to 16
- valid_mask: int32 [16, 1024], P('dp', 'fsdp'), may hold values from 0 to 1, as said below
- time_steps: int32 [16], P('dp'), may hold values from 0 to 999
- qkv_weight: float32 [1024, 3072], P(('dp', 'fsdp')), may hold values from -0.1875 to 0.1875
- out_weight: float32 [1024, 1024], P(('dp', 'fsdp')), may hold values from -4 to 4
- up_weight: float32 [1024, 4096], P(('dp', 'fsdp')), may hold values from -0.1875 to 0.1875
- down_weight: float32 [4096, 1024], P(('dp', 'fsdp')), may hold values from -0.09375 to 0.09375
- time_weight: float32 [256, 2048], P(('dp', 'fsdp')), may hold values from -0.375 to 0.375
- time_bias: float32 [2048], P(('dp', 'fsdp')), may hold values from -4 to 4
- norm_gain: float32 [1024], P(('dp', 'fsdp')), may hold values from 0.25 to 1.75
- norm_bias: float32 [1024], P(('dp', 'fsdp')), may hold values from -4 to 4
- up_bias: float32 [4096], P(('dp', 'fsdp')), may hold values from -6 to 6
- down_bias: float32 [1024], P(('dp', 'fsdp')), may hold values from -4 to 4
Outputs:
- activations: bfloat16 [16, 1024, 1024], P('dp', 'fsdp')
- loss: float32 [1], replicated
- input_grad: float32 [16, 1024, 1024], P('dp', 'fsdp')
- qkv_weight_grad: float32 [1024, 3072], P(('dp', 'fsdp'))
- out_weight_grad: float32 [1024, 1024], P(('dp', 'fsdp'))
- up_weight_grad: float32 [1024, 4096], P(('dp', 'fsdp'))
- down_weight_grad: float32 [4096, 1024], P(('dp', 'fsdp'))
- time_weight_grad: float32 [256, 2048], P(('dp', 'fsdp'))
- time_bias_grad: float32 [2048], P(('dp', 'fsdp'))
- norm_gain_grad: float32 [1024], P(('dp', 'fsdp'))
- norm_bias_grad: float32 [1024], P(('dp', 'fsdp'))
- up_bias_grad: float32 [4096], P(('dp', 'fsdp'))
- down_bias_grad: float32 [1024], P(('dp', 'fsdp'))
Inputs may be any that keep to these rules, and one draw needn't show every extreme that they name: `valid_mask`: 1 marks a token whose output counts in the loss; the first token of every sequence counts.
All inputs are finite; a program needn't handle non-finite values.
Results may differ from a plain program's by a relative error of at most 0.012.
The roundings to bfloat16 on the way count: a program that leaves them out, or rounds other values in their place, can miss the bound.
Values may be sent and summed in bfloat16 or wider, within the bound.
No kernel may reach another device: no remote copies, remote signals or barrier semaphores. Data moves between devices by JAX's collectives and lax.ppermute only.
A program may use at most 192 MiB of HBM per device.

v0:
```python
from functools import partial
import math

import jax
import jax.numpy as jnp
from jax import lax
from jax.sharding import PartitionSpec as P

HD = 64
TE = 256
MB = 2


highest = lax.Precision.HIGHEST
epsilon = 1e-05


def rotation(positions):
    half_width = HD // 2
    spread = jnp.exp(jnp.arange(half_width, dtype=jnp.float32) * (-2.0 * math.log(10000.0) / HD))
    angles = positions[:, None] * spread[None, :]
    return (jnp.cos(angles)[:, None, :], jnp.sin(angles)[:, None, :])


def rotate(values, cosine, sine_part):
    half_width = HD // 2
    first_half = values[..., :half_width]
    second_half = values[..., half_width:]
    return jnp.concatenate(
        [
            first_half * cosine - second_half * sine_part,
            second_half * cosine + first_half * sine_part,
        ],
        axis=-1,
    )


def unrotate(values, cosine, sine_part):
    half_width = HD // 2
    first_half = values[..., :half_width]
    second_half = values[..., half_width:]
    return jnp.concatenate(
        [
            first_half * cosine + second_half * sine_part,
            second_half * cosine - first_half * sine_part,
        ],
        axis=-1,
    )


def time_features(time_steps):
    half_width = TE // 2
    spread = jnp.exp(jnp.arange(half_width, dtype=jnp.float32) * (-math.log(10000.0) / half_width))
    angles = time_steps.astype(jnp.float32)[:, None] * spread[None, :]
    return jnp.concatenate([jnp.sin(angles), jnp.cos(angles)], axis=-1)


def normalize(values):
    centre = values - jnp.mean(values, axis=-1, keepdims=True)
    return centre * lax.rsqrt(jnp.mean(centre * centre, axis=-1, keepdims=True) + epsilon)


def first_norm(source, condition):
    width = source.shape[-1]
    return normalize(source) * (1.0 + condition[:, None, :width]) + condition[:, None, width:]


def second_norm(middle, gain_value, shift_value):
    return normalize(middle) * gain_value + shift_value


def attend(queries, keys_in, values_in):
    scores = (
        jnp.einsum("sqhd,skhd->shqk", queries, keys_in, preferred_element_type=jnp.float32) * 0.125
    )
    log_total = jax.nn.logsumexp(scores, axis=-1, keepdims=True)
    probs = jnp.exp(scores - log_total).astype(jnp.bfloat16)
    mixture = jnp.einsum("shqk,skhd->sqhd", probs, values_in, preferred_element_type=jnp.float32)
    return (mixture, log_total)


def attend_back(queries, keys_in, values_in, log_total, mixture_grad):
    again = (
        jnp.einsum("sqhd,skhd->shqk", queries, keys_in, preferred_element_type=jnp.float32) * 0.125
    )
    prob_full = jnp.exp(again - log_total)
    prob_low = prob_full.astype(jnp.bfloat16)
    prob_grad = jnp.einsum(
        "sqhd,skhd->shqk", mixture_grad, values_in, preferred_element_type=jnp.float32
    )
    score_grad = (
        prob_full * (prob_grad - jnp.sum(prob_full * prob_grad, axis=-1, keepdims=True))
    ).astype(jnp.bfloat16)
    query_grad = (
        jnp.einsum("shqk,skhd->sqhd", score_grad, keys_in, preferred_element_type=jnp.float32)
        * 0.125
    )
    key_part = (
        jnp.einsum("shqk,sqhd->skhd", score_grad, queries, preferred_element_type=jnp.float32)
        * 0.125
    )
    value_part = jnp.einsum(
        "shqk,sqhd->skhd", prob_low, mixture_grad, preferred_element_type=jnp.float32
    )
    return (query_grad, key_part, value_part)


def body(
    inputs,
    teacher,
    valid_mask,
    time_steps,
    qkv_weight,
    out_weight,
    up_weight,
    down_weight,
    time_weight,
    time_bias,
    norm_gain,
    norm_bias,
    up_bias,
    down_bias,
):
    fsdp_size = lax.axis_size("fsdp")
    local_len = inputs.shape[1]
    width = inputs.shape[2]
    heads = width // HD
    seq_len = local_len * fsdp_size
    per_batch = inputs.shape[0] // MB
    token_total = lax.axis_size("dp") * inputs.shape[0] * seq_len
    loss_scale = token_total * width / 2
    positions = (
        lax.axis_index("fsdp") * local_len + jnp.arange(local_len, dtype=jnp.int32)
    ).astype(jnp.float32)
    cosine, sine_part = rotation(positions)
    valid_marks = valid_mask.astype(jnp.float32)
    valid_total = lax.psum(jnp.sum(valid_marks), ("dp", "fsdp"))
    factor = loss_scale / (valid_total * width)
    qkv_low = qkv_weight.astype(jnp.bfloat16)
    out_low = out_weight.astype(jnp.bfloat16)
    up_low = up_weight.astype(jnp.bfloat16)
    down_low = down_weight.astype(jnp.bfloat16)
    time_low = time_weight.astype(jnp.bfloat16)
    time_bias_low = time_bias.astype(jnp.bfloat16)
    gain_low = norm_gain.astype(jnp.bfloat16)
    shift_low = norm_bias.astype(jnp.bfloat16)
    up_bias_low = up_bias.astype(jnp.bfloat16)
    down_bias_low = down_bias.astype(jnp.bfloat16)
    outputs = []
    input_grads = []
    loss_part = jnp.zeros((), jnp.float32)
    totals = None
    for batch_index in range(MB):
        start = batch_index * per_batch
        source = inputs[start : start + per_batch].astype(jnp.float32)
        target = teacher[start : start + per_batch].astype(jnp.float32)
        batch_marks = valid_marks[start : start + per_batch]
        features = time_features(time_steps[start : start + per_batch]).astype(jnp.bfloat16)
        ahead = (
            lax.all_gather(qkv_low, ("dp", "fsdp"), axis=0, tiled=True),
            lax.all_gather(out_low, ("dp", "fsdp"), axis=0, tiled=True),
            lax.all_gather(up_low, ("dp", "fsdp"), axis=0, tiled=True),
            lax.all_gather(down_low, ("dp", "fsdp"), axis=0, tiled=True),
            lax.all_gather(time_low, ("dp", "fsdp"), axis=0, tiled=True),
            lax.all_gather(time_bias_low, ("dp", "fsdp"), axis=0, tiled=True),
            lax.all_gather(gain_low, ("dp", "fsdp"), axis=0, tiled=True),
            lax.all_gather(shift_low, ("dp", "fsdp"), axis=0, tiled=True),
            lax.all_gather(up_bias_low, ("dp", "fsdp"), axis=0, tiled=True),
            lax.all_gather(down_bias_low, ("dp", "fsdp"), axis=0, tiled=True),
        )
        (
            qkv_full,
            out_full,
            up_full,
            down_full,
            time_full,
            time_bias_full,
            gain_full,
            shift_full,
            up_bias_full,
            down_bias_full,
        ) = ahead
        condition = jnp.dot(
            features, time_full, preferred_element_type=jnp.float32
        ) + time_bias_full.astype(jnp.float32)
        hidden = first_norm(source, condition).astype(jnp.bfloat16)
        project = jnp.einsum("sqd,de->sqe", hidden, qkv_full, preferred_element_type=jnp.float32)
        query_rot = rotate(
            project[..., :width].reshape(per_batch, local_len, heads, HD), cosine, sine_part
        ).astype(jnp.bfloat16)
        key_rot = (
            rotate(
                project[..., width : 2 * width].reshape(per_batch, local_len, heads, HD),
                cosine,
                sine_part,
            )
            .astype(jnp.bfloat16)
            .reshape(per_batch, local_len, width)
        )
        value_low = project[..., 2 * width :].astype(jnp.bfloat16)
        key_all, value_all = (
            lax.all_gather(key_rot, "fsdp", axis=1, tiled=True),
            lax.all_gather(value_low, "fsdp", axis=1, tiled=True),
        )
        key_heads = key_all.reshape(per_batch, seq_len, heads, HD)
        value_heads = value_all.reshape(per_batch, seq_len, heads, HD)
        mixture_heads, log_total = attend(query_rot, key_heads, value_heads)
        mixture = mixture_heads.astype(jnp.bfloat16).reshape(per_batch, local_len, width)
        middle = source + jnp.einsum(
            "sqd,de->sqe", mixture, out_full, preferred_element_type=jnp.float32
        )
        gain_value = gain_full.astype(jnp.float32)
        shift_value = shift_full.astype(jnp.float32)
        second = second_norm(middle, gain_value, shift_value).astype(jnp.bfloat16)
        inner_sum = jnp.einsum(
            "sqd,df->sqf", second, up_full, preferred_element_type=jnp.float32
        ) + up_bias_full.astype(jnp.float32)
        active = jax.nn.gelu(inner_sum, approximate=False).astype(jnp.bfloat16)
        result = middle + (
            jnp.einsum("sqf,fd->sqd", active, down_full, preferred_element_type=jnp.float32)
            + down_bias_full.astype(jnp.float32)
        )
        differ = result - target
        loss_part = loss_part + jnp.sum(batch_marks[:, :, None] * differ * differ)
        outputs.append(result.astype(jnp.bfloat16))
        result_grad = 2.0 * batch_marks[:, :, None] * differ * factor
        behind = (
            lax.all_gather(qkv_low, ("dp", "fsdp"), axis=0, tiled=True),
            lax.all_gather(out_low, ("dp", "fsdp"), axis=0, tiled=True),
            lax.all_gather(up_low, ("dp", "fsdp"), axis=0, tiled=True),
            lax.all_gather(down_low, ("dp", "fsdp"), axis=0, tiled=True),
            lax.all_gather(time_low, ("dp", "fsdp"), axis=0, tiled=True),
            lax.all_gather(time_bias_low, ("dp", "fsdp"), axis=0, tiled=True),
            lax.all_gather(gain_low, ("dp", "fsdp"), axis=0, tiled=True),
            lax.all_gather(shift_low, ("dp", "fsdp"), axis=0, tiled=True),
            lax.all_gather(up_bias_low, ("dp", "fsdp"), axis=0, tiled=True),
            lax.all_gather(down_bias_low, ("dp", "fsdp"), axis=0, tiled=True),
        )
        (
            qkv_full,
            out_full,
            up_full,
            down_full,
            time_full,
            time_bias_full,
            gain_full,
            shift_full,
            up_bias_full,
            down_bias_full,
        ) = behind
        down_in = result_grad.astype(jnp.bfloat16)
        down_term = jnp.einsum("sqf,sqd->fd", active, down_in, preferred_element_type=jnp.float32)
        down_bias_term = jnp.sum(down_in.astype(jnp.float32), axis=(0, 1))
        active_grad = jnp.einsum(
            "sqd,fd->sqf", down_in, down_full, preferred_element_type=jnp.float32
        )
        gelu_value, gelu_pull = jax.vjp(partial(jax.nn.gelu, approximate=False), inner_sum)
        inner_grad = gelu_pull(active_grad)[0].astype(jnp.bfloat16)
        up_bias_term = jnp.sum(inner_grad.astype(jnp.float32), axis=(0, 1))
        up_term = jnp.einsum("sqd,sqf->df", second, inner_grad, preferred_element_type=jnp.float32)
        second_grad = jnp.einsum(
            "sqf,df->sqd", inner_grad, up_full, preferred_element_type=jnp.float32
        )
        norm_value, norm_pull = jax.vjp(
            second_norm, middle, gain_full.astype(jnp.float32), shift_full.astype(jnp.float32)
        )
        middle_norm_grad, gain_term, shift_term = norm_pull(second_grad)
        middle_grad = result_grad + middle_norm_grad
        branch_grad = middle_grad.astype(jnp.bfloat16)
        out_term = jnp.einsum(
            "sqd,sqe->de", mixture, branch_grad, preferred_element_type=jnp.float32
        )
        mixture_grad = jnp.einsum(
            "sqe,de->sqd", branch_grad, out_full, preferred_element_type=jnp.float32
        ).astype(jnp.bfloat16)
        mixture_grad_heads = mixture_grad.reshape(per_batch, local_len, heads, HD)
        query_grad, key_part, value_part = attend_back(
            query_rot, key_heads, value_heads, log_total, mixture_grad_heads
        )
        key_part = key_part.reshape(per_batch, seq_len, width)
        value_part = value_part.reshape(per_batch, seq_len, width)
        key_grad, value_grad = (
            lax.psum_scatter(
                key_part.astype(jnp.bfloat16), "fsdp", scatter_dimension=1, tiled=True
            ).astype(jnp.float32),
            lax.psum_scatter(
                value_part.astype(jnp.bfloat16), "fsdp", scatter_dimension=1, tiled=True
            ).astype(jnp.float32),
        )
        query_grad = unrotate(query_grad, cosine, sine_part).reshape(per_batch, local_len, width)
        key_grad = unrotate(
            key_grad.reshape(per_batch, local_len, heads, HD), cosine, sine_part
        ).reshape(per_batch, local_len, width)
        project_grad = jnp.concatenate([query_grad, key_grad, value_grad], axis=-1).astype(
            jnp.bfloat16
        )
        qkv_term = jnp.einsum(
            "sqd,sqe->de", hidden, project_grad, preferred_element_type=jnp.float32
        )
        hidden_grad = jnp.einsum(
            "sqe,de->sqd", project_grad, qkv_full, preferred_element_type=jnp.float32
        )
        first_value, first_pull = jax.vjp(first_norm, source, condition)
        source_norm_grad, condition_grad = first_pull(hidden_grad)
        time_term = jnp.dot(features.astype(jnp.float32).T, condition_grad, precision=highest)
        time_bias_term = jnp.sum(condition_grad, axis=0)
        input_grads.append(middle_grad + source_norm_grad)
        batch_terms = (
            qkv_term,
            out_term,
            up_term,
            down_term,
            time_term,
            time_bias_term,
            gain_term,
            shift_term,
            up_bias_term,
            down_bias_term,
        )
        totals = batch_terms if totals is None else jax.tree.map(jnp.add, totals, batch_terms)
    (
        qkv_sum,
        out_sum,
        up_sum,
        down_sum,
        time_sum,
        time_bias_sum,
        gain_sum,
        shift_sum,
        up_bias_sum,
        down_bias_sum,
    ) = totals
    finished = (
        lax.psum_scatter(qkv_sum, ("dp", "fsdp"), scatter_dimension=0, tiled=True),
        lax.psum_scatter(out_sum, ("dp", "fsdp"), scatter_dimension=0, tiled=True),
        lax.psum_scatter(up_sum, ("dp", "fsdp"), scatter_dimension=0, tiled=True),
        lax.psum_scatter(down_sum, ("dp", "fsdp"), scatter_dimension=0, tiled=True),
        lax.psum_scatter(time_sum, ("dp", "fsdp"), scatter_dimension=0, tiled=True),
        lax.psum_scatter(time_bias_sum, ("dp", "fsdp"), scatter_dimension=0, tiled=True),
        lax.psum_scatter(gain_sum, ("dp", "fsdp"), scatter_dimension=0, tiled=True),
        lax.psum_scatter(shift_sum, ("dp", "fsdp"), scatter_dimension=0, tiled=True),
        lax.psum_scatter(up_bias_sum, ("dp", "fsdp"), scatter_dimension=0, tiled=True),
        lax.psum_scatter(down_bias_sum, ("dp", "fsdp"), scatter_dimension=0, tiled=True),
    )
    loss_sum = lax.psum(loss_part, ("dp", "fsdp"))
    loss_value = (loss_sum / (valid_total * width)).reshape(1)
    activations = jnp.concatenate(outputs, axis=0)
    input_grad = jnp.concatenate(input_grads, axis=0)
    return (
        activations,
        loss_value,
        input_grad,
        finished[0],
        finished[1],
        finished[2],
        finished[3],
        finished[4],
        finished[5],
        finished[6],
        finished[7],
        finished[8],
        finished[9],
    )


def solution(mesh):
    placed = (
        P("dp", "fsdp", None),
        P("dp", "fsdp", None),
        P("dp", "fsdp"),
        P("dp"),
        P(("dp", "fsdp"), None),
        P(("dp", "fsdp"), None),
        P(("dp", "fsdp"), None),
        P(("dp", "fsdp"), None),
        P(("dp", "fsdp"), None),
        P(("dp", "fsdp")),
        P(("dp", "fsdp")),
        P(("dp", "fsdp")),
        P(("dp", "fsdp")),
        P(("dp", "fsdp")),
    )
    return jax.shard_map(
        body,
        mesh=mesh,
        in_specs=placed,
        out_specs=(
            P("dp", "fsdp", None),
            P(),
            P("dp", "fsdp", None),
            P(("dp", "fsdp"), None),
            P(("dp", "fsdp"), None),
            P(("dp", "fsdp"), None),
            P(("dp", "fsdp"), None),
            P(("dp", "fsdp"), None),
            P(("dp", "fsdp")),
            P(("dp", "fsdp")),
            P(("dp", "fsdp")),
            P(("dp", "fsdp")),
            P(("dp", "fsdp")),
        ),
        check_vma=False,
    )
```

profile of v0, /device:TPU:9, one launch (start us, length us, event | category | flops | bytes accessed | tf_op | source)
XLA Modules:
  0.0 1572.2 jit_solution(4720287454006815786)
XLA Ops:
  17.9 40.3 %all-reduce.14 = (bf16[2048]{0:T(1024)(128)(2,1)S(1)}, bf16[1024]{0:T(1024)(128)(2,1)S(1)}, bf16[1024]{0:T(1024)(128)(2,1)S(1)}, bf16[1024]{0:T(1024)(128)(2,1)S(1)}) all-reduce(bf16[2048]{0:T(1024)(128)(2,1)S(1)} %dynamic-update-slice, bf16[1024]{0:T(1024)(128)(2,1)S(1)} %dynamic-update-slice.2, ...), channel_id=1, replica_groups=mesh['dp'=8,'fsdp'=4] {'dp','fsdp'}, use_global_device_ids=true, to_apply=%add.4 | all-reduce | flops 5120 | bytes 20480
  60.8 5.3 all-gather.11.cloned.1.call-done
  69.6 69.4 %all-gather.13.cloned.1.call-done = bf16[1024,3072]{1,0:T(8,128)(2,1)} async-done(((bf16[32,3072]{1,0:T(8,128)(2,1)}), bf16[1024,3072]{1,0:T(8,128)(2,1)}) %all-gather.13.cloned.1.call-update) | async-done | bytes 6291472 | tf_op jit(solution)/shard_map/all_gather | solution.py:160
  139.0 4.7 convolution_bitcast_fusion.1
  159.1 37.4 %psum.15 = f32[]{:T(128)} all-reduce(f32[]{:T(128)} %convert_reduce_fusion.6), channel_id=1, replica_groups=mesh['dp'=8,'fsdp'=4] {'dp','fsdp'}, use_global_device_ids=true, to_apply=%region_16.0 | all-reduce | flops 1 | bytes 8 | tf_op jit(solution)/shard_map/psum | solution.py:137
  196.6 37.1 %all-gather = bf16[32,1,128]{2,1,0:T(2,128)(2,1)S(1)} all-gather(bf16[1,1,128]{2,1,0:T(2,128)(2,1)S(1)} %convert_bitcast_fusion), channel_id=1, replica_groups=mesh['dp'=8,'fsdp'=4] {'dp','fsdp'}, dimensions={0}, use_global_device_ids=true | all-gather | bytes 8448 | tf_op jit(solution)/shard_map/all_gather | solution.py:168
  237.9 4.9 multiply_reduce_fusion.3
  248.6 4.5 convolution_convert_fusion.3
  256.0 76.5 %all-gather.21.cloned.1.call-done = bf16[1024,4096]{1,0:T(8,128)(2,1)} async-done(((bf16[32,4096]{1,0:T(8,128)(2,1)}), bf16[1024,4096]{1,0:T(8,128)(2,1)}) %all-gather.21.cloned.1.call-update) | async-done | bytes 8388624 | tf_op jit(solution)/shard_map/all_gather | solution.py:162
  332.4 16.3 %multiply_convert_fusion.5 = (bf16[256,4096]{1,0:T(8,128)(2,1)}, f32[256,4096]{1,0:T(8,128)}, f32[256,4096]{1,0:T(8,128)}) fusion(f32[4096]{0:T(1024)S(1)} %bitcast.318, bf16[1024,4096]{1,0:T(8,128)(2,1)} %all-gather.21.cloned.1.call-done, f32[1,256,1024]{2,1,0:T(8,128)S(1)} %get-tuple-element.100, f32[1024]{0:T(1024)S(1)} %convert_element_type.347, ...), kind=kOutput, calls=%fused_computation.40 | convolution fusion | flops 2218000384 | bytes 19949568 | tf_op jit(solution)/shard_map/sqd,df->sqf/dot_general | solution.py:215
  348.7 62.7 %all-gather.23.cloned.1.call-done = bf16[4096,1024]{1,0:T(8,128)(2,1)} async-done(((bf16[128,1024]{1,0:T(8,128)(2,1)}), bf16[4096,1024]{1,0:T(8,128)(2,1)}) %all-gather.23.cloned.1.call-update) | async-done | bytes 8388624 | tf_op jit(solution)/shard_map/all_gather | solution.py:163
  411.4 7.2 convert_reduce_fusion.5
  418.6 12.7 convert_reduce_fusion.1
  438.3 15.6 multiply_reduce_fusion.1
  455.6 8.5 multiply_convert_fusion.1
  468.1 10.9 convolution_convert_fusion.1
  479.1 7.0 fusion.23
  486.1 11.6 reduce-scatter.10.cloned.1.call-done
  500.5 31.3 %reduce-scatter.12.cloned.1.call-done = bf16[1,256,1024]{1,2,0:T(8,128)(2,1)} async-done(((bf16[1,1024,1024]{1,2,0:T(8,128)(2,1)}), bf16[1,256,1024]{1,2,0:T(8,128)(2,1)}) %reduce-scatter.12.cloned.1.call-update) | async-done | bytes 524304 | tf_op jit(solution)/shard_map/reduce_scatter | solution.py:286
  531.9 5.0 fusion.43
  538.3 4.7 convolution_bitcast_fusion
  551.1 21.2 %all-gather.27.cloned.1.call-done = bf16[1,1024,1024]{1,2,0:T(8,128)(2,1)} async-done(((bf16[1,256,1024]{1,2,0:T(8,128)(2,1)}), bf16[1,1024,1024]{1,2,0:T(8,128)(2,1)}) %all-gather.27.cloned.1.call-update) | async-done | bytes 2097168 | tf_op jit(solution)/shard_map/all_gather | solution.py:202
  572.3 4.2 multiply_reduce_fusion.2
  576.5 3.8 exponential_reduce_fusion
  582.7 14.3 all-gather.25.cloned.1.call-done
  599.9 8.2 convolution_convert_fusion.2
  609.3 15.8 %multiply_convert_fusion.4 = (bf16[256,4096]{1,0:T(8,128)(2,1)S(1)}, f32[256,4096]{1,0:T(8,128)S(1)}, f32[256,4096]{1,0:T(8,128)}) fusion(f32[4096]{0:T(1024)S(1)} %bitcast.319, bf16[1024,4096]{1,0:T(8,128)(2,1)} %all-gather.21.cloned.1.call-done, f32[1,256,1024]{2,1,0:T(8,128)S(1)} %get-tuple-element.110, f32[256]{0:T(256)S(1)} %fusion.90, ...), kind=kOutput, calls=%fused_computation.27 | convolution fusion | flops 2218000384 | bytes 19949568 | tf_op jit(solution)/shard_map/sqd,df->sqf/dot_general | solution.py:215
  625.2 4.0 convert_reduce_fusion.4
  629.2 11.8 convert_reduce_fusion
  641.0 7.4 fusion.48
  653.8 15.6 multiply_reduce_fusion
  671.0 8.1 multiply_convert_fusion
  683.2 9.9 convolution_convert_fusion
  693.3 6.7 fusion.22
  700.1 14.3 reduce-scatter.14.cloned.1.call-done
  715.9 32.5 %reduce-scatter.16.cloned.1.call-done = bf16[1,256,1024]{1,2,0:T(8,128)(2,1)} async-done(((bf16[1,1024,1024]{1,2,0:T(8,128)(2,1)}), bf16[1,256,1024]{1,2,0:T(8,128)(2,1)}) %reduce-scatter.16.cloned.1.call-update) | async-done | bytes 524304 | tf_op jit(solution)/shard_map/reduce_scatter | solution.py:286
  748.5 4.9 fusion.45
  765.2 6.7 convolution_add_fusion.2
  773.0 4.0 fusion.71
  777.0 9.9 convolution_add_fusion
  787.5 4.4 fusion.113
  792.0 10.0 convolution_add_fusion.1
  808.5 39.9 %all-reduce.13 = (f32[]{:T(128)}, f32[2048]{0:T(1024)S(1)}, f32[1024]{0:T(1024)S(1)}, f32[1024]{0:T(1024)S(1)}, f32[4096]{0:T(1024)S(1)}, /*index=5*/f32[1024]{0:T(1024)S(1)}) all-reduce(f32[]{:T(128)S(6)} %add.342, f32[2048]{0:T(1024)S(1)} %add.356, f32[1024]{0:T(1024)S(1)} %add.357, ...), channel_id=1, replica_groups=mesh['dp'=8,'fsdp'=4] {'dp','fsdp'}, use_global_device_ids=true, to_apply=%region_14.0 | all-reduce | flops 9217 | bytes 73736 | tf_op jit(solution)/shard_map/psum | solution.py:345
  855.8 13.0 reduce-scatter.26.cloned.1.call-done
  868.8 139.6 %reduce-scatter.20.cloned.1.call-done = f32[32,1024]{1,0:T(8,128)} async-done(((f32[1024,1024]{1,0:T(8,128)}), f32[32,1024]{1,0:T(8,128)}) %reduce-scatter.20.cloned.1.call-update) | async-done | bytes 131088 | tf_op jit(solution)/shard_map/reduce_scatter | solution.py:335
  1008.4 181.1 %reduce-scatter.18.cloned.1.call-done = f32[32,3072]{1,0:T(8,128)} async-done(((f32[1024,3072]{1,0:T(8,128)}), f32[32,3072]{1,0:T(8,128)}) %reduce-scatter.18.cloned.1.call-update) | async-done | bytes 393232 | tf_op jit(solution)/shard_map/reduce_scatter | solution.py:334
  1189.6 187.2 %reduce-scatter.24.cloned.1.call-done = f32[128,1024]{1,0:T(8,128)} async-done(((f32[4096,1024]{1,0:T(8,128)}), f32[128,1024]{1,0:T(8,128)}) %reduce-scatter.24.cloned.1.call-update) | async-done | bytes 524304 | tf_op jit(solution)/shard_map/reduce_scatter | solution.py:337
  1376.7 187.2 %reduce-scatter.22.cloned.1.call-done = f32[32,4096]{1,0:T(8,128)} async-done(((f32[1024,4096]{1,0:T(8,128)}), f32[32,4096]{1,0:T(8,128)}) %reduce-scatter.22.cloned.1.call-update) | async-done | bytes 524304 | tf_op jit(solution)/shard_map/reduce_scatter | solution.py:336
  (426 shorter events, 111.5 us)
Async XLA Ops:
  7.2 131.8 %copy-start.4 = (bf16[2,256,1024]{2,1,0:T(8,128)(2,1)S(1)}, bf16[2,256,1024]{2,1,0:T(8,128)(2,1)}, u32[]{:S(2)}) copy-start(bf16[2,256,1024]{2,1,0:T(8,128)(2,1)} %param.14) | copy-start | bytes 3145732
  7.2 58.9 %all-gather.11.cloned.1.call-start = ((), (), s32[]{:S(2)}) async-start(), calls=%async_computation.9 | async-start | bytes 1081344 | tf_op jit(solution)/shard_map/all_gather | solution.py:164
  8.8 130.2 %all-gather.13.cloned.1.call-start = ((), (), s32[]{:S(2)}) async-start(), calls=%async_computation.10 | async-start | bytes 6488064 | tf_op jit(solution)/shard_map/all_gather | solution.py:160
  10.6 224.4 %all-gather.15.cloned.1.call-start = ((), (), s32[]{:S(2)}) async-start(), calls=%async_computation.11 | async-start | bytes 2621440 | tf_op jit(solution)/shard_map/all_gather | solution.py:203
  59.4 84.3 %copy-start.72 = (f32[256]{0:T(256)}, f32[256]{0:T(256)S(1)}, u32[]{:S(2)}) copy-start(f32[256]{0:T(256)S(1)} %broadcast_multiply_fusion.5) | copy-start | bytes 3076
  60.8 82.9 %copy-start.75 = (f32[256]{0:T(256)}, f32[256]{0:T(256)S(1)}, u32[]{:S(2)}) copy-start(f32[256]{0:T(256)S(1)} %fusion.87) | copy-start | bytes 3076
  69.6 74.1 %copy-start.68 = (f32[1,1024]{1,0:T(1,128)}, f32[1,1024]{1,0:T(1,128)S(1)}, u32[]{:S(2)}) copy-start(f32[1,1024]{1,0:T(1,128)S(1)} %get-tuple-element.86) | copy-start | bytes 12292
  146.2 91.7 %all-gather.17.cloned.1.call-start = ((), (), s32[]{:S(2)}) async-start(), calls=%async_computation.12 | async-start | bytes 2621440 | tf_op jit(solution)/shard_map/all_gather | solution.py:202
  149.6 47.0 %copy-start.115 = (f32[128]{0:T(128)S(1)}, f32[128]{0:T(128)}, u32[]{:S(2)}) copy-start(f32[128]{0:T(128)} %param.26) | copy-start | bytes 1540
  152.2 90.5 %copy-start.30 = (bf16[256,16,32]{0,2,1:T(8,128)(2,1)}, bf16[256,16,32]{0,2,1:T(8,128)(2,1)S(1)}, u32[]{:S(2)}) copy-start(bf16[256,16,32]{0,2,1:T(8,128)(2,1)S(1)} %get-tuple-element.69) | copy-start | bytes 786436
  153.1 99.9 %all-gather.19.cloned.1.call-start = ((), (), s32[]{:S(2)}) async-start(), calls=%async_computation.13 | async-start | bytes 2162688 | tf_op jit(solution)/shard_map/all_gather | solution.py:161
  154.8 177.7 %all-gather.21.cloned.1.call-start = ((), (), s32[]{:S(2)}) async-start(), calls=%async_computation.14 | async-start | bytes 8650752 | tf_op jit(solution)/shard_map/all_gather | solution.py:162
  156.6 254.8 %all-gather.23.cloned.1.call-start = ((), (), s32[]{:S(2)}) async-start(), calls=%async_computation.15 | async-start | bytes 8650752 | tf_op jit(solution)/shard_map/all_gather | solution.py:163
  158.5 339.3 %reduce-scatter.10.cloned.1.call-start = ((), (), s32[]{:S(2)}) async-start(), calls=%async_computation.18 | async-start | bytes 2621440 | tf_op jit(solution)/shard_map/reduce_scatter | solution.py:283
  233.7 98.8 %copy-start.94 = (f32[32,1,128]{2,1,0:T(1,128)}, f32[32,1,128]{2,1,0:T(1,128)S(1)}, u32[]{:S(2)}) copy-start(f32[32,1,128]{2,1,0:T(1,128)S(1)} %convert_element_type.401) | copy-start | bytes 49156
  233.7 177.7 %copy-start.113 = (f32[1024]{0:T(1024)}, f32[1024]{0:T(1024)S(1)}, u32[]{:S(2)}) copy-start(f32[1024]{0:T(1024)S(1)} %convert_element_type.355) | copy-start | bytes 12292
  255.7 178.9 %copy-start.11 = (f32[1,256,1024]{2,1,0:T(8,128)}, f32[1,256,1024]{2,1,0:T(8,128)S(1)}, u32[]{:S(2)}) copy-start(f32[1,256,1024]{2,1,0:T(8,128)S(1)} %get-tuple-element.100) | copy-start | bytes 3145732
  255.7 178.9 %copy-start.82 = (f32[256]{0:T(256)}, f32[256]{0:T(256)S(1)}, u32[]{:S(2)}) copy-start(f32[256]{0:T(256)S(1)} %broadcast_multiply_fusion.4) | copy-start | bytes 3076
  256.0 178.6 %copy-start.87 = (f32[256]{0:T(256)}, f32[256]{0:T(256)S(1)}, u32[]{:S(2)}) copy-start(f32[256]{0:T(256)S(1)} %fusion.88) | copy-start | bytes 3076
  332.4 79.0 %copy-start.36 = (bf16[2,256,1024]{2,1,0:T(8,128)(2,1)S(1)}, bf16[2,256,1024]{2,1,0:T(8,128)(2,1)}, u32[]{:S(2)}) copy-start(bf16[2,256,1024]{2,1,0:T(8,128)(2,1)} %param.15) | copy-start | bytes 3145732
  468.0 63.8 %reduce-scatter.12.cloned.1.call-start = ((), (), s32[]{:S(2)}) async-start(), calls=%async_computation.19 | async-start | bytes 2621440 | tf_op jit(solution)/shard_map/reduce_scatter | solution.py:286
  479.0 93.3 %all-gather.27.cloned.1.call-start = ((), (), s32[]{:S(2)}) async-start(), calls=%async_computation.17 | async-start | bytes 2621440 | tf_op jit(solution)/shard_map/all_gather | solution.py:202
  479.1 59.2 %copy-start.66 = (f32[1,1024]{1,0:T(1,128)}, f32[1,1024]{1,0:T(1,128)S(1)}, u32[]{:S(2)}) copy-start(f32[1,1024]{1,0:T(1,128)S(1)} %get-tuple-element.87) | copy-start | bytes 12292
  479.1 59.2 %copy-start.70 = (f32[1,1024]{1,0:T(1,128)}, f32[1,1024]{1,0:T(1,128)S(1)}, u32[]{:S(2)}) copy-start(f32[1,1024]{1,0:T(1,128)S(1)} %get-tuple-element.88) | copy-start | bytes 12292
  486.1 45.8 %copy-start.73 = (f32[256]{0:T(256)S(1)}, f32[256]{0:T(256)}, u32[]{:S(2)}) copy-start(f32[256]{0:T(256)} %copy-done.72) | copy-start | bytes 3076
  500.5 36.4 %copy-start.46 = (bf16[1,256,16,64]{1,3,2,0:T(8,128)(2,1)}, bf16[1,256,16,64]{1,3,2,0:T(8,128)(2,1)S(1)}, u32[]{:S(2)}) copy-start(bf16[1,256,16,64]{1,3,2,0:T(8,128)(2,1)S(1)} %pad_maximum_fusion.12) | copy-start | bytes 1572868
  500.5 36.4 %copy-start.48 = (bf16[1,256,16,64]{1,3,2,0:T(8,128)(2,1)}, bf16[1,256,16,64]{1,3,2,0:T(8,128)(2,1)S(1)}, u32[]{:S(2)}) copy-start(bf16[1,256,16,64]{1,3,2,0:T(8,128)(2,1)S(1)} %pad_maximum_fusion.13) | copy-start | bytes 1572868
  547.9 28.5 %copy-start.33 = (bf16[256,16,32]{0,2,1:T(8,128)(2,1)}, bf16[256,16,32]{0,2,1:T(8,128)(2,1)S(1)}, u32[]{:S(2)}) copy-start(bf16[256,16,32]{0,2,1:T(8,128)(2,1)S(1)} %get-tuple-element.61) | copy-start | bytes 786436
  548.8 48.2 %all-gather.25.cloned.1.call-start = ((), (), s32[]{:S(2)}) async-start(), calls=%async_computation.16 | async-start | bytes 2621440 | tf_op jit(solution)/shard_map/all_gather | solution.py:203
  551.0 163.3 %reduce-scatter.14.cloned.1.call-start = ((), (), s32[]{:S(2)}) async-start(), calls=%async_computation.20 | async-start | bytes 2621440 | tf_op jit(solution)/shard_map/reduce_scatter | solution.py:283
  582.7 25.4 %copy-start.62 = (f32[16,256]{1,0:T(8,128)}, f32[16,256]{1,0:T(8,128)S(1)}, u32[]{:S(2)}) copy-start(f32[16,256]{1,0:T(8,128)S(1)} %log_add_fusion) | copy-start | bytes 49156
  609.0 39.4 %copy-start.7 = (f32[1,256,1024]{2,1,0:T(8,128)}, f32[1,256,1024]{2,1,0:T(8,128)S(1)}, u32[]{:S(2)}) copy-start(f32[1,256,1024]{2,1,0:T(8,128)S(1)} %get-tuple-element.110) | copy-start | bytes 3145732
  609.0 39.4 %copy-start.85 = (f32[256]{0:T(256)}, f32[256]{0:T(256)S(1)}, u32[]{:S(2)}) copy-start(f32[256]{0:T(256)S(1)} %broadcast_multiply_fusion.2) | copy-start | bytes 3076
  609.3 39.1 %copy-start.89 = (f32[256]{0:T(256)}, f32[256]{0:T(256)S(1)}, u32[]{:S(2)}) copy-start(f32[256]{0:T(256)S(1)} %fusion.90) | copy-start | bytes 3076
  683.1 65.3 %reduce-scatter.16.cloned.1.call-start = ((), (), s32[]{:S(2)}) async-start(), calls=%async_computation.21 | async-start | bytes 2621440 | tf_op jit(solution)/shard_map/reduce_scatter | solution.py:286
  693.2 175.7 %reduce-scatter.26.cloned.1.call-start = ((), (), s32[]{:S(2)}) async-start(), calls=%async_computation.26 | async-start | bytes 2162688 | tf_op jit(solution)/shard_map/reduce_scatter | solution.py:338
  693.3 22.2 %copy-start.53 = (f32[256,32]{0,1:T(8,128)S(1)}, f32[256,32]{0,1:T(8,128)}, u32[]{:S(2)}) copy-start(f32[256,32]{0,1:T(8,128)} %copy-done.51) | copy-start | bytes 98308
  700.0 48.4 %copy-start.67 = (f32[1,1024]{1,0:T(1,128)S(1)}, f32[1,1024]{1,0:T(1,128)}, u32[]{:S(2)}) copy-start(f32[1,1024]{1,0:T(1,128)} %copy-done.66) | copy-start | bytes 12292
  700.0 48.4 %copy-start.81 = (f32[256]{0:T(256)S(1)}, f32[256]{0:T(256)}, u32[]{:S(2)}) copy-start(f32[256]{0:T(256)} %copy-done.80) | copy-start | bytes 3076
  715.9 32.6 %copy-start.41 = (bf16[1,256,16,64]{1,3,2,0:T(8,128)(2,1)}, bf16[1,256,16,64]{1,3,2,0:T(8,128)(2,1)S(1)}, u32[]{:S(2)}) copy-start(bf16[1,256,16,64]{1,3,2,0:T(8,128)(2,1)S(1)} %pad_maximum_fusion.14) | copy-start | bytes 1572868
  715.9 32.6 %copy-start.43 = (bf16[1,256,16,64]{1,3,2,0:T(8,128)(2,1)}, bf16[1,256,16,64]{1,3,2,0:T(8,128)(2,1)S(1)}, u32[]{:S(2)}) copy-start(bf16[1,256,16,64]{1,3,2,0:T(8,128)(2,1)S(1)} %pad_maximum_fusion.15) | copy-start | bytes 1572868
  756.1 252.3 %reduce-scatter.20.cloned.1.call-start = ((), (), s32[]{:S(2)}) async-start(), calls=%async_computation.23 | async-start | bytes 4325376 | tf_op jit(solution)/shard_map/reduce_scatter | solution.py:335
  760.8 428.7 %reduce-scatter.18.cloned.1.call-start = ((), (), s32[]{:S(2)}) async-start(), calls=%async_computation.22 | async-start | bytes 12976128 | tf_op jit(solution)/shard_map/reduce_scatter | solution.py:334
  772.0 604.8 %reduce-scatter.24.cloned.1.call-start = ((), (), s32[]{:S(2)}) async-start(), calls=%async_computation.25 | async-start | bytes 17301504 | tf_op jit(solution)/shard_map/reduce_scatter | solution.py:337
  786.9 777.1 %reduce-scatter.22.cloned.1.call-start = ((), (), s32[]{:S(2)}) async-start(), calls=%async_computation.24 | async-start | bytes 17301504 | tf_op jit(solution)/shard_map/reduce_scatter | solution.py:336
  802.0 50.0 %copy-start.14 = (f32[1,256,1024]{2,1,0:T(8,128)S(1)}, f32[1,256,1024]{2,1,0:T(8,128)}, u32[]{:S(2)}) copy-start(f32[1,256,1024]{2,1,0:T(8,128)} %copy-done.12) | copy-start | bytes 3145732
  802.0 49.9 %copy-start.17 = (f32[1,256,1024]{2,1,0:T(8,128)S(1)}, f32[1,256,1024]{2,1,0:T(8,128)}, u32[]{:S(2)}) copy-start(f32[1,256,1024]{2,1,0:T(8,128)} %copy-done.15) | copy-start | bytes 3145732
  802.0 49.9 %copy-start.97 = (f32[256]{0:T(256)S(1)}, f32[256]{0:T(256)}, u32[]{:S(2)}) copy-start(f32[256]{0:T(256)} %copy-done.96) | copy-start | bytes 3076
  (98 other events, 698.2 us)
Sparse Core Ops, SparseCore 0:
  11.5 54.5 all-gather.10
  69.5 69.4 all-gather.12
  146.4 21.4 all-gather.14
  169.8 23.1 all-gather.16
  196.2 55.5 all-gather.18
  255.1 77.3 all-gather.20
  335.3 76.0 all-gather.22
  468.1 29.5 reduce-scatter.9
  500.4 31.4 reduce-scatter.11
  549.0 23.2 all-gather.26
  574.4 22.5 all-gather.24
  683.2 31.0 reduce-scatter.13
  717.0 31.4 reduce-scatter.15
  756.3 112.5 reduce-scatter.25
  871.6 136.7 reduce-scatter.19
  1015.9 173.5 reduce-scatter.17
  1192.3 184.4 reduce-scatter.23
  1379.5 184.4 reduce-scatter.21
where the time goes:
time: 1580 us; the launch traced here: 1570 us
  waiting for transfers between devices  1050 us (66%)
  matrix products  243 us (15%)
  blocking collectives  155 us (10%)
  other arithmetic  64.6 us (4%)
  local copies, waits for them, and re-layouts  39.9 us (3%)
  between operations  21.4 us (1%)
    reduce_scatter x1, waiting for transfers between devices, body(): lax.psum_scatter(up_sum, ('dp', 'fsdp'), scatter_dimension=0, tiled=True)  187 us
    reduce_scatter x1, waiting for transfers between devices, body(): lax.psum_scatter(down_sum, ('dp', 'fsdp'), scatter_dimension=0, tiled=True)  187 us
    reduce_scatter x1, waiting for transfers between devices, body(): lax.psum_scatter(qkv_sum, ('dp', 'fsdp'), scatter_dimension=0, tiled=True)  181 us
    reduce_scatter x1, waiting for transfers between devices, body(): lax.psum_scatter(out_sum, ('dp', 'fsdp'), scatter_dimension=0, tiled=True)  140 us
    all_gather x1, waiting for transfers between devices, body(): lax.all_gather(up_low, ('dp', 'fsdp'), axis=0, tiled=True)  76.5 us
    all_gather x1, waiting for transfers between devices, body(): lax.all_gather(qkv_low, ('dp', 'fsdp'), axis=0, tiled=True)  69.4 us
    reduce_scatter x2, waiting for transfers between devices, body(): lax.psum_scatter(value_part.astype(jnp.bfloat16), 'fsdp', scatter_dimensi...  63.9 us
    all_gather x1, waiting for transfers between devices, body(): lax.all_gather(down_low, ('dp', 'fsdp'), axis=0, tiled=True)  62.7 us
  transfers between devices with their start and end apart: 18, of which 15 were waited for; matrix products, arithmetic and copies ran while one was open for 11% of the time, Pallas kernels for 0%

commit v1 on v0

v1 whole, which is shorter than its diff:
```python
import math

import jax
import jax.numpy as jnp
from jax import lax
from jax.sharding import PartitionSpec as P

HD = 64
TE = 256

b16 = jnp.bfloat16
f32 = jnp.float32
highest = lax.Precision.HIGHEST
epsilon = 1e-05
core_pairs = [(i, i ^ 1) for i in range(4)]
x_pairs = [(i, i ^ 2) for i in range(4)]


def swap_core(v):
    return lax.ppermute(v, "fsdp", core_pairs)


def swap_x(v):
    return lax.ppermute(v, "fsdp", x_pairs)


def swap_y(v):
    return lax.ppermute(v, "dp", [(i, i ^ 1) for i in range(lax.axis_size("dp"))])


def shift_z(v, k):
    size = lax.axis_size("dp")
    depth = size // 2
    return lax.ppermute(v, "dp", [(i, ((i // 2 + k) % depth) * 2 + i % 2) for i in range(size)])


def place():
    f = lax.axis_index("fsdp")
    d = lax.axis_index("dp")
    return f // 2, f % 2, d % 2, d // 2, lax.axis_size("dp") // 2


def pick(v, index, axis=0):
    return lax.dynamic_index_in_dim(v, index, axis, False)


def gather_chips(piece):
    x, c, y, z, depth = place()
    rows, cols = piece.shape
    half = rows // 2
    stack = jnp.zeros((depth, rows, cols), piece.dtype)
    stack = lax.dynamic_update_slice(stack, piece[None], (z, 0, 0))
    for k in range(1, depth):
        got = shift_z(piece, k)
        stack = lax.dynamic_update_slice(stack, got[None], ((z - k) % depth, 0, 0))
    top = stack[:, :half]
    low = stack[:, half:]
    top_x = swap_x(top)
    low_y = swap_y(low)
    top_far = swap_y(jnp.stack([top, top_x]))
    low_far = swap_x(jnp.stack([low, low_y]))
    whole = jnp.zeros((depth, 2, 2, rows, cols), piece.dtype)

    def put(whole, part, yy, xx, at):
        return lax.dynamic_update_slice(whole, part[:, None, None], (0, yy, xx, at, 0))

    whole = put(whole, top, y, x, 0)
    whole = put(whole, top_x, y, 1 - x, 0)
    whole = put(whole, top_far[0], 1 - y, x, 0)
    whole = put(whole, top_far[1], 1 - y, 1 - x, 0)
    whole = put(whole, low, y, x, half)
    whole = put(whole, low_y, 1 - y, x, half)
    whole = put(whole, low_far[0], y, 1 - x, half)
    whole = put(whole, low_far[1], 1 - y, 1 - x, half)
    return whole.reshape(4 * depth, rows, cols)


def add_low(a, b):
    return (a.astype(f32) + b.astype(f32)).astype(a.dtype)


def scatter_chips(parts):
    x, c, y, z, depth = place()
    chips, rows, cols = parts.shape
    half = rows // 2
    grid = parts.reshape(depth, 2, 2, rows, cols)
    top = grid[:, :, :, :half]
    low = grid[:, :, :, half:]
    top = add_low(pick(top, x, 2), swap_x(pick(top, 1 - x, 2)))
    low = add_low(pick(low, y, 1), swap_y(pick(low, 1 - y, 1)))
    top = add_low(pick(top, y, 1), swap_y(pick(top, 1 - y, 1)))
    low = add_low(pick(low, x, 1), swap_x(pick(low, 1 - x, 1)))
    both = jnp.concatenate([top, low], axis=1)
    total = pick(both, z).astype(f32)
    for k in range(1, depth):
        total = total + shift_z(pick(both, (z + k) % depth), k).astype(f32)
    return total


def scatter_small(parts):
    x, c, y, z, depth = place()
    grid = parts.reshape(depth, 2, 2, 1, parts.shape[-1])
    grid = pick(grid, x, 2) + swap_x(pick(grid, 1 - x, 2))
    grid = pick(grid, y, 1) + swap_y(pick(grid, 1 - y, 1))
    total = pick(grid, z)
    for k in range(1, depth):
        total = total + shift_z(pick(grid, (z + k) % depth), k)
    return total[0]


def stats(v):
    mean = jnp.mean(v, axis=-1, keepdims=True)
    centre = v - mean
    rate = lax.rsqrt(jnp.mean(centre * centre, axis=-1, keepdims=True) + epsilon)
    return centre * rate, rate


def norm_back(g, n, rate):
    return (g - jnp.mean(g, -1, keepdims=True) - n * jnp.mean(g * n, -1, keepdims=True)) * rate


def rotate(v, cosine, sine):
    a, b = jnp.split(v, 2, axis=-1)
    return jnp.concatenate([a * cosine - b * sine, b * cosine + a * sine], axis=-1)


def dot(a, b, da, db):
    return lax.dot_general(a, b, (((da,), (db,)), ((), ())), preferred_element_type=f32)


def attend(q, k, v):
    scores = jnp.einsum("qhd,khd->hqk", q, k, preferred_element_type=f32) * 0.125
    log_total = jax.nn.logsumexp(scores, axis=-1, keepdims=True)
    probs = jnp.exp(scores - log_total).astype(b16)
    return jnp.einsum("hqk,khd->qhd", probs, v, preferred_element_type=f32), log_total


def attend_back(q, k, v, log_total, mixture_grad):
    scores = jnp.einsum("qhd,khd->hqk", q, k, preferred_element_type=f32) * 0.125
    full = jnp.exp(scores - log_total)
    prob_grad = jnp.einsum("qhd,khd->hqk", mixture_grad, v, preferred_element_type=f32)
    score_grad = (full * (prob_grad - jnp.sum(full * prob_grad, -1, keepdims=True))).astype(b16)
    dq = jnp.einsum("hqk,khd->qhd", score_grad, k, preferred_element_type=f32) * 0.125
    dk = jnp.einsum("hqk,qhd->khd", score_grad, q, preferred_element_type=f32) * 0.125
    dv = jnp.einsum("hqk,qhd->khd", full.astype(b16), mixture_grad, preferred_element_type=f32)
    return dq, dk, dv


def body(
    inputs, teacher, valid_mask, time_steps, qkv_weight, out_weight, up_weight, down_weight,
    time_weight, time_bias, norm_gain, norm_bias, up_bias, down_bias,
):
    x, c, y, z, depth = place()
    chips = 4 * depth
    seqs, block, width = inputs.shape
    rows = qkv_weight.shape[0]
    hidden_width = up_weight.shape[1]
    half = width // 2
    core_heads = half // HD
    tokens = 4 * block
    mine = 2 * block
    f = 2 * x + c
    ff = hidden_width // 2

    def collect(v):
        return jnp.concatenate([pick(v, x), swap_x(pick(v, 1 - x))], axis=0)

    source_low = collect(inputs)
    source_all = jnp.concatenate([source_low, swap_core(source_low)], axis=0)
    marks = valid_mask.astype(b16)
    target_marks = collect(
        jnp.concatenate([teacher, jnp.broadcast_to(marks[:, :, None], (seqs, block, 128))], axis=2)
    )
    target = target_marks[:, :width].astype(f32)
    mark = target_marks[:, width : width + 1].astype(f32)
    blocks = jnp.stack([f, f ^ 2, f ^ 1, f ^ 3])
    positions = (blocks[:, None] * block + jnp.arange(block)[None, :]).reshape(tokens).astype(f32)

    def own_other(v):
        return pick(v, c, 2), pick(v, 1 - c, 2)

    count = jnp.sum(valid_mask)
    counts = jnp.stack([count // 256, count % 256]).astype(b16)
    vector = jnp.concatenate(
        [v.astype(b16) for v in (time_bias, norm_gain, norm_bias, up_bias, down_bias)] + [counts]
    )
    vector = jnp.pad(vector, (0, 384 - vector.shape[0])).reshape(3, 128)
    vector = jnp.pad(vector, ((0, rows - 3), (0, 0)))
    qkv_own, qkv_other = own_other(qkv_weight.astype(b16).reshape(rows, 3, 2, half))
    up_own, up_other = own_other(up_weight.astype(b16).reshape(rows, -1, 2, down_weight.shape[0]))
    shape = (rows, -1)
    own = jnp.concatenate([vector, qkv_own.reshape(shape), up_own.reshape(shape)], axis=1)
    other = swap_core(
        jnp.concatenate([vector, qkv_other.reshape(shape), up_other.reshape(shape)], axis=1)
    )
    first = jnp.where(c == 0, own, other)
    second_rows = jnp.where(c == 0, other, own)
    chip = jnp.concatenate([first, second_rows], axis=0)
    cut = 128 + 3 * half
    group_1 = jnp.concatenate(
        [chip[:, :cut], time_weight.astype(b16).reshape(2 * rows, -1)], axis=1
    )
    group_2 = jnp.concatenate(
        [chip[:, cut:], out_weight.astype(b16).reshape(2 * rows, -1)], axis=1
    )
    group_3 = down_weight.astype(b16)
    all_1 = gather_chips(group_1)
    all_2 = gather_chips(group_2)
    all_3 = gather_chips(group_3)
    qkv_full = all_1[:, :, 128:cut].reshape(width, 3 * half)
    time_full = all_1[:, :, cut:].reshape(TE // 2, 2 * width)
    up_full = all_2[:, :, :ff].reshape(width, ff)
    out_half = all_2[:, :, ff:].reshape(chips, 1, rows, width)
    out_far = swap_core(out_half)
    out_full = jnp.concatenate(
        [jnp.where(c == 0, out_half, out_far), jnp.where(c == 0, out_far, out_half)], axis=1
    ).reshape(width, width)
    down_full = all_3.reshape(ff, width)
    vectors = all_1[:, :, :128].reshape(chips, 2, rows, 128)[:, :, :3].reshape(chips, 2, 384)
    vectors = vectors.astype(f32)
    at = 0

    def take(n):
        nonlocal at
        at += n
        return vectors[:, :, at - n : at]

    bias_time = take(time_bias.shape[0]).reshape(2 * width)
    gain = take(rows).reshape(width)
    shift = take(rows).reshape(width)
    bias_up = pick(take(up_bias.shape[0]), c, 1).reshape(ff)
    bias_down = take(rows).reshape(width)
    counted = take(2).reshape(-1, 2)
    valid_total = jnp.sum(counted[:, 0]) * 256.0 + jnp.sum(counted[:, 1])
    token_total = lax.axis_size("dp") * seqs * tokens
    factor = (token_total * width / 2) / (valid_total * width)

    spread = jnp.exp(jnp.arange(TE // 2, dtype=f32) * (-math.log(10000.0) / (TE // 2)))
    angle = pick(time_steps, x).astype(f32) * spread
    features = jnp.concatenate([jnp.sin(angle), jnp.cos(angle)]).astype(b16)
    feature_core = pick(features.reshape(chips, 2, -1), c, 1).reshape(1, TE // 2)
    part = dot(feature_core, time_full, 1, 0)
    condition = (part + swap_core(part))[0] + bias_time
    scale = 1.0 + condition[:width]
    n1, rate1 = stats(source_all.astype(f32))
    hidden = (n1 * scale + condition[width:]).astype(b16)
    n1 = n1[:mine]
    rate1 = rate1[:mine]
    project = dot(hidden, qkv_full, 1, 0)
    turn = jnp.exp(jnp.arange(HD // 2, dtype=f32) * (-2.0 * math.log(10000.0) / HD))
    angles = positions[:, None] * turn[None, :]
    cosine = jnp.cos(angles)[:, None]
    sine = jnp.sin(angles)[:, None]
    heads = (tokens, core_heads, HD)
    q = rotate(project[:, :half].reshape(heads), cosine, sine).astype(b16)
    k = rotate(project[:, half : 2 * half].reshape(heads), cosine, sine).astype(b16)
    v = project[:, 2 * half :].reshape(heads).astype(b16)
    mixed, log_total = attend(q, k, v)
    mixed = mixed.astype(b16).reshape(tokens, half)
    mixed_far = swap_core(mixed[mine:])
    mixture = jnp.where(
        c == 0,
        jnp.concatenate([mixed[:mine], mixed_far], axis=1),
        jnp.concatenate([mixed_far, mixed[:mine]], axis=1),
    )
    middle = source_low.astype(f32) + dot(mixture, out_full, 1, 0)
    n2, rate2 = stats(middle)
    second = (n2 * gain + shift).astype(b16)
    second_all = jnp.concatenate([second, swap_core(second)], axis=0)
    inner = dot(second_all, up_full, 1, 0) + bias_up
    flat = 0.5 * (1.0 + lax.erf(inner * (2.0**-0.5)))
    active = (inner * flat).astype(b16)
    slope = flat + inner * jnp.exp(-0.5 * inner * inner) * ((2.0 * math.pi) ** -0.5)
    down = dot(active, down_full, 1, 0)
    result = middle + (down[:mine] + swap_core(down[mine:].astype(b16)).astype(f32) + bias_down)

    differ = result - target
    loss_part = jnp.sum(mark * differ * differ)
    result_grad = 2.0 * mark * differ * factor

    def spread_out(v):
        far = swap_x(v[block:])
        near = v[:block]
        return jnp.stack([jnp.where(x == 0, near, far), jnp.where(x == 0, far, near)])

    activations = spread_out(result.astype(b16))

    down_in = result_grad.astype(b16)
    down_in_all = jnp.concatenate([down_in, swap_core(down_in)], axis=0)
    down_bias_part = jnp.sum(down_in.astype(f32), axis=0)
    inner_grad = (dot(down_in_all, down_full, 1, 1) * slope).astype(b16)
    second_part = dot(inner_grad, up_full, 1, 1)
    second_grad = second_part[:mine] + swap_core(second_part[mine:].astype(b16)).astype(f32)
    down_term = dot(active, down_in_all, 0, 0).astype(b16)
    down_sum = scatter_chips(down_term.reshape(chips, -1, width))
    up_bias_part = jnp.sum(inner_grad.astype(f32), axis=0)
    up_term = dot(second_all, inner_grad, 0, 0).astype(b16)
    up_sum = scatter_chips(up_term.reshape(chips, -1, ff))
    gain_part = jnp.sum(second_grad * n2, axis=0)
    shift_part = jnp.sum(second_grad, axis=0)
    middle_grad = result_grad + norm_back(second_grad * gain, n2, rate2)
    branch = middle_grad.astype(b16)
    mixture_grad = dot(branch, out_full, 1, 1).astype(b16).reshape(mine, 2, half)
    mixture_grad = jnp.concatenate(
        [pick(mixture_grad, c, 1), swap_core(pick(mixture_grad, 1 - c, 1))], axis=0
    )
    out_term = dot(mixture, branch, 0, 0).astype(b16).reshape(chips, 2, rows, width)
    out_term = add_low(pick(out_term, c, 1), swap_core(pick(out_term, 1 - c, 1)))
    dq, dk, dv = attend_back(q, k, v, log_total, mixture_grad.reshape(heads))
    dq = rotate(dq, cosine, -sine)
    dk = rotate(dk, cosine, -sine)
    flat_shape = (tokens, half)
    project_grad = jnp.concatenate(
        [dq.reshape(flat_shape), dk.reshape(flat_shape), dv.reshape(flat_shape)], axis=1
    ).astype(b16)
    qkv_term = dot(hidden, project_grad, 0, 0).astype(b16)
    hidden_part = dot(project_grad, qkv_full, 1, 1)
    hidden_grad = hidden_part[:mine] + swap_core(hidden_part[mine:].astype(b16)).astype(f32)
    input_grad = spread_out(middle_grad + norm_back(hidden_grad * scale, n1, rate1))
    condition_part = jnp.concatenate([jnp.sum(hidden_grad * n1, 0), jnp.sum(hidden_grad, 0)])
    condition_grad = condition_part + swap_core(condition_part)
    time_term = (feature_core.reshape(-1, 1).astype(f32) * condition_grad[None]).astype(b16)
    last = jnp.concatenate(
        [
            qkv_term.reshape(chips, 2 * rows, 3 * half),
            out_term.reshape(chips, 2 * rows, half),
            time_term.reshape(chips, 2 * rows, -1),
        ],
        axis=2,
    )
    last_sum = scatter_chips(last)
    qkv_sum = last_sum[:, : 3 * half]
    out_sum = last_sum[:, 3 * half : 4 * half].reshape(rows, width)
    time_sum = last_sum[:, 4 * half :].reshape(-1, 2 * width)

    small = jnp.concatenate(
        [
            v.reshape(chips, 2, -1)
            for v in (condition_part, gain_part, shift_part, down_bias_part)
        ],
        axis=2,
    ).reshape(chips, -1)
    small_count = small.shape[1]
    small = jnp.concatenate(
        [small, up_bias_part.reshape(chips, -1), jnp.broadcast_to(loss_part, (chips, 64))], axis=1
    )
    small_sum = scatter_small(small)
    pairs = small_sum[:small_count].reshape(2, -1)
    up_bias_sum = small_sum[small_count : small_count + up_bias.shape[0]]
    loss_sum = small_sum[small_count + up_bias.shape[0] :]
    lead = pairs.shape[1]
    far = swap_core(jnp.concatenate([pick(pairs, 1 - c), loss_sum]))
    vec = pick(pairs, c) + far[:lead]
    loss = ((loss_sum[0] + far[lead]) / (valid_total * width)).reshape(1)

    def columns(total, inner_size):
        total = total.reshape(2, rows, -1, inner_size)
        near = pick(total, c)
        far = swap_core(pick(total, 1 - c))
        return jnp.stack(
            [jnp.where(c == 0, near, far), jnp.where(c == 0, far, near)], axis=2
        ).reshape(rows, -1)

    r2 = 2 * rows
    return (
        activations,
        loss,
        input_grad,
        columns(qkv_sum, half),
        out_sum,
        columns(up_sum, down_weight.shape[0]),
        down_sum,
        time_sum,
        vec[:r2],
        vec[r2 : r2 + rows],
        vec[r2 + rows : r2 + 2 * rows],
        up_bias_sum,
        vec[r2 + 2 * rows :],
    )


def solution(mesh):
    both = ("dp", "fsdp")
    tokens = P("dp", "fsdp", None)
    weight = P(both, None)
    vector = P(both)
    return jax.shard_map(
        body,
        mesh=mesh,
        in_specs=(tokens, tokens, P("dp", "fsdp"), P("dp")) + (weight,) * 5 + (vector,) * 5,
        out_specs=(tokens, P(), tokens) + (weight,) * 5 + (vector,) * 5,
        check_vma=False,
    )
```

time: 1580 us -> 670 us (0.42)
  waiting for transfers between devices: 1050 us -> 214 us
  blocking collectives: 155 us -> 0 us
  matrix products: 243 us -> 147 us
  starting transfers between devices: 1.13 us -> 70.4 us
  local copies, waits for them, and re-layouts: 39.9 us -> 103 us
  other arithmetic: 64.6 us -> 118 us
    reduce_scatter x9 -> x0, waiting for transfers between devices: 798 us -> none  [the longest x1 187 us: body(): lax.psum_scatter(up_sum, ('dp', 'fsdp'), scatter_dimension=0, tiled=True)]
    all_gather x9 -> x0, waiting for transfers between devices: 249 us -> none  [the longest x1 76.5 us: body(): lax.all_gather(up_low, ('dp', 'fsdp'), axis=0, tiled=True)]
    ppermute x0 -> x67, waiting for transfers between devices: none -> 214 us  [the longest x21 75.7 us: shift_z(): lax.ppermute(v, 'dp', [(i, (i // 2 + k) % depth * 2 + i % 2) for i in ran...]
    dot_general x38 -> x19, matrix products: 243 us -> 147 us  [the longest x13 62.8 us: dot(): lax.dot_general(a, b, (((da,), (db,)), ((), ())), preferred_element_type=...]
    psum x2 -> x0, blocking collectives: 77.3 us -> none  [the longest x1 39.9 us: body(): loss_sum = lax.psum(loss_part, ('dp', 'fsdp'))]
    ppermute x0 -> x67, starting transfers between devices: none -> 70.4 us  [the longest x21 29.5 us: shift_z(): lax.ppermute(v, 'dp', [(i, (i // 2 + k) % depth * 2 + i % 2) for i in ran...]
    unnamed x1 -> x0, blocking collectives: 40.3 us -> none
    all_gather x1 -> x0, blocking collectives: 37.1 us -> none  [body(): lax.all_gather(up_bias_low, ('dp', 'fsdp'), axis=0, tiled=True)]
  transfers between devices with their start and end apart: 18 -> 67, of which waited for: 15 -> 21; matrix products, arithmetic and copies ran while one was open for 11% -> 46% of each run, Pallas kernels for 0% -> 0%
where the time goes in v1:
time: 670 us; the launch traced here: 663 us
  waiting for transfers between devices  214 us (32%)
  matrix products  147 us (22%)
  other arithmetic  118 us (18%)
  local copies, waits for them, and re-layouts  103 us (15%)
  starting transfers between devices  70.4 us (11%)
  between operations  10.1 us (2%)
    ppermute x21, waiting for transfers between devices, shift_z(): lax.ppermute(v, 'dp', [(i, (i // 2 + k) % depth * 2 + i % 2) for i in ran...  75.7 us
    ppermute x13, waiting for transfers between devices, swap_y(): lax.ppermute(v, 'dp', [(i, i ^ 1) for i in range(lax.axis_size('dp'))])  73.5 us
    ppermute x17, waiting for transfers between devices, swap_x(): return lax.ppermute(v, 'fsdp', x_pairs)  64.7 us
    dot_general x13, matrix products, dot(): lax.dot_general(a, b, (((da,), (db,)), ((), ())), preferred_element_type=...  62.8 us
    ppermute x21, starting transfers between devices, shift_z(): lax.ppermute(v, 'dp', [(i, (i // 2 + k) % depth * 2 + i % 2) for i in ran...  29.5 us
    convert_element_type x1, other arithmetic, attend_back(): (full * (prob_grad - jnp.sum(full * prob_grad, -1, keepdims=True))).astyp...  28.2 us
    unnamed x208, local copies, waits for them, and re-layouts  23.9 us
    ppermute x16, starting transfers between devices, swap_core(): return lax.ppermute(v, 'fsdp', core_pairs)  23 us
  transfers between devices with their start and end apart: 67, of which 21 were waited for; matrix products, arithmetic and copies ran while one was open for 46% of the time, Pallas kernels for 0%

profile of v1, /device:TPU:9, one launch (start us, length us, event | category | flops | bytes accessed | tf_op | source)
XLA Modules:
  0.0 662.6 jit_solution(758426909517557630)
XLA Ops:
  40.4 18.9 %collective-permute-done.3 = bf16[64,1920]{1,0:T(8,128)(2,1)S(1)} collective-permute-done((bf16[64,1920]{1,0:T(8,128)(2,1)S(1)}, bf16[64,1920]{1,0:T(8,128)(2,1)S(1)}, u32[]{:S(2)}, u32[]{:S(2)}) %collective-permute-start.3) | collective-permute-done | bytes 245792 | tf_op jit(solution)/shard_map/ppermute | solution.py:34
  62.2 7.4 %collective-permute-done.5 = bf16[64,1920]{1,0:T(8,128)(2,1)S(1)} collective-permute-done((bf16[64,1920]{1,0:T(8,128)(2,1)S(1)}, bf16[64,1920]{1,0:T(8,128)(2,1)S(1)}, u32[]{:S(2)}, u32[]{:S(2)}) %collective-permute-start.5) | collective-permute-done | bytes 245792 | tf_op jit(solution)/shard_map/ppermute | solution.py:34
  72.0 8.4 %collective-permute-done.12 = bf16[64,2560]{1,0:T(8,128)(2,1)S(1)} collective-permute-done((bf16[64,2560]{1,0:T(8,128)(2,1)S(1)}, bf16[64,2560]{1,0:T(8,128)(2,1)S(1)}, u32[]{:S(2)}, u32[]{:S(2)}) %collective-permute-start.12) | collective-permute-done | bytes 327712 | tf_op jit(solution)/shard_map/ppermute | solution.py:34
  87.8 7.3 %collective-permute-done.6 = bf16[4,32,1920]{2,1,0:T(8,128)(2,1)S(1)} collective-permute-done((bf16[4,32,1920]{2,1,0:T(8,128)(2,1)S(1)}, bf16[4,32,1920]{2,1,0:T(8,128)(2,1)S(1)}, u32[]{:S(2)}, u32[]{:S(2)}) %collective-permute-start.6) | collective-permute-done | bytes 491552 | tf_op jit(solution)/shard_map/ppermute | solution.py:24
  95.9 10.9 %collective-permute-done.17 = bf16[4,32,2560]{2,1,0:T(8,128)(2,1)S(1)} collective-permute-done((bf16[4,32,2560]{2,1,0:T(8,128)(2,1)S(1)}, bf16[4,32,2560]{2,1,0:T(8,128)(2,1)S(1)}, u32[]{:S(2)}, u32[]{:S(2)}) %collective-permute-start.17) | collective-permute-done | bytes 655392 | tf_op jit(solution)/shard_map/ppermute | solution.py:28
  112.9 16.6 %collective-permute-done.25 = bf16[2,4,64,1024]{3,2,1,0:T(8,128)(2,1)S(1)} collective-permute-done((bf16[2,4,64,1024]{3,2,1,0:T(8,128)(2,1)S(1)}, bf16[2,4,64,1024]{3,2,1,0:T(8,128)(2,1)S(1)}, u32[]{:S(2)}, u32[]{:S(2)}) %collective-permute-start.25) | collective-permute-done | bytes 1048608 | tf_op jit(solution)/shard_map/ppermute | solution.py:28
  129.8 20.6 %collective-permute-done.7 = bf16[2,4,32,1920]{3,2,1,0:T(8,128)(2,1)S(1)} collective-permute-done((bf16[2,4,32,1920]{3,2,1,0:T(8,128)(2,1)S(1)}, bf16[2,4,32,1920]{3,2,1,0:T(8,128)(2,1)S(1)}, u32[]{:S(2)}, u32[]{:S(2)}) %collective-permute-start.7) | collective-permute-done | bytes 983072 | tf_op jit(solution)/shard_map/ppermute | solution.py:28
  163.4 3.9 slice.333
  169.5 5.5 fusion.54
  178.6 3.1 copy.165
  183.1 2.9 copy.166
  186.1 3.0 subtract_convert_fusion.3
  189.1 13.2 %multiply_reduce_fusion.1 = (f32[8,1024]{1,0:T(8,128)S(1)}, f32[8,1024,1024]{1,2,0:T(8,128)}) fusion(bf16[1024,8,32]{0,2,1:T(8,128)(2,1)S(1)} %get-tuple-element.109, bf16[1024,8,32]{0,2,1:T(8,128)(2,1)S(1)} %get-tuple-element.110, bf16[1024,8,32]{0,2,1:T(8,128)(2,1)S(1)} %get-tuple-element.57, bf16[1024,8,32]{0,2,1:T(8,128)(2,1)S(1)} %get-tuple-element.56), kind=kOutput, calls=%fused_computation.4 | convolution fusion | flops 1094705152 | bytes 35684352 | tf_op jit(solution)/shard_map/qhd,khd->hqk/dot_general | solution.py:132
  202.4 13.6 %exponential_reduce_fusion = f32[8,1024]{1,0:T(8,128)S(1)} fusion(f32[8,1024,1024]{1,2,0:T(8,128)} %get-tuple-element.130, f32[8,1024]{1,0:T(8,128)S(1)} %is-finite_select_fusion), kind=kLoop, calls=%fused_computation.3 | loop fusion | flops 25157632 | bytes 33619968 | tf_op jit(solution)/shard_map/reduce_sum | solution.py:133
  223.6 13.6 %fusion.31 = bf16[1024,8,64]{0,2,1:T(8,128)(2,1)S(1)} fusion(bf16[1024,8,64]{0,2,1:T(8,128)(2,1)S(1)} %bitcast.452, f32[8,1024,1024]{1,2,0:T(8,128)} %get-tuple-element.130, f32[8,1024]{1,0:T(8,128)S(1)} %log_add_fusion), kind=kOutput, calls=%fused_computation.107 | convolution fusion | flops 1099431936 | bytes 35684352 | tf_op jit(solution)/shard_map/hqk,khd->qhd/dot_general | solution.py:135
  249.6 8.6 %multiply_convert_fusion.1 = (bf16[1024,2048]{1,0:T(8,128)(2,1)S(1)}, f32[1024,2048]{1,0:T(8,128)}) fusion(f32[2048]{0:T(1024)S(1)} %fusion.113, bf16[1024,2048]{1,0:T(8,128)(2,1)S(1)} %bitcast.461, bf16[512,1024]{1,0:T(8,128)(2,1)S(1)} %collective-permute-done.20, bf16[512,1024]{1,0:T(8,128)(2,1)S(1)} %add_convert_fusion.1), kind=kOutput, calls=%fused_computation.14 | convolution fusion | flops 4311744512 | bytes 18882560 | tf_op jit(solution)/shard_map/dot_general | solution.py:128
  258.2 4.5 fusion.159
  265.2 14.7 %collective-permute-done.30 = bf16[256,1152]{1,0:T(8,128)(2,1)S(1)} collective-permute-done((bf16[256,1152]{1,0:T(8,128)(2,1)S(1)}, bf16[256,1152]{1,0:T(8,128)(2,1)S(1)}, u32[]{:S(2)}, u32[]{:S(2)}) %collective-permute-start.30) | collective-permute-done | bytes 589856 | tf_op jit(solution)/shard_map/ppermute | solution.py:24
  283.1 3.9 fusion.16
  292.4 4.1 fusion.7
  298.7 6.5 collective-permute-done.29
  307.5 10.6 %convert_reduce_fusion = (f32[2048]{0:T(1024)S(1)}, bf16[1024,2048]{1,0:T(8,128)(2,1)S(1)}) fusion(f32[1024,2048]{1,0:T(8,128)} %get-tuple-element.134, f32[2048]{0:T(1024)S(1)} %fusion.113, bf16[2048,1024]{1,0:T(8,128)(2,1)S(1)} %bitcast.466, bf16[512,1024]{1,0:T(8,128)(2,1)} %collective-permute-done.31, bf16[512,1024]{1,0:T(8,128)(2,1)} %get-tuple-element.34), kind=kOutput, calls=%fused_computation.13 | convolution fusion | flops 4326422528 | bytes 18890752 | tf_op jit(solution)/shard_map/dot_general | solution.py:128
  318.2 4.5 fusion.160
  322.7 5.0 convolution_convert_fusion.2
  330.7 6.4 convolution_convert_fusion.1
  354.5 3.5 constant_dynamic-slice_fusion.20
  358.0 3.6 copy.189
  365.0 2.8 convolution_convert_fusion.3
  376.3 12.6 %collective-permute-done.54 = bf16[4,2,32,2048]{3,2,1,0:T(8,128)(2,1)} collective-permute-done((bf16[4,2,32,2048]{3,2,1,0:T(8,128)(2,1)}, bf16[4,2,32,2048]{3,2,1,0:T(8,128)(2,1)}, u32[]{:S(2)}, u32[]{:S(2)}) %collective-permute-start.54) | collective-permute-done | bytes 1048608 | tf_op jit(solution)/shard_map/ppermute | solution.py:28
  398.1 14.8 %fusion.28 = bf16[8,64,1024]{2,1,0:T(8,128)(2,1)} fusion(f32[8,1024,1024]{1,2,0:T(8,128)} %get-tuple-element.130, f32[8,1024]{1,0:T(8,128)S(1)} %log_add_fusion, bf16[512,8,64]{0,2,1:T(8,128)(2,1)S(1)} %bitcast.458, bf16[512,8,64]{0,2,1:T(8,128)(2,1)S(1)} %bitcast.456), kind=kOutput, calls=%fused_computation.89 | convolution fusion | flops 1101529088 | bytes 35684352 | tf_op jit(solution)/shard_map/hqk,qhd->khd/dot_general | solution.py:145
  412.9 22.7 %multiply_reduce_fusion = (f32[8,1024]{1,0:T(8,128)S(1)}, f32[8,1024,1024]{1,2,0:T(8,128)}) fusion(f32[8,1024,1024]{1,2,0:T(8,128)} %get-tuple-element.130, f32[8,1024]{1,0:T(8,128)S(1)} %log_add_fusion, bf16[1024,8,64]{0,2,1:T(8,128)(2,1)S(1)} %bitcast.453, bf16[512,8,64]{0,2,1:T(8,128)(2,1)S(1)} %bitcast.459, bf16[512,8,64]{0,2,1:T(8,128)(2,1)S(1)} %bitcast.457), kind=kOutput, calls=%fused_computation.1 | convolution fusion | flops 1109385216 | bytes 69271552 | tf_op jit(solution)/shard_map/qhd,khd->hqk/dot_general | solution.py:141
  435.6 28.2 %multiply_convert_fusion = bf16[8,1024,1024]{1,2,0:T(8,128)(2,1)} fusion(f32[8,1024,1024]{1,2,0:T(8,128)} %get-tuple-element.138, f32[8,1024,1024]{1,2,0:T(8,128)} %get-tuple-element.130, f32[8,1024]{1,0:T(8,128)S(1)} %get-tuple-element.137, f32[8,1024]{1,0:T(8,128)S(1)} %log_add_fusion), kind=kLoop, calls=%fused_computation | loop fusion | flops 41943040 | bytes 83951616 | tf_op jit(solution)/shard_map/convert_element_type | solution.py:142
  463.8 11.4 %multiply_bitcast_fusion = f32[1024,8,64]{0,2,1:T(8,128)S(1)} fusion(bf16[8,1024,1024]{1,2,0:T(8,128)(2,1)} %multiply_convert_fusion, bf16[1024,8,32]{0,2,1:T(8,128)(2,1)} %copy-done.31, bf16[1024,8,32]{0,2,1:T(8,128)(2,1)} %copy-done.30), kind=kOutput, calls=%fused_computation.64 | convolution fusion | flops 1076363264 | bytes 19922944 | tf_op jit(solution)/shard_map/hqk,qhd->khd/dot_general | solution.py:144
  475.2 8.9 %multiply_bitcast_fusion.1 = f32[1024,8,64]{0,2,1:T(8,128)S(1)} fusion(bf16[8,1024,1024]{1,2,0:T(8,128)(2,1)} %multiply_convert_fusion, bf16[1024,8,32]{0,2,1:T(8,128)(2,1)S(1)} %copy-done.27, bf16[1024,8,32]{0,2,1:T(8,128)(2,1)S(1)} %copy-done.29), kind=kOutput, calls=%fused_computation.65 | convolution fusion | flops 1076363264 | bytes 19922944 | tf_op jit(solution)/shard_map/hqk,khd->qhd/dot_general | solution.py:143
  496.7 5.6 convolution_convert_fusion
  502.4 3.5 fusion.35
  508.6 9.4 %collective-permute-done.57 = bf16[64,2048]{1,0:T(8,128)(2,1)S(1)} collective-permute-done((bf16[64,2048]{1,0:T(8,128)(2,1)S(1)}, bf16[64,2048]{1,0:T(8,128)(2,1)S(1)}, u32[]{:S(2)}, u32[]{:S(2)}) %collective-permute-start.57) | collective-permute-done | bytes 262176 | tf_op jit(solution)/shard_map/ppermute | solution.py:34
  518.2 4.2 collective-permute-done.58
  522.4 7.8 %collective-permute-start.34 = (bf16[512,1024]{1,0:T(8,128)(2,1)}, bf16[512,1024]{1,0:T(8,128)(2,1)S(1)}, u32[]{:S(2)}, u32[]{:S(2)}) collective-permute-start(bf16[512,1024]{1,0:T(8,128)(2,1)} %slice.479), channel_id=1, source_target_pairs={{0,1},{1,0},{2,3},{3,2},{4,5},{5,4},{6,7},{7,6},{8,9},{9,8},{10,11... | collective-permute-start | bytes 3145736 | tf_op jit(solution)/shard_map/ppermute | solution.py:20
  530.6 3.5 collective-permute-done.66
  539.6 3.2 multiply_reduce_fusion.2
  543.4 2.9 collective-permute-start.43
  560.6 4.2 collective-permute-start.38
  570.0 32.7 %collective-permute-done.44 = bf16[4,2,32,2304]{3,2,0,1:T(8,128)(2,1)} collective-permute-done((bf16[4,2,32,2304]{3,2,0,1:T(8,128)(2,1)S(1)}, bf16[4,2,32,2304]{3,2,0,1:T(8,128)(2,1)}, u32[]{:S(2)}, u32[]{:S(2)}) %collective-permute-start.44) | collective-permute-done | bytes 1179680 | tf_op jit(solution)/shard_map/ppermute | solution.py:24
  606.9 11.5 %collective-permute-done.45 = bf16[4,32,2304]{2,1,0:T(8,128)(2,1)S(1)} collective-permute-done((bf16[4,32,2304]{2,1,0:T(8,128)(2,1)S(1)}, bf16[4,32,2304]{2,1,0:T(8,128)(2,1)S(1)}, u32[]{:S(2)}, u32[]{:S(2)}) %collective-permute-start.45) | collective-permute-done | bytes 589856 | tf_op jit(solution)/shard_map/ppermute | solution.py:28
  622.4 3.3 collective-permute-start.49
  630.1 15.4 %collective-permute-done.49 = bf16[64,2304]{1,0:T(8,128)(2,1)} collective-permute-done((bf16[64,2304]{1,0:T(8,128)(2,1)}, bf16[64,2304]{1,0:T(8,128)(2,1)}, u32[]{:S(2)}, u32[]{:S(2)}) %collective-permute-start.49) | collective-permute-done | bytes 294944 | tf_op jit(solution)/shard_map/ppermute | solution.py:34
  645.6 6.8 %collective-permute-done.50 = bf16[64,2304]{1,0:T(8,128)(2,1)} collective-permute-done((bf16[64,2304]{1,0:T(8,128)(2,1)}, bf16[64,2304]{1,0:T(8,128)(2,1)}, u32[]{:S(2)}, u32[]{:S(2)}) %collective-permute-start.50) | collective-permute-done | bytes 294944 | tf_op jit(solution)/shard_map/ppermute | solution.py:34
  (570 shorter events, 212.3 us)
Async XLA Ops:
  2.7 33.4 %collective-permute-start.22 = (bf16[128,1024]{1,0:T(8,128)(2,1)}, bf16[128,1024]{1,0:T(8,128)(2,1)}, u32[]{:S(2)}, u32[]{:S(2)}) collective-permute-start(bf16[128,1024]{1,0:T(8,128)(2,1)} %get-tuple-element.36), channel_id=1, source_target_pairs={{0,16},{4,20},{8,24},{12,28},{16,0},{20,4},{24,8},{28,12},{1,17},{... | collective-permute-start | bytes 786440 | tf_op jit(solution)/shard_map/ppermute | solution.py:34
  5.0 27.4 %collective-permute-start.21 = (bf16[128,1024]{1,0:T(8,128)(2,1)}, bf16[128,1024]{1,0:T(8,128)(2,1)}, u32[]{:S(2)}, u32[]{:S(2)}) collective-permute-start(bf16[128,1024]{1,0:T(8,128)(2,1)} %get-tuple-element.36), channel_id=1, source_target_pairs={{0,8},{4,12},{8,16},{12,20},{16,24},{20,28},{24,0},{28,4},{1,9},{5... | collective-permute-start | bytes 786440 | tf_op jit(solution)/shard_map/ppermute | solution.py:34
  5.0 32.1 %collective-permute-start.23 = (bf16[128,1024]{1,0:T(8,128)(2,1)}, bf16[128,1024]{1,0:T(8,128)(2,1)}, u32[]{:S(2)}, u32[]{:S(2)}) collective-permute-start(bf16[128,1024]{1,0:T(8,128)(2,1)} %get-tuple-element.36), channel_id=1, source_target_pairs={{0,24},{4,28},{8,0},{12,4},{16,8},{20,12},{24,16},{28,20},{1,25},{... | collective-permute-start | bytes 786440 | tf_op jit(solution)/shard_map/ppermute | solution.py:34
  22.3 49.3 %collective-permute-start = (bf16[256,1024]{1,0:T(8,128)(2,1)}, bf16[256,1024]{1,0:T(8,128)(2,1)S(1)}, u32[]{:S(2)}, u32[]{:S(2)}) collective-permute-start(bf16[256,1024]{1,0:T(8,128)(2,1)} %get-tuple-element.94), channel_id=1, source_target_pairs={{0,2},{1,3},{2,0},{3,1},{4,6},{5,7},{6,4},{7,5},{8,10},{9,11},{10,... | collective-permute-start | bytes 1572872 | tf_op jit(solution)/shard_map/ppermute | solution.py:24
  30.8 30.7 %collective-permute-start.4 = (bf16[64,1920]{1,0:T(8,128)(2,1)S(1)}, bf16[64,1920]{1,0:T(8,128)(2,1)S(1)}, u32[]{:S(2)}, u32[]{:S(2)}) collective-permute-start(bf16[64,1920]{1,0:T(8,128)(2,1)S(1)} %get-tuple-element.38), channel_id=1, source_target_pairs={{0,16},{4,20},{8,24},{12,28},{16,0},{20,4},{24,8},{28,12},{1,17},{... | collective-permute-start | bytes 737288 | tf_op jit(solution)/shard_map/ppermute | solution.py:34
  32.4 26.9 %collective-permute-start.3 = (bf16[64,1920]{1,0:T(8,128)(2,1)S(1)}, bf16[64,1920]{1,0:T(8,128)(2,1)S(1)}, u32[]{:S(2)}, u32[]{:S(2)}) collective-permute-start(bf16[64,1920]{1,0:T(8,128)(2,1)S(1)} %get-tuple-element.38), channel_id=1, source_target_pairs={{0,8},{4,12},{8,16},{12,20},{16,24},{20,28},{24,0},{28,4},{1,9},{5... | collective-permute-start | bytes 737288 | tf_op jit(solution)/shard_map/ppermute | solution.py:34
  36.1 33.5 %collective-permute-start.5 = (bf16[64,1920]{1,0:T(8,128)(2,1)S(1)}, bf16[64,1920]{1,0:T(8,128)(2,1)S(1)}, u32[]{:S(2)}, u32[]{:S(2)}) collective-permute-start(bf16[64,1920]{1,0:T(8,128)(2,1)S(1)} %get-tuple-element.38), channel_id=1, source_target_pairs={{0,24},{4,28},{8,0},{12,4},{16,8},{20,12},{24,16},{28,20},{1,25},{... | collective-permute-start | bytes 737288 | tf_op jit(solution)/shard_map/ppermute | solution.py:34
  37.2 44.6 %collective-permute-start.13 = (bf16[64,2560]{1,0:T(8,128)(2,1)S(1)}, bf16[64,2560]{1,0:T(8,128)(2,1)S(1)}, u32[]{:S(2)}, u32[]{:S(2)}) collective-permute-start(bf16[64,2560]{1,0:T(8,128)(2,1)S(1)} %get-tuple-element.40), channel_id=1, source_target_pairs={{0,16},{4,20},{8,24},{12,28},{16,0},{20,4},{24,8},{28,12},{1,17},{... | collective-permute-start | bytes 983048 | tf_op jit(solution)/shard_map/ppermute | solution.py:34
  59.4 21.1 %collective-permute-start.12 = (bf16[64,2560]{1,0:T(8,128)(2,1)S(1)}, bf16[64,2560]{1,0:T(8,128)(2,1)S(1)}, u32[]{:S(2)}, u32[]{:S(2)}) collective-permute-start(bf16[64,2560]{1,0:T(8,128)(2,1)S(1)} %get-tuple-element.40), channel_id=1, source_target_pairs={{0,8},{4,12},{8,16},{12,20},{16,24},{20,28},{24,0},{28,4},{1,9},{5... | collective-permute-start | bytes 983048 | tf_op jit(solution)/shard_map/ppermute | solution.py:34
  61.6 22.1 %collective-permute-start.14 = (bf16[64,2560]{1,0:T(8,128)(2,1)S(1)}, bf16[64,2560]{1,0:T(8,128)(2,1)S(1)}, u32[]{:S(2)}, u32[]{:S(2)}) collective-permute-start(bf16[64,2560]{1,0:T(8,128)(2,1)S(1)} %get-tuple-element.40), channel_id=1, source_target_pairs={{0,24},{4,28},{8,0},{12,4},{16,8},{20,12},{24,16},{28,20},{1,25},{... | collective-permute-start | bytes 983048 | tf_op jit(solution)/shard_map/ppermute | solution.py:34
  69.6 15.4 %collective-permute-start.26 = (bf16[4,64,1024]{2,1,0:T(8,128)(2,1)S(1)}, bf16[4,64,1024]{2,1,0:T(8,128)(2,1)S(1)}, u32[]{:S(2)}, u32[]{:S(2)}) collective-permute-start(bf16[4,64,1024]{2,1,0:T(8,128)(2,1)S(1)} %get-tuple-element.89), channel_id=1, source_target_pairs={{0,4},{4,0},{8,12},{12,8},{16,20},{20,16},{24,28},{28,24},{1,5},{5... | collective-permute-start | bytes 1572872 | tf_op jit(solution)/shard_map/ppermute | solution.py:28
  71.6 15.8 %collective-permute-start.24 = (bf16[4,64,1024]{2,1,0:T(8,128)(2,1)S(1)}, bf16[4,64,1024]{2,1,0:T(8,128)(2,1)S(1)}, u32[]{:S(2)}, u32[]{:S(2)}) collective-permute-start(bf16[4,64,1024]{2,1,0:T(8,128)(2,1)S(1)} %get-tuple-element.90), channel_id=1, source_target_pairs={{0,2},{1,3},{2,0},{3,1},{4,6},{5,7},{6,4},{7,5},{8,10},{9,11},{10,... | collective-permute-start | bytes 1572872 | tf_op jit(solution)/shard_map/ppermute | solution.py:24
  83.7 27.2 %collective-permute-start.1 = (bf16[512,1024]{1,0:T(8,128)(2,1)S(1)}, bf16[512,1024]{1,0:T(8,128)(2,1)S(1)}, u32[]{:S(2)}, u32[]{:S(2)}) collective-permute-start(bf16[512,1024]{1,0:T(8,128)(2,1)S(1)} %pad_maximum_fusion.16), channel_id=1, source_target_pairs={{0,1},{1,0},{2,3},{3,2},{4,5},{5,4},{6,7},{7,6},{8,9},{9,8},{10,11... | collective-permute-start | bytes 3145736 | tf_op jit(solution)/shard_map/ppermute | solution.py:20
  85.0 21.8 %collective-permute-start.17 = (bf16[4,32,2560]{2,1,0:T(8,128)(2,1)S(1)}, bf16[4,32,2560]{2,1,0:T(8,128)(2,1)S(1)}, u32[]{:S(2)}, u32[]{:S(2)}) collective-permute-start(bf16[4,32,2560]{2,1,0:T(8,128)(2,1)S(1)} %get-tuple-element.72), channel_id=1, source_target_pairs={{0,4},{4,0},{8,12},{12,8},{16,20},{20,16},{24,28},{28,24},{1,5},{5... | collective-permute-start | bytes 1966088 | tf_op jit(solution)/shard_map/ppermute | solution.py:28
  87.4 21.9 %collective-permute-start.15 = (bf16[4,32,2560]{2,1,0:T(8,128)(2,1)S(1)}, bf16[4,32,2560]{2,1,0:T(8,128)(2,1)S(1)}, u32[]{:S(2)}, u32[]{:S(2)}) collective-permute-start(bf16[4,32,2560]{2,1,0:T(8,128)(2,1)S(1)} %get-tuple-element.73), channel_id=1, source_target_pairs={{0,2},{1,3},{2,0},{3,1},{4,6},{5,7},{6,4},{7,5},{8,10},{9,11},{10,... | collective-permute-start | bytes 1966088 | tf_op jit(solution)/shard_map/ppermute | solution.py:24
  95.1 34.3 %collective-permute-start.25 = (bf16[2,4,64,1024]{3,2,1,0:T(8,128)(2,1)S(1)}, bf16[2,4,64,1024]{3,2,1,0:T(8,128)(2,1)S(1)}, u32[]{:S(2)}, u32[]{:S(2)}) collective-permute-start(bf16[2,4,64,1024]{3,2,1,0:T(8,128)(2,1)S(1)} %pad_maximum_fusion.19), channel_id=1, source_target_pairs={{0,4},{4,0},{8,12},{12,8},{16,20},{20,16},{24,28},{28,24},{1,5},{5... | collective-permute-start | bytes 3145736 | tf_op jit(solution)/shard_map/ppermute | solution.py:28
  95.4 151.3 %collective-permute-start.27 = (bf16[2,4,64,1024]{3,2,1,0:T(8,128)(2,1)}, bf16[2,4,64,1024]{3,2,1,0:T(8,128)(2,1)}, u32[]{:S(2)}, u32[]{:S(2)}) collective-permute-start(bf16[2,4,64,1024]{3,2,1,0:T(8,128)(2,1)} %pad_maximum_fusion.20), channel_id=1, source_target_pairs={{0,2},{1,3},{2,0},{3,1},{4,6},{5,7},{6,4},{7,5},{8,10},{9,11},{10,... | collective-permute-start | bytes 3145736 | tf_op jit(solution)/shard_map/ppermute | solution.py:24
  106.9 43.5 %collective-permute-start.7 = (bf16[2,4,32,1920]{3,2,1,0:T(8,128)(2,1)S(1)}, bf16[2,4,32,1920]{3,2,1,0:T(8,128)(2,1)S(1)}, u32[]{:S(2)}, u32[]{:S(2)}) collective-permute-start(bf16[2,4,32,1920]{3,2,1,0:T(8,128)(2,1)S(1)} %pad_maximum_fusion.25), channel_id=1, source_target_pairs={{0,4},{4,0},{8,12},{12,8},{16,20},{20,16},{24,28},{28,24},{1,5},{5... | collective-permute-start | bytes 2949128 | tf_op jit(solution)/shard_map/ppermute | solution.py:28
  109.3 43.4 %collective-permute-start.9 = (bf16[2,4,32,1920]{3,2,1,0:T(8,128)(2,1)S(1)}, bf16[2,4,32,1920]{3,2,1,0:T(8,128)(2,1)S(1)}, u32[]{:S(2)}, u32[]{:S(2)}) collective-permute-start(bf16[2,4,32,1920]{3,2,1,0:T(8,128)(2,1)S(1)} %pad_maximum_fusion.26), channel_id=1, source_target_pairs={{0,2},{1,3},{2,0},{3,1},{4,6},{5,7},{6,4},{7,5},{8,10},{9,11},{10,... | collective-permute-start | bytes 2949128 | tf_op jit(solution)/shard_map/ppermute | solution.py:24
  110.9 105.0 %collective-permute-start.16 = (bf16[2,4,32,2560]{3,2,1,0:T(8,128)(2,1)}, bf16[2,4,32,2560]{3,2,1,0:T(8,128)(2,1)}, u32[]{:S(2)}, u32[]{:S(2)}) collective-permute-start(bf16[2,4,32,2560]{3,2,1,0:T(8,128)(2,1)} %pad_maximum_fusion.11), channel_id=1, source_target_pairs={{0,4},{4,0},{8,12},{12,8},{16,20},{20,16},{24,28},{28,24},{1,5},{5... | collective-permute-start | bytes 3932168 | tf_op jit(solution)/shard_map/ppermute | solution.py:28
  129.4 89.0 %collective-permute-start.18 = (bf16[2,4,32,2560]{3,2,1,0:T(8,128)(2,1)}, bf16[2,4,32,2560]{3,2,1,0:T(8,128)(2,1)}, u32[]{:S(2)}, u32[]{:S(2)}) collective-permute-start(bf16[2,4,32,2560]{3,2,1,0:T(8,128)(2,1)} %pad_maximum_fusion.12), channel_id=1, source_target_pairs={{0,2},{1,3},{2,0},{3,1},{4,6},{5,7},{6,4},{7,5},{8,10},{9,11},{10,... | collective-permute-start | bytes 3932168 | tf_op jit(solution)/shard_map/ppermute | solution.py:24
  223.5 15.5 %collective-permute-start.19 = (bf16[16,1,32,1024]{3,2,1,0:T(8,128)(2,1)S(1)}, bf16[16,1,32,1024]{3,2,1,0:T(8,128)(2,1)}, u32[]{:S(2)}, u32[]{:S(2)}) collective-permute-start(bf16[16,1,32,1024]{3,2,1,0:T(8,128)(2,1)S(1)} %bitcast.460), channel_id=1, source_target_pairs={{0,1},{1,0},{2,3},{3,2},{4,5},{5,4},{6,7},{7,6},{8,9},{9,8},{10,11... | collective-permute-start | bytes 3145736 | tf_op jit(solution)/shard_map/ppermute | solution.py:20
  263.9 19.2 %collective-permute-start.28 = (bf16[512,1024]{1,0:T(8,128)(2,1)}, bf16[512,1024]{1,0:T(8,128)(2,1)}, u32[]{:S(2)}, u32[]{:S(2)}) collective-permute-start(bf16[512,1024]{1,0:T(8,128)(2,1)} %slice.481), channel_id=1, source_target_pairs={{0,1},{1,0},{2,3},{3,2},{4,5},{5,4},{6,7},{7,6},{8,9},{9,8},{10,11... | collective-permute-start | bytes 3145736 | tf_op jit(solution)/shard_map/ppermute | solution.py:20
  289.7 17.9 %collective-permute-start.31 = (bf16[512,1024]{1,0:T(8,128)(2,1)}, bf16[512,1024]{1,0:T(8,128)(2,1)}, u32[]{:S(2)}, u32[]{:S(2)}) collective-permute-start(bf16[512,1024]{1,0:T(8,128)(2,1)} %get-tuple-element.34), channel_id=1, source_target_pairs={{0,1},{1,0},{2,3},{3,2},{4,5},{5,4},{6,7},{7,6},{8,9},{9,8},{10,11... | collective-permute-start | bytes 3145736 | tf_op jit(solution)/shard_map/ppermute | solution.py:20
  328.4 20.1 %collective-permute-start.32 = (bf16[512,1024]{1,0:T(8,128)(2,1)S(1)}, bf16[512,1024]{1,0:T(8,128)(2,1)S(1)}, u32[]{:S(2)}, u32[]{:S(2)}) collective-permute-start(bf16[512,1024]{1,0:T(8,128)(2,1)S(1)} %slice.480), channel_id=1, source_target_pairs={{0,1},{1,0},{2,3},{3,2},{4,5},{5,4},{6,7},{7,6},{8,9},{9,8},{10,11... | collective-permute-start | bytes 3145736 | tf_op jit(solution)/shard_map/ppermute | solution.py:20
  342.2 26.8 %collective-permute-start.62 = (bf16[4,2,64,1024]{3,2,0,1:T(8,128)(2,1)}, bf16[4,2,64,1024]{3,2,0,1:T(8,128)(2,1)}, u32[]{:S(2)}, u32[]{:S(2)}) collective-permute-start(bf16[4,2,64,1024]{3,2,0,1:T(8,128)(2,1)} %bitcast.436), channel_id=1, source_target_pairs={{0,4},{4,0},{8,12},{12,8},{16,20},{20,16},{24,28},{28,24},{1,5},{5... | collective-permute-start | bytes 3145736 | tf_op jit(solution)/shard_map/ppermute | solution.py:28
  344.7 28.6 %collective-permute-start.60 = (bf16[4,2,64,1024]{3,2,0,1:T(8,128)(2,1)}, bf16[4,2,64,1024]{3,2,0,1:T(8,128)(2,1)}, u32[]{:S(2)}, u32[]{:S(2)}) collective-permute-start(bf16[4,2,64,1024]{3,2,0,1:T(8,128)(2,1)} %bitcast.437), channel_id=1, source_target_pairs={{0,2},{1,3},{2,0},{3,1},{4,6},{5,7},{6,4},{7,5},{8,10},{9,11},{10,... | collective-permute-start | bytes 3145736 | tf_op jit(solution)/shard_map/ppermute | solution.py:24
  346.0 42.8 %collective-permute-start.54 = (bf16[4,2,32,2048]{3,2,1,0:T(8,128)(2,1)}, bf16[4,2,32,2048]{3,2,1,0:T(8,128)(2,1)}, u32[]{:S(2)}, u32[]{:S(2)}) collective-permute-start(bf16[4,2,32,2048]{3,2,1,0:T(8,128)(2,1)} %dynamic-slice_bitcast_fusion.2), channel_id=1, source_target_pairs={{0,4},{4,0},{8,12},{12,8},{16,20},{20,16},{24,28},{28,24},{1,5},{5... | collective-permute-start | bytes 3145736 | tf_op jit(solution)/shard_map/ppermute | solution.py:28
  347.3 44.4 %collective-permute-start.52 = (bf16[4,2,32,2048]{3,2,0,1:T(8,128)(2,1)}, bf16[4,2,32,2048]{3,2,0,1:T(8,128)(2,1)}, u32[]{:S(2)}, u32[]{:S(2)}) collective-permute-start(bf16[4,2,32,2048]{3,2,0,1:T(8,128)(2,1)} %bitcast.438), channel_id=1, source_target_pairs={{0,2},{1,3},{2,0},{3,1},{4,6},{5,7},{6,4},{7,5},{8,10},{9,11},{10,... | collective-permute-start | bytes 3145736 | tf_op jit(solution)/shard_map/ppermute | solution.py:24
  363.0 31.6 %collective-permute-start.33 = (bf16[512,512]{1,0:T(8,128)(2,1)S(1)}, bf16[512,512]{1,0:T(8,128)(2,1)S(1)}, u32[]{:S(2)}, u32[]{:S(2)}) collective-permute-start(bf16[512,512]{1,0:T(8,128)(2,1)S(1)} %bitcast.490), channel_id=1, source_target_pairs={{0,1},{1,0},{2,3},{3,2},{4,5},{5,4},{6,7},{7,6},{8,9},{9,8},{10,11... | collective-permute-start | bytes 1572872 | tf_op jit(solution)/shard_map/ppermute | solution.py:20
  369.0 166.1 %collective-permute-start.42 = (bf16[16,32,1024]{2,1,0:T(8,128)(2,1)}, bf16[16,32,1024]{2,1,0:T(8,128)(2,1)}, u32[]{:S(2)}, u32[]{:S(2)}) collective-permute-start(bf16[16,32,1024]{2,1,0:T(8,128)(2,1)} %dynamic-slice_bitcast_fusion.3), channel_id=1, source_target_pairs={{0,1},{1,0},{2,3},{3,2},{4,5},{5,4},{6,7},{7,6},{8,9},{9,8},{10,11... | collective-permute-start | bytes 3145736 | tf_op jit(solution)/shard_map/ppermute | solution.py:20
  373.3 110.9 %collective-permute-start.63 = (bf16[4,64,1024]{2,1,0:T(8,128)(2,1)}, bf16[4,64,1024]{2,1,0:T(8,128)(2,1)}, u32[]{:S(2)}, u32[]{:S(2)}) collective-permute-start(bf16[4,64,1024]{2,1,0:T(8,128)(2,1)} %dynamic-slice_bitcast_fusion.6), channel_id=1, source_target_pairs={{0,2},{1,3},{2,0},{3,1},{4,6},{5,7},{6,4},{7,5},{8,10},{9,11},{10,... | collective-permute-start | bytes 1572872 | tf_op jit(solution)/shard_map/ppermute | solution.py:24
  388.9 96.7 %collective-permute-start.61 = (bf16[4,64,1024]{2,1,0:T(8,128)(2,1)}, bf16[4,64,1024]{2,1,0:T(8,128)(2,1)}, u32[]{:S(2)}, u32[]{:S(2)}) collective-permute-start(bf16[4,64,1024]{2,1,0:T(8,128)(2,1)} %dynamic-slice_bitcast_fusion.7), channel_id=1, source_target_pairs={{0,4},{4,0},{8,12},{12,8},{16,20},{20,16},{24,28},{28,24},{1,5},{5... | collective-permute-start | bytes 1572872 | tf_op jit(solution)/shard_map/ppermute | solution.py:28
  391.7 97.3 %collective-permute-start.55 = (bf16[4,32,2048]{2,1,0:T(8,128)(2,1)}, bf16[4,32,2048]{2,1,0:T(8,128)(2,1)}, u32[]{:S(2)}, u32[]{:S(2)}) collective-permute-start(bf16[4,32,2048]{2,1,0:T(8,128)(2,1)} %dynamic-slice_bitcast_fusion.8), channel_id=1, source_target_pairs={{0,2},{1,3},{2,0},{3,1},{4,6},{5,7},{6,4},{7,5},{8,10},{9,11},{10,... | collective-permute-start | bytes 1572872 | tf_op jit(solution)/shard_map/ppermute | solution.py:24
  395.6 94.5 %collective-permute-start.53 = (bf16[4,32,2048]{2,1,0:T(8,128)(2,1)}, bf16[4,32,2048]{2,1,0:T(8,128)(2,1)}, u32[]{:S(2)}, u32[]{:S(2)}) collective-permute-start(bf16[4,32,2048]{2,1,0:T(8,128)(2,1)} %dynamic-slice_bitcast_fusion.9), channel_id=1, source_target_pairs={{0,4},{4,0},{8,12},{12,8},{16,20},{20,16},{24,28},{28,24},{1,5},{5... | collective-permute-start | bytes 1572872 | tf_op jit(solution)/shard_map/ppermute | solution.py:28
  487.0 43.5 %collective-permute-start.64 = (bf16[128,1024]{1,0:T(8,128)(2,1)S(1)}, bf16[128,1024]{1,0:T(8,128)(2,1)S(1)}, u32[]{:S(2)}, u32[]{:S(2)}) collective-permute-start(bf16[128,1024]{1,0:T(8,128)(2,1)S(1)} %get-tuple-element.79), channel_id=1, source_target_pairs={{0,8},{4,12},{8,16},{12,20},{16,24},{20,28},{24,0},{28,4},{1,9},{5... | collective-permute-start | bytes 786440 | tf_op jit(solution)/shard_map/ppermute | solution.py:34
  491.4 15.8 %collective-permute-start.56 = (bf16[64,2048]{1,0:T(8,128)(2,1)S(1)}, bf16[64,2048]{1,0:T(8,128)(2,1)S(1)}, u32[]{:S(2)}, u32[]{:S(2)}) collective-permute-start(bf16[64,2048]{1,0:T(8,128)(2,1)S(1)} %get-tuple-element.82), channel_id=1, source_target_pairs={{0,8},{4,12},{8,16},{12,20},{16,24},{20,28},{24,0},{28,4},{1,9},{5... | collective-permute-start | bytes 786440 | tf_op jit(solution)/shard_map/ppermute | solution.py:34
  492.5 25.5 %collective-permute-start.57 = (bf16[64,2048]{1,0:T(8,128)(2,1)S(1)}, bf16[64,2048]{1,0:T(8,128)(2,1)S(1)}, u32[]{:S(2)}, u32[]{:S(2)}) collective-permute-start(bf16[64,2048]{1,0:T(8,128)(2,1)S(1)} %get-tuple-element.83), channel_id=1, source_target_pairs={{0,16},{4,20},{8,24},{12,28},{16,0},{20,4},{24,8},{28,12},{1,17},{... | collective-permute-start | bytes 786440 | tf_op jit(solution)/shard_map/ppermute | solution.py:34
  493.1 29.3 %collective-permute-start.58 = (bf16[64,2048]{1,0:T(8,128)(2,1)S(1)}, bf16[64,2048]{1,0:T(8,128)(2,1)S(1)}, u32[]{:S(2)}, u32[]{:S(2)}) collective-permute-start(bf16[64,2048]{1,0:T(8,128)(2,1)S(1)} %get-tuple-element.84), channel_id=1, source_target_pairs={{0,24},{4,28},{8,0},{12,4},{16,8},{20,12},{24,16},{28,20},{1,25},{... | collective-permute-start | bytes 786440 | tf_op jit(solution)/shard_map/ppermute | solution.py:34
  507.2 23.4 %collective-permute-start.65 = (bf16[128,1024]{1,0:T(8,128)(2,1)S(1)}, bf16[128,1024]{1,0:T(8,128)(2,1)S(1)}, u32[]{:S(2)}, u32[]{:S(2)}) collective-permute-start(bf16[128,1024]{1,0:T(8,128)(2,1)S(1)} %get-tuple-element.80), channel_id=1, source_target_pairs={{0,16},{4,20},{8,24},{12,28},{16,0},{20,4},{24,8},{28,12},{1,17},{... | collective-permute-start | bytes 786440 | tf_op jit(solution)/shard_map/ppermute | solution.py:34
  518.0 16.1 %collective-permute-start.66 = (bf16[128,1024]{1,0:T(8,128)(2,1)S(1)}, bf16[128,1024]{1,0:T(8,128)(2,1)S(1)}, u32[]{:S(2)}, u32[]{:S(2)}) collective-permute-start(bf16[128,1024]{1,0:T(8,128)(2,1)S(1)} %get-tuple-element.81), channel_id=1, source_target_pairs={{0,24},{4,28},{8,0},{12,4},{16,8},{20,12},{24,16},{28,20},{1,25},{... | collective-permute-start | bytes 786440 | tf_op jit(solution)/shard_map/ppermute | solution.py:34
  522.4 17.2 %collective-permute-start.34 = (bf16[512,1024]{1,0:T(8,128)(2,1)}, bf16[512,1024]{1,0:T(8,128)(2,1)S(1)}, u32[]{:S(2)}, u32[]{:S(2)}) collective-permute-start(bf16[512,1024]{1,0:T(8,128)(2,1)} %slice.479), channel_id=1, source_target_pairs={{0,1},{1,0},{2,3},{3,2},{4,5},{5,4},{6,7},{7,6},{8,9},{9,8},{10,11... | collective-permute-start | bytes 3145736 | tf_op jit(solution)/shard_map/ppermute | solution.py:20
  552.7 102.9 %collective-permute-start.41 = (f32[256,1024]{1,0:T(8,128)}, f32[256,1024]{1,0:T(8,128)}, u32[]{:S(2)}, u32[]{:S(2)}) collective-permute-start(f32[256,1024]{1,0:T(8,128)} %slice.371), channel_id=1, source_target_pairs={{0,2},{1,3},{2,0},{3,1},{4,6},{5,7},{6,4},{7,5},{8,10},{9,11},{10,... | collective-permute-start | bytes 3145736 | tf_op jit(solution)/shard_map/ppermute | solution.py:24
  556.1 46.6 %collective-permute-start.44 = (bf16[4,2,32,2304]{3,2,0,1:T(8,128)(2,1)S(1)}, bf16[4,2,32,2304]{3,2,0,1:T(8,128)(2,1)}, u32[]{:S(2)}, u32[]{:S(2)}) collective-permute-start(bf16[4,2,32,2304]{3,2,0,1:T(8,128)(2,1)S(1)} %dynamic-slice_bitcast_fusion.1), channel_id=1, source_target_pairs={{0,2},{1,3},{2,0},{3,1},{4,6},{5,7},{6,4},{7,5},{8,10},{9,11},{10,... | collective-permute-start | bytes 3538952 | tf_op jit(solution)/shard_map/ppermute | solution.py:24
  565.9 39.1 %collective-permute-start.46 = (bf16[4,2,32,2304]{3,2,0,1:T(8,128)(2,1)}, bf16[4,2,32,2304]{3,2,0,1:T(8,128)(2,1)}, u32[]{:S(2)}, u32[]{:S(2)}) collective-permute-start(bf16[4,2,32,2304]{3,2,0,1:T(8,128)(2,1)} %dynamic-slice_bitcast_fusion), channel_id=1, source_target_pairs={{0,4},{4,0},{8,12},{12,8},{16,20},{20,16},{24,28},{28,24},{1,5},{5... | collective-permute-start | bytes 3538952 | tf_op jit(solution)/shard_map/ppermute | solution.py:28
  567.6 59.5 %collective-permute-start.40 = (f32[224]{0:T(256)S(1)}, f32[224]{0:T(256)S(1)}, u32[]{:S(2)}, u32[]{:S(2)}) collective-permute-start(f32[224]{0:T(256)S(1)} %pad_maximum_fusion.39), channel_id=1, source_target_pairs={{0,1},{1,0},{2,3},{3,2},{4,5},{5,4},{6,7},{7,6},{8,9},{9,8},{10,11... | collective-permute-start | bytes 2696 | tf_op jit(solution)/shard_map/ppermute | solution.py:20
  622.4 23.2 %collective-permute-start.49 = (bf16[64,2304]{1,0:T(8,128)(2,1)}, bf16[64,2304]{1,0:T(8,128)(2,1)}, u32[]{:S(2)}, u32[]{:S(2)}) collective-permute-start(bf16[64,2304]{1,0:T(8,128)(2,1)} %get-tuple-element.75), channel_id=1, source_target_pairs={{0,16},{4,20},{8,24},{12,28},{16,0},{20,4},{24,8},{28,12},{1,17},{... | collective-permute-start | bytes 884744 | tf_op jit(solution)/shard_map/ppermute | solution.py:34
  625.6 26.8 %collective-permute-start.50 = (bf16[64,2304]{1,0:T(8,128)(2,1)}, bf16[64,2304]{1,0:T(8,128)(2,1)}, u32[]{:S(2)}, u32[]{:S(2)}) collective-permute-start(bf16[64,2304]{1,0:T(8,128)(2,1)} %get-tuple-element.76), channel_id=1, source_target_pairs={{0,24},{4,28},{8,0},{12,4},{16,8},{20,12},{24,16},{28,20},{1,25},{... | collective-permute-start | bytes 884744 | tf_op jit(solution)/shard_map/ppermute | solution.py:34
  (122 other events, 1379.6 us)

commit v2 on v1

v2 whole, which is shorter than its diff:
```python
import math

import jax
import jax.numpy as jnp
from jax import lax
from jax.experimental import pallas as pl
from jax.experimental.pallas import tpu as pltpu
from jax.sharding import PartitionSpec as P

HD = 64
TE = 256

b16 = jnp.bfloat16
f32 = jnp.float32
highest = lax.Precision.HIGHEST
epsilon = 1e-05
little = pl.CostEstimate(flops=1, transcendentals=0, bytes_accessed=1)


def swap_core(v):
    return lax.ppermute(v, "core", [(0, 1), (1, 0)])


def swap_x(v):
    return lax.ppermute(v, "x", [(0, 1), (1, 0)])


def swap_y(v):
    return lax.ppermute(v, "y", [(0, 1), (1, 0)])


def shift_z(v, k):
    depth = lax.axis_size("z")
    return lax.ppermute(v, "z", [(i, (i + k) % depth) for i in range(depth)])


def place():
    return tuple(lax.axis_index(a) for a in ("x", "core", "y", "z")) + (lax.axis_size("z"),)


def pick(v, index, axis=0):
    return lax.dynamic_index_in_dim(v, index, axis, False)


def unread(deps):
    return [pl.BlockSpec(memory_space=pl.ANY)] * len(deps)


def move(place_of, sources, outs, copies, deps=()):
    def kernel(where, *refs):
        x, c, y, z = (where[i] for i in range(4))
        given = refs[: len(sources)]
        made = refs[len(sources) + len(deps) :]
        for source, read, out, write in copies(x, c, y, z):
            made[out][write] = given[source][read]

    near = pl.BlockSpec(memory_space=pltpu.VMEM)
    return pl.pallas_call(
        kernel,
        in_specs=[pl.BlockSpec(memory_space=pltpu.SMEM)] + [near] * len(sources) + unread(deps),
        out_specs=[near] * len(outs),
        out_shape=outs,
        compiler_params=pltpu.CompilerParams(vmem_limit_bytes=32 << 20),
        cost_estimate=little,
        name="move",
    )(place_of, *sources, *deps)


def tie(*values):
    return lax.optimization_barrier(values)


def gather_z(piece, tiled=False):
    return [piece] + [shift_z(piece, k) for k in range(1, place()[4])]


def stack_z(pieces, tiled=False, deps=()):
    x, c, y, z, depth = place()
    rows, cols = pieces[0].shape
    half = rows // 2
    if tiled:

        def copies(x, c, y, z):
            return [
                (k, pl.ds(h * half, half), h, lax.rem(z - k + depth, depth))
                for k in range(depth)
                for h in range(2)
            ]

        shape = jax.ShapeDtypeStruct((depth, half, cols), b16)
        return list(move(jnp.stack([x, c, y, z]), pieces, [shape, shape], copies, deps))
    stack = jnp.zeros((depth, rows, cols), b16)
    for k in range(depth):
        stack = lax.dynamic_update_slice(stack, pieces[k][None], ((z - k) % depth, 0, 0))
    return [stack[:, :half], stack[:, half:]]


def gather_near(stacks):
    top, low = stacks
    return top, low, swap_x(top), swap_y(low)


def gather_far(near):
    top, low, top_x, low_y = near
    return swap_y(jnp.stack([top, top_x])), swap_x(jnp.stack([low, low_y]))


def assemble(near, far, cuts, tiled=False):
    x, c, y, z, depth = place()
    top, low, top_x, low_y = near
    top_far, low_far = far
    half, cols = top.shape[1:]
    rows = 2 * half
    if tiled:
        every = slice(None)

        def copies(x, c, y, z):
            made = []
            for n in range(len(cuts) - 1):
                run = pl.ds(cuts[n], cuts[n + 1] - cuts[n])
                one = (every, every, run)
                up, down = pl.ds(0, half), pl.ds(half, half)
                made += [
                    (0, one, n, (every, y, x, up)),
                    (2, one, n, (every, y, 1 - x, up)),
                    (4, (0,) + one, n, (every, 1 - y, x, up)),
                    (4, (1,) + one, n, (every, 1 - y, 1 - x, up)),
                    (1, one, n, (every, y, x, down)),
                    (3, one, n, (every, 1 - y, x, down)),
                    (5, (0,) + one, n, (every, y, 1 - x, down)),
                    (5, (1,) + one, n, (every, 1 - y, 1 - x, down)),
                ]
            return made

        shapes = [
            jax.ShapeDtypeStruct((depth, 2, 2, rows, cuts[n + 1] - cuts[n]), top.dtype)
            for n in range(len(cuts) - 1)
        ]
        parts = move(
            jnp.stack([x, c, y, z]), [top, low, top_x, low_y, top_far, low_far], shapes, copies
        )
        return [p.reshape(4 * depth, rows, -1) for p in parts]
    whole = jnp.zeros((depth, 2, 2, rows, cols), top.dtype)

    def put(whole, part, yy, xx, at):
        return lax.dynamic_update_slice(whole, part[:, None, None], (0, yy, xx, at, 0))

    whole = put(whole, top, y, x, 0)
    whole = put(whole, top_x, y, 1 - x, 0)
    whole = put(whole, top_far[0], 1 - y, x, 0)
    whole = put(whole, top_far[1], 1 - y, 1 - x, 0)
    whole = put(whole, low, y, x, half)
    whole = put(whole, low_y, 1 - y, x, half)
    whole = put(whole, low_far[0], y, 1 - x, half)
    whole = put(whole, low_far[1], 1 - y, 1 - x, half)
    whole = whole.reshape(4 * depth, rows, cols)
    return [whole[:, :, cuts[n] : cuts[n + 1]] for n in range(len(cuts) - 1)]


def add_low(a, b):
    return (a.astype(f32) + b.astype(f32)).astype(a.dtype)


def exchange(v, axes):
    return lax.all_to_all(v, axes, 0, 0, tiled=True)


def add_up(v):
    total = v[0].astype(f32)
    for i in range(1, len(v)):
        total = total + v[i].astype(f32)
    return total


def add_near(got, where, tiled):
    depth = got.shape[1]
    if not tiled:
        z = lax.axis_index("z")
        both = add_up(got).astype(b16)
        return [pick(both, (z + k) % depth) for k in range(depth)]

    def kernel(where, got, *outs):
        for k in range(depth):
            at = lax.rem(where[3] + k, depth)
            total = got[0, at].astype(f32)
            for i in range(1, got.shape[0]):
                total = total + got[i, at].astype(f32)
            outs[k][...] = total.astype(b16)

    near = pl.BlockSpec(memory_space=pltpu.VMEM)
    return pl.pallas_call(
        kernel,
        in_specs=[pl.BlockSpec(memory_space=pltpu.SMEM), near],
        out_specs=[near] * depth,
        out_shape=[jax.ShapeDtypeStruct(got.shape[2:], b16)] * depth,
        compiler_params=pltpu.CompilerParams(vmem_limit_bytes=32 << 20),
        cost_estimate=little,
        name="add_near",
    )(where, got)


def stack_terms(first, second):
    chips, top, width = first.shape
    rows, runs = second.shape[1], second.shape[2] // width
    shape = (chips, top + runs * rows, width)
    if top % 16 or rows % 16:
        return jnp.concatenate([first] + jnp.split(second, runs, axis=2), axis=1)

    def kernel(first, second, made):
        made[:, :top] = first[...]
        for n in range(runs):
            made[:, top + n * rows : top + (n + 1) * rows] = second[
                :, :, n * width : (n + 1) * width
            ]

    near = pl.BlockSpec(memory_space=pltpu.VMEM)
    return pl.pallas_call(
        kernel,
        in_specs=[near, near],
        out_specs=near,
        out_shape=jax.ShapeDtypeStruct(shape, first.dtype),
        compiler_params=pltpu.CompilerParams(vmem_limit_bytes=40 << 20),
        cost_estimate=little,
        name="stack_terms",
    )(first, second)


def send_z(parts):
    return [parts[0]] + [shift_z(v, k) for k, v in enumerate(parts) if k]


def regroup(v, cuts):
    runs = [slice(cuts[n], cuts[n + 1]) for n in range(len(cuts) - 1)]
    if v.shape[2] % 16 or v.shape[3] % 128:
        return [jnp.swapaxes(v[..., run], 0, 1) for run in runs]

    def kernel(given, *made):
        for out, run in zip(made, runs):
            for i in range(v.shape[0]):
                for j in range(v.shape[1]):
                    out[j, i] = given[i, j, :, run]

    near = pl.BlockSpec(memory_space=pltpu.VMEM)
    return pl.pallas_call(
        kernel,
        in_specs=[near],
        out_specs=[near] * len(runs),
        out_shape=[
            jax.ShapeDtypeStruct((v.shape[1], v.shape[0], v.shape[2], r.stop - r.start), v.dtype)
            for r in runs
        ],
        compiler_params=pltpu.CompilerParams(vmem_limit_bytes=32 << 20),
        cost_estimate=little,
        name="regroup",
    )(v)


def swap_order(v):
    return regroup(v, [0, v.shape[3]])[0]


def scatter_send(parts, where, tiled, deps=()):
    x, c, y, z, depth = place()
    chips, rows, cols = parts.shape
    half = rows // 2
    if not tiled:
        grid = parts.reshape(depth, 2, 2, rows, cols)
        return [pick(grid[:, :, :, :half], 1 - x, 2), pick(grid[:, :, :, half:], 1 - y, 1)]

    def copies(x, c, y, z):
        return [
            (0, (slice(None), slice(None), 1 - x, 0), 0, slice(None)),
            (0, (slice(None), 1 - y, slice(None), 1), 1, slice(None)),
        ]

    shape = jax.ShapeDtypeStruct((depth, 2, half, cols), parts.dtype)
    grid = parts.reshape(depth, 2, 2, 2, half, cols)
    return list(move(where, [grid], [shape, shape], copies, deps))


def scatter_near(parts, got, where, tiled):
    x, c, y, z, depth = place()
    chips, rows, cols = parts.shape
    half = rows // 2
    if not tiled:
        grid = parts.reshape(depth, 2, 2, rows, cols)
        top = add_low(pick(grid[:, :, :, :half], x, 2), got[0])
        low = add_low(pick(grid[:, :, :, half:], y, 1), got[1])
        return pick(top, y, 1), pick(top, 1 - y, 1), pick(low, x, 1), pick(low, 1 - x, 1)

    def kernel(where, grid, top, low, keep_t, send_t, keep_l, send_l):
        x, y = where[0], where[2]
        for out, yy in ((keep_t, y), (send_t, 1 - y)):
            out[...] = add_low(grid[:, yy, x, 0], top[:, yy])
        for out, xx in ((keep_l, x), (send_l, 1 - x)):
            out[...] = add_low(grid[:, y, xx, 1], low[:, xx])

    near = pl.BlockSpec(memory_space=pltpu.VMEM)
    shape = jax.ShapeDtypeStruct((depth, half, cols), parts.dtype)
    return pl.pallas_call(
        kernel,
        in_specs=[pl.BlockSpec(memory_space=pltpu.SMEM)] + [near] * 3,
        out_specs=[near] * 4,
        out_shape=[shape] * 4,
        compiler_params=pltpu.CompilerParams(vmem_limit_bytes=32 << 20),
        cost_estimate=little,
        name="scatter_near",
    )(where, parts.reshape(depth, 2, 2, 2, half, cols), got[0], got[1])


def scatter_far(keep, got, where, tiled):
    x, c, y, z, depth = place()
    half, cols = keep[0].shape[1:]
    if not tiled:
        both = jnp.concatenate([add_low(k, g) for k, g in zip(keep, got)], axis=1)
        return [pick(both, (z + k) % depth) for k in range(depth)]

    def kernel(where, top, low, top_got, low_got, *outs):
        for k in range(depth):
            at = lax.rem(where[3] + k, depth)
            outs[k][:half] = add_low(top[at], top_got[at])
            outs[k][half:] = add_low(low[at], low_got[at])

    near = pl.BlockSpec(memory_space=pltpu.VMEM)
    shape = jax.ShapeDtypeStruct((2 * half, cols), keep[0].dtype)
    return pl.pallas_call(
        kernel,
        in_specs=[pl.BlockSpec(memory_space=pltpu.SMEM)] + [near] * 4,
        out_specs=[near] * depth,
        out_shape=[shape] * depth,
        compiler_params=pltpu.CompilerParams(vmem_limit_bytes=32 << 20),
        cost_estimate=little,
        name="scatter_far",
    )(where, keep[0], keep[1], got[0], got[1])


class Scatter:
    def __init__(self, parts, where, tiled, deps=()):
        self.parts, self.where, self.tiled = parts, where, tiled
        self.got = scatter_send(parts, where, tiled, deps)

    def near(self):
        top, low = self.got
        self.got = [swap_x(top), swap_y(low)]

    def add_near(self):
        keep_t, send_t, keep_l, send_l = scatter_near(self.parts, self.got, self.where, self.tiled)
        self.keep, self.got = [keep_t, keep_l], [send_t, send_l]

    def far(self):
        self.got = [swap_y(self.got[0]), swap_x(self.got[1])]

    def add_far(self):
        self.got = list(scatter_far(self.keep, self.got, self.where, self.tiled))

    def along(self):
        self.got = [self.got[0]] + [shift_z(v, k) for k, v in enumerate(self.got) if k]

    def total(self):
        return sum(v.astype(f32) for v in self.got)


def gather_small(v):
    chips = 4 * lax.axis_size("z")
    return exchange(jnp.broadcast_to(v, (chips,) + v.shape), ("z", "y", "x"))


def project_kernel(source, scale, shift, weight, hidden_out, project_out):
    v = source[...].astype(f32)
    centre = v - jnp.mean(v, axis=1, keepdims=True)
    rate = lax.rsqrt(jnp.mean(centre * centre, axis=1, keepdims=True) + epsilon)
    hidden = (centre * rate * scale[...] + shift[...]).astype(b16)
    hidden_out[...] = hidden
    project_out[...] = jnp.dot(hidden, weight[...], preferred_element_type=f32)


def project_tokens(source, scale, shift, weight):
    tokens, width = source.shape
    cols = weight.shape[1]
    step = 256
    row = pl.BlockSpec((1, width), lambda i: (0, 0))
    return pl.pallas_call(
        project_kernel,
        grid=(tokens // step,),
        in_specs=[
            pl.BlockSpec((step, width), lambda i: (i, 0)),
            row,
            row,
            pl.BlockSpec((width, cols), lambda i: (0, 0)),
        ],
        out_specs=[
            pl.BlockSpec((step, width), lambda i: (i, 0)),
            pl.BlockSpec((step, cols), lambda i: (i, 0)),
        ],
        out_shape=[
            jax.ShapeDtypeStruct((tokens, width), b16),
            jax.ShapeDtypeStruct((tokens, cols), f32),
        ],
        compiler_params=pltpu.CompilerParams(vmem_limit_bytes=48 << 20),
        cost_estimate=little,
        name="project",
    )(source, scale, shift, weight)


def stats(v):
    mean = jnp.mean(v, axis=-1, keepdims=True)
    centre = v - mean
    rate = lax.rsqrt(jnp.mean(centre * centre, axis=-1, keepdims=True) + epsilon)
    return centre * rate, rate


def norm_back(g, n, rate):
    return (g - jnp.mean(g, -1, keepdims=True) - n * jnp.mean(g * n, -1, keepdims=True)) * rate


def dot(a, b, da, db):
    return lax.dot_general(a, b, (((da,), (db,)), ((), ())), preferred_element_type=f32)


LOG2E = 1.4426950408889634
CHUNK = 512


def nn(a, b):
    return lax.dot_general(a, b, (((1,), (0,)), ((), ())), preferred_element_type=f32)


def nt(a, b):
    return lax.dot_general(a, b, (((1,), (1,)), ((), ())), preferred_element_type=f32)


def lane_halves(v):
    lane = lax.broadcasted_iota(jnp.int32, v.shape, 1)
    zero = jnp.zeros_like(v)
    return jnp.where(lane < HD, v, zero), jnp.where(lane < HD, zero, v)


def turn(v, cosine, sine):
    width = v.shape[1]
    lane = lax.broadcasted_iota(jnp.int32, v.shape, 1)
    swapped = jnp.where(
        lane % HD < HD // 2,
        pltpu.roll(v, width - HD // 2, 1),
        pltpu.roll(v, HD // 2, 1),
    )
    return v * cosine + swapped * sine


def attend_kernel(project_in, cos_in, sin_in, *refs):
    turned_out, mix_out, log_out = refs[-3:]
    cosine = cos_in[...]
    sine = sin_in[...]
    tokens = cosine.shape[0]
    q = turn(project_in[:, :128], cosine, sine).astype(b16)
    k = turn(project_in[:, 128:256], cosine, sine).astype(b16)
    v = project_in[:, 256:].astype(b16)
    turned_out[:, :128] = q
    turned_out[:, 128:256] = k
    turned_out[:, 256:] = v
    keys = lane_halves(k)
    v_turned = v.astype(f32).T.astype(b16)
    for at in range(0, tokens, CHUNK):
        part = q[at : at + CHUNK]
        mixed = []
        for h in range(2):
            scores = nt(keys[h], part) * (0.125 * LOG2E)
            top = jnp.max(scores, axis=0, keepdims=True)
            weight = jnp.exp2(scores - top)
            total = jnp.sum(weight, axis=0, keepdims=True)
            log_out[0, h : h + 1, at : at + CHUNK] = top + jnp.log2(total)
            probs = (weight * (1.0 / total)).astype(b16)
            mixed.append(nn(v_turned[h * HD : (h + 1) * HD], probs))
        mix_out[at : at + CHUNK] = jnp.concatenate(mixed, axis=0).T.astype(b16)


def attend(project, cosine, sine, start, pairs, deps=()):
    tokens = project.shape[0]
    table = pl.BlockSpec((tokens, 128), lambda p: (0, 0))
    return pl.pallas_call(
        attend_kernel,
        grid=(pairs,),
        in_specs=[pl.BlockSpec((tokens, 384), lambda p: (0, start + p)), table, table]
        + unread(deps),
        out_specs=[
            pl.BlockSpec((tokens, 384), lambda p: (0, p)),
            pl.BlockSpec((tokens, 128), lambda p: (0, p)),
            pl.BlockSpec((1, 2, tokens), lambda p: (p, 0, 0)),
        ],
        out_shape=[
            jax.ShapeDtypeStruct((tokens, 384 * pairs), b16),
            jax.ShapeDtypeStruct((tokens, 128 * pairs), b16),
            jax.ShapeDtypeStruct((pairs, 2, tokens), f32),
        ],
        compiler_params=pltpu.CompilerParams(vmem_limit_bytes=48 << 20),
        cost_estimate=little,
        name="attend",
    )(project, cosine, sine, *deps)


def attend_back_kernel(
    turned_in, grad_in, log_in, cos_in, sin_in, *refs
):
    grad_out, dk_sum, dv_sum, dq_turned = refs[-4:]
    q = turned_in[:, :128]
    k = turned_in[:, 128:256]
    tokens = q.shape[0]
    keys = lane_halves(k)
    values = lane_halves(turned_in[:, 256:])
    k_turned = k.astype(f32).T.astype(b16)
    for at in range(0, tokens, CHUNK):
        q_part = q[at : at + CHUNK]
        g_part = grad_in[at : at + CHUNK]
        q_halves = lane_halves(q_part)
        g_halves = lane_halves(g_part)
        for h in range(2):
            scores = nt(keys[h], q_part) * (0.125 * LOG2E)
            full = jnp.exp2(scores - log_in[0, h : h + 1, at : at + CHUNK])
            prob_grad = nt(values[h], g_part)
            product = full * prob_grad
            total = jnp.sum(product, axis=0, keepdims=True)
            score_grad = (product - full * total).astype(b16)
            dv_h = nn(full.astype(b16), g_halves[h])
            dk_h = nn(score_grad, q_halves[h])
            dq_turned[h * HD : (h + 1) * HD, at : at + CHUNK] = nn(
                k_turned[h * HD : (h + 1) * HD], score_grad
            )
            dk = dk_h if h == 0 else dk + dk_h
            dv = dv_h if h == 0 else dv + dv_h
        if at == 0:
            dk_sum[...] = dk
            dv_sum[...] = dv
        else:
            dk_sum[...] += dk
            dv_sum[...] += dv
    cosine = cos_in[...]
    sine = -sin_in[...]
    grad_out[:, :128] = turn(dq_turned[...].T * 0.125, cosine, sine).astype(b16)
    grad_out[:, 128:256] = turn(dk_sum[...] * 0.125, cosine, sine).astype(b16)
    grad_out[:, 256:] = dv_sum[...].astype(b16)


def attend_back(turned, log_total, mixture_grad, cosine, sine, start, grad_start, pairs, deps=()):
    tokens = turned.shape[0]
    table = pl.BlockSpec((tokens, 128), lambda p: (0, 0))
    return pl.pallas_call(
        attend_back_kernel,
        grid=(pairs,),
        in_specs=[
            pl.BlockSpec((tokens, 384), lambda p: (0, start + p)),
            pl.BlockSpec((tokens, 128), lambda p: (0, grad_start + p)),
            pl.BlockSpec((1, 2, tokens), lambda p: (start + p, 0, 0)),
            table,
            table,
        ]
        + unread(deps),
        out_specs=pl.BlockSpec((tokens, 384), lambda p: (0, p)),
        out_shape=jax.ShapeDtypeStruct((tokens, 384 * pairs), b16),
        scratch_shapes=[
            pltpu.VMEM((tokens, 128), f32),
            pltpu.VMEM((tokens, 128), f32),
            pltpu.VMEM((128, tokens), f32),
        ],
        compiler_params=pltpu.CompilerParams(vmem_limit_bytes=48 << 20),
        cost_estimate=little,
        name="attend_back",
    )(turned, mixture_grad, log_total, cosine, sine, *deps)


def prepare_kernel(where, vector, qkv, up, out, time, own, other, out_low, time_low):
    c = where[1]
    rows, width = out.shape
    half = width // 2
    step = 128
    for there, made in ((c, own), (1 - c, other)):
        made[:, :128] = jnp.zeros((rows, 128), b16)
        made[:3, :128] = vector[...].astype(b16)
        for p in range(half // 128):
            for n in range(3):
                at = pl.multiple_of(n * width + there * half + p * 128, 128)
                to = 128 + (3 * p + n) * 128
                made[:, to : to + 128] = qkv[:, pl.ds(at, 128)].astype(b16)
        to = 128 + 3 * half
        for n in range(up.shape[1] // (2 * step)):
            at = pl.multiple_of((2 * n + there) * step, 128)
            made[:, to + n * step : to + (n + 1) * step] = up[:, pl.ds(at, step)].astype(b16)
    for n in range(2):
        out_low[n * rows : (n + 1) * rows] = out[:, n * half : (n + 1) * half].astype(b16)
    te_rows = time.shape[0]
    folds = 2 * rows // te_rows
    cols = time.shape[1] // folds
    for n in range(0, folds, 2):
        pair = [time[:, (n + i) * cols : (n + i + 1) * cols] for i in range(2)]
        time_low[n * te_rows : (n + 2) * te_rows] = jnp.concatenate(pair, axis=0).astype(b16)


def prepare(where, vector, qkv, up, out, time):
    rows, width = out.shape
    cols = 128 + 3 * width // 2 + up.shape[1] // 2
    near = pl.BlockSpec(memory_space=pltpu.VMEM)
    return pl.pallas_call(
        prepare_kernel,
        in_specs=[pl.BlockSpec(memory_space=pltpu.SMEM)] + [near] * 5,
        out_specs=[near] * 4,
        out_shape=[
            jax.ShapeDtypeStruct((rows, cols), b16),
            jax.ShapeDtypeStruct((rows, cols), b16),
            jax.ShapeDtypeStruct((2 * rows, width // 2), b16),
            jax.ShapeDtypeStruct((2 * rows, time.size // (2 * rows)), b16),
        ],
        cost_estimate=little,
        name="prepare",
    )(where, vector, qkv, up, out, time)


def body(
    inputs, teacher, valid_mask, time_steps, qkv_weight, out_weight, up_weight, down_weight,
    time_weight, time_bias, norm_gain, norm_bias, up_bias, down_bias,
):
    x, c, y, z, depth = place()
    chips = 4 * depth
    k_chip = 4 * z + 2 * y + x
    seqs, block, width = inputs.shape
    rows = qkv_weight.shape[0]
    ff_rows = down_weight.shape[0]
    half = width // 2
    tokens = 4 * block
    mine = 2 * block
    ff = up_weight.shape[1] // 2
    pairs = half // 128

    tiled = rows % 32 == 0 and ff_rows % 128 == 0
    where = jnp.stack([x, c, y, z])

    count = jnp.sum(valid_mask)
    step = pick(time_steps, x)
    whole_numbers = jnp.stack([count // 256, count % 256, step // 32, step % 32]).astype(f32)
    vector = jnp.concatenate([time_bias, norm_gain, norm_bias, up_bias, down_bias, whole_numbers])
    vector = jnp.pad(vector, (0, 384 - vector.shape[0])).reshape(3, 128)
    te_rows = time_weight.shape[0]
    te_folds = 2 * rows // te_rows
    cut = 128 + 3 * half
    if tiled:
        own, other, out_low, time_low = prepare(
            where, vector, qkv_weight, up_weight, out_weight, time_weight
        )
    else:

        def own_other(v):
            return [pick(v, i, 2).reshape(rows, -1).astype(b16) for i in (c, 1 - c)]

        def fold(v, n):
            return jnp.concatenate(jnp.split(v.astype(b16), n, axis=1), axis=0)

        vector = jnp.pad(vector.astype(b16), ((0, rows - 3), (0, 0)))
        qkv_cut = qkv_weight.reshape(rows, 3, 2, pairs, 128).transpose(0, 3, 2, 1, 4)
        qkv_own, qkv_other = own_other(qkv_cut.reshape(rows, pairs, 2, 3 * 128))
        up_own, up_other = own_other(up_weight.reshape(rows, -1, 2, ff_rows))
        own = jnp.concatenate([vector, qkv_own, up_own], axis=1)
        other = jnp.concatenate([vector, qkv_other, up_other], axis=1)
        out_low, time_low = fold(out_weight, 2), fold(time_weight, te_folds)
    other = swap_core(other)
    last = own.shape[1]
    if tiled:
        first_half, second_half = pl.ds(0, rows), pl.ds(rows, rows)

        def copies(x, c, y, z):
            made = []
            for source, at in ((0, c), (1, 1 - c)):
                made.append((source, (slice(None), pl.ds(0, cut)), 0, (at, slice(None), pl.ds(0, cut))))
                made.append((source, (slice(None), pl.ds(cut, ff)), 1, (at, slice(None), pl.ds(0, ff))))
            for at, half_rows in enumerate((first_half, second_half)):
                made.append((3, (half_rows,), 0, (at, slice(None), pl.ds(cut, time_low.shape[1]))))
                made.append((2, (half_rows,), 1, (at, slice(None), pl.ds(ff, half))))
            return made

        shapes = [
            jax.ShapeDtypeStruct((2, rows, cut + time_low.shape[1]), b16),
            jax.ShapeDtypeStruct((2, rows, ff + half), b16),
        ]
        piece_1, piece_2 = move(where, [own, other, out_low, time_low], shapes, copies)
        piece_1 = piece_1.reshape(2 * rows, -1)
        piece_2 = piece_2.reshape(2 * rows, -1)
    else:
        chip = jnp.concatenate(
            [jnp.where(c == 0, own, other), jnp.where(c == 0, other, own)], axis=0
        )
        piece_1 = jnp.concatenate([chip[:, :cut], time_low], axis=1)
        piece_2 = jnp.concatenate([chip[:, cut:], out_low], axis=1)
    down_full = lax.all_gather(down_weight.astype(b16), ("z", "y", "x"), axis=0, tiled=True)

    source_far = swap_x(pick(inputs, 1 - x))
    piece_1, source_far = tie(piece_1, source_far)
    marks = valid_mask.astype(b16)
    target_marks = jnp.concatenate(
        [teacher, jnp.broadcast_to(marks[:, :, None], (seqs, block, 128))], axis=2
    )
    target_far, source_far = tie(pick(target_marks, 1 - x), source_far)
    target_far = swap_x(target_far)
    pieces_1 = gather_z(piece_1, tiled)
    stack_1 = stack_z(pieces_1, tiled)
    target_far, stack_1[0] = tie(target_far, stack_1[0])
    piece_2, stack_1[1] = tie(piece_2, stack_1[1])
    pieces_2 = gather_z(piece_2, tiled)
    near_1 = list(gather_near(stack_1))
    near_1[2], near_1[3], pieces_2[1] = tie(near_1[2], near_1[3], pieces_2[1])
    source_far, near_1[0] = tie(source_far, near_1[0])
    source_low = jnp.concatenate([pick(inputs, x), source_far], axis=0)
    source_all = jnp.concatenate([source_low, swap_core(source_low)], axis=0)
    far_1 = list(gather_far(near_1))
    vectors, qkv_full, time_full = assemble(
        near_1, far_1, [0, 128, cut, piece_1.shape[1]], tiled
    )
    qkv_full = qkv_full.reshape(width, 3 * half)
    near_2 = list(gather_near(stack_z(pieces_2, tiled, tuple(far_1))))
    f = 2 * x + c
    blocks = jnp.stack([f, f ^ 2, f ^ 1, f ^ 3])
    positions = (blocks[:, None] * block + jnp.arange(block)[None, :]).reshape(tokens).astype(f32)
    pace = jnp.exp(jnp.arange(HD // 2, dtype=f32) * (-2.0 * math.log(10000.0) / HD))
    angles = positions[:, None] * pace[None, :]
    cosine = jnp.tile(jnp.cos(angles), (1, 4))
    sine = jnp.sin(angles)
    sine = jnp.tile(jnp.concatenate([-sine, sine], axis=1), (1, 2))

    vectors = vectors.reshape(chips, 2, rows, 128)[:, :, :3].reshape(chips, 2, 384)
    vectors = vectors.astype(f32)
    at = 0

    def take(n):
        nonlocal at
        at += n
        return vectors[:, :, at - n : at]

    bias_time = take(time_bias.shape[0]).reshape(2 * width)
    gain = take(rows).reshape(width)
    shift = take(rows).reshape(width)
    bias_up = pick(take(ff_rows), c, 1).reshape(ff)
    bias_down = take(rows).reshape(width)
    numbers = take(4)
    valid_total = jnp.sum(numbers[:, :, 0]) * 256.0 + jnp.sum(numbers[:, :, 1])
    steps = numbers[:, 0, 2] * 32.0 + numbers[:, 0, 3]
    token_total = 2 * depth * seqs * tokens
    factor = (token_total * width / 2) / (valid_total * width)

    spread = jnp.exp(jnp.arange(TE // 2, dtype=f32) * (-math.log(10000.0) / (TE // 2)))
    angle = steps[:, None] * spread[None]
    features = jnp.concatenate([jnp.sin(angle), jnp.cos(angle)], axis=1).astype(b16)
    feature_core = pick(pick(features, k_chip).reshape(chips, 2, te_rows), c, 1)
    time_parts = time_full.reshape(chips, te_folds, te_rows, -1).astype(f32)
    part = jnp.sum(feature_core.astype(f32)[:, None, :, None] * time_parts, axis=(0, 2))
    part = part.reshape(-1, 128)
    condition = (part + swap_core(part)).reshape(2, width) + bias_time.reshape(2, width)
    scale = 1.0 + condition[:1]
    hidden, project = project_tokens(source_all, scale, condition[1:], qkv_full)
    near_2[2], near_2[3], project = tie(near_2[2], near_2[3], project)
    far_2 = list(gather_far(near_2))
    ahead = pairs // 2
    turned_a, mixed_a, log_a = attend(project, cosine, sine, 0, ahead)
    turned_b, mixed_b, log_b = attend(project, cosine, sine, ahead, pairs - ahead, (mixed_a,))
    far_2[0], mixed_a, mixed_b = tie(far_2[0], mixed_a, mixed_b)
    up_full, out_half = assemble(near_2, far_2, [0, ff, ff + half], tiled)
    up_full = up_full.reshape(width, ff)
    out_far = swap_core(out_half)
    if tiled:

        def copies(x, c, y, z):
            every = slice(None)
            return [
                (n, (every, pl.ds(h * rows, rows)), 0, (every, at, every, pl.ds(h * half, half)))
                for n, at in ((0, c), (1, 1 - c))
                for h in range(2)
            ]

        shape = jax.ShapeDtypeStruct((chips, 2, rows, width), b16)
        out_full = move(where, [out_half, out_far], [shape], copies)[0]
    else:
        out_both = jnp.stack(
            [jnp.where(c == 0, out_half, out_far), jnp.where(c == 0, out_far, out_half)], axis=1
        ).reshape(chips, 2, 2, rows, half)
        out_full = jnp.concatenate([out_both[:, :, 0], out_both[:, :, 1]], axis=-1)
    out_full = out_full.reshape(width, width)
    mixed = jnp.concatenate([mixed_a, mixed_b], axis=1)
    mixed_far = swap_core(mixed[mine:])
    mixture = jnp.where(
        c == 0,
        jnp.concatenate([mixed[:mine], mixed_far], axis=1),
        jnp.concatenate([mixed_far, mixed[:mine]], axis=1),
    )
    middle = source_low.astype(f32) + dot(mixture, out_full, 1, 0)
    n2, rate2 = stats(middle)
    second = (n2 * gain + shift).astype(b16)
    second_all = jnp.concatenate([second, swap_core(second)], axis=0)
    inner = dot(second_all, up_full, 1, 0) + bias_up
    flat = 0.5 * (1.0 + lax.erf(inner * (2.0**-0.5)))
    active = (inner * flat).astype(b16)
    slope = flat + inner * jnp.exp(-0.5 * inner * inner) * ((2.0 * math.pi) ** -0.5)
    down = dot(active, down_full, 1, 0)
    result = middle + (down[:mine] + swap_core(down[mine:].astype(b16)).astype(f32) + bias_down)

    target_marks = jnp.concatenate([pick(target_marks, x), target_far], axis=0)
    target = target_marks[:, :width].astype(f32)
    mark = target_marks[:, width : width + 1].astype(f32)
    differ = result - target
    loss_part = jnp.sum(mark * differ * differ)
    result_grad = 2.0 * mark * differ * factor

    def spread_out(v):
        far = swap_x(v[block:].astype(b16)).astype(v.dtype)
        near = v[:block]
        return jnp.stack([jnp.where(x == 0, near, far), jnp.where(x == 0, far, near)])

    down_in = result_grad.astype(b16)
    down_in_all = jnp.concatenate([down_in, swap_core(down_in)], axis=0)
    near_axes = ("y", "x")
    result_low = result.astype(b16)
    result_far = swap_x(result_low[block:])
    down_term = dot(active, down_in_all, 0, 0).astype(b16)
    down_in_all, down_term = tie(down_in_all, down_term)
    down_sum = lax.psum_scatter(down_term, ("z", "y", "x"), scatter_dimension=0, tiled=True)
    inner_grad = (dot(down_in_all, down_full, 1, 1) * slope).astype(b16)
    second_part = dot(inner_grad, up_full, 1, 1)
    second_send, second_all = tie(second_part[mine:].astype(b16), second_all)
    second_got = swap_core(second_send)
    up_term = dot(second_all, inner_grad, 0, 0).astype(b16)
    up_sum = Scatter(up_term.reshape(chips, -1, ff), where, tiled)
    second_got, up_sum.got[0] = tie(second_got, up_sum.got[0])
    up_sum.near()
    second_grad = second_part[:mine] + second_got.astype(f32)
    middle_grad = result_grad + norm_back(second_grad * gain, n2, rate2)
    branch = middle_grad.astype(b16)
    mixture_grad = dot(branch, out_full, 1, 1).astype(b16)
    mixture_far, branch = tie(
        lax.dynamic_slice_in_dim(mixture_grad, (1 - c) * half, half, 1), branch
    )
    mixture_far = swap_core(mixture_far)
    out_term = dot(mixture, branch, 0, 0).astype(b16).reshape(chips, 2, rows, width)
    mixture_far, out_send, out_keep = tie(
        mixture_far, pick(out_term, 1 - c, 1), pick(out_term, c, 1)
    )
    out_got = swap_core(out_send)
    mixture_grad = jnp.concatenate(
        [lax.dynamic_slice_in_dim(mixture_grad, c * half, half, 1), mixture_far], axis=0
    )

    def pair_back(p, deps):
        turned, log = (turned_a, log_a) if p < ahead else (turned_b, log_b)
        at = p if p < ahead else p - ahead
        return attend_back(turned, log, mixture_grad, cosine, sine, at, p, 1, deps)

    grads = [pair_back(0, ())]
    for p in range(1, pairs - 1):
        grads.append(pair_back(p, (grads[-1],)))
    up_sum.got[0], up_sum.got[1], grads[-1] = tie(up_sum.got[0], up_sum.got[1], grads[-1])
    up_sum.add_near()
    grads.append(pair_back(pairs - 1, (grads[-1], up_sum.keep[0])))
    up_sum.far()
    project_grad = jnp.concatenate(grads, axis=1)
    qkv_term = dot(hidden, project_grad, 0, 0).astype(b16).reshape(chips, 2 * rows, -1)
    qkv_cols = qkv_term.shape[2]
    out_term = add_low(out_keep, out_got)
    out_term = jnp.concatenate([out_term[:, :, :half], out_term[:, :, half:]], axis=1)
    last_sum = Scatter(jnp.concatenate([qkv_term, out_term], axis=2), where, tiled)
    project_grad, last_sum.got[0] = tie(project_grad, last_sum.got[0])
    last_sum.near()
    hidden_part = dot(project_grad, qkv_full, 1, 1)
    hidden_got, hidden_keep, *up_sum.got = tie(
        hidden_part[mine:].astype(b16), hidden_part[:mine], *up_sum.got
    )
    hidden_got = swap_core(hidden_got)
    up_sum.add_far()
    up_sum.got[0], hidden_got = tie(up_sum.got[0], hidden_got)
    up_sum.along()
    hidden_grad = hidden_keep + hidden_got.astype(f32)
    n1, rate1 = stats(source_low.astype(f32))
    activations = jnp.stack(
        [
            jnp.where(x == 0, result_low[:block], result_far),
            jnp.where(x == 0, result_far, result_low[:block]),
        ]
    )
    input_grad = middle_grad + norm_back(hidden_grad * scale, n1, rate1)

    small = jnp.concatenate(
        [
            jnp.sum(hidden_grad * n1, 0),
            jnp.sum(hidden_grad, 0),
            jnp.sum(second_grad * n2, 0),
            jnp.sum(second_grad, 0),
            jnp.sum(down_in.astype(f32), 0),
            jnp.full((128,), loss_part),
        ]
    )
    small = small.reshape(-1, 128)
    small_got = swap_core(small)
    last_sum.got[0], input_grad = tie(last_sum.got[0], input_grad)
    last_sum.add_near()
    small_got, input_grad, last_sum.got[0] = tie(small_got, input_grad, last_sum.got[0])
    last_sum.far()
    small = small + small_got
    up_bias_part = jnp.sum(inner_grad.astype(f32), 0).reshape(-1, 128)
    fill = jnp.zeros((-(small.shape[0] + up_bias_part.shape[0]) % 8, 128), f32)
    small = jnp.concatenate([small, up_bias_part, fill], axis=0)
    small = gather_small(small)
    input_grad = spread_out(input_grad)
    up_sum = up_sum.total()
    last_sum.add_far()
    last_sum.along()
    last_sum = last_sum.total()
    down_sum = down_sum.astype(f32)
    index = 2 * k_chip + c
    feature_rows = lax.dynamic_slice_in_dim(features, index * te_rows, te_rows, 1).astype(f32)
    time_sum = lax.dot_general(
        feature_rows,
        small[:, : 2 * width // 128].reshape(chips, -1),
        (((0,), (0,)), ((), ())),
        precision=highest,
    )
    sums = jnp.sum(small, axis=0).reshape(-1)

    def share(start, size, index):
        return lax.dynamic_slice_in_dim(sums[start:], index * size, size, 0)

    time_bias_sum = share(0, 2 * rows, index)
    gain_sum = share(2 * width, rows, index)
    shift_sum = share(3 * width, rows, index)
    down_bias_sum = share(4 * width, rows, index)
    up_bias_sum = share(5 * width + 128, ff_rows, k_chip)
    loss = (sums[5 * width] / (valid_total * width)).reshape(1)

    def columns(total, inner_size):
        total = total.reshape(2, rows, -1, inner_size)
        near = pick(total, c)
        far = swap_core(pick(total, 1 - c))
        return jnp.stack(
            [jnp.where(c == 0, near, far), jnp.where(c == 0, far, near)], axis=2
        ).reshape(rows, -1)

    out_sum = last_sum[:, qkv_cols:]
    out_sum = jnp.concatenate([out_sum[:rows], out_sum[rows:]], axis=1)
    qkv_sum = last_sum[:, :qkv_cols].reshape(2 * rows, pairs, 3, 128)
    qkv_sum = qkv_sum.transpose(0, 2, 1, 3).reshape(2 * rows, -1)
    return (
        activations,
        loss,
        input_grad,
        columns(qkv_sum, half),
        out_sum,
        columns(up_sum, ff_rows),
        down_sum,
        time_sum,
        time_bias_sum,
        gain_sum,
        shift_sum,
        up_bias_sum,
        down_bias_sum,
    )


def solution(mesh):
    split = mesh.devices.reshape(-1, 2, 2, 2)
    finer = jax.sharding.Mesh(split, ("z", "y", "x", "core"))
    both = ("z", "y", "x", "core")
    tokens = P(("z", "y"), ("x", "core"), None)
    weight = P(both, None)
    vector = P(both)
    return jax.shard_map(
        body,
        mesh=finer,
        in_specs=(tokens, tokens, P(("z", "y"), ("x", "core")), P(("z", "y"))) + (weight,) * 5 + (vector,) * 5,
        out_specs=(tokens, P(), tokens) + (weight,) * 5 + (vector,) * 5,
        check_vma=False,
    )
```

time: 670 us -> 480 us (0.72)
  matrix products: 147 us -> 59.6 us
  other arithmetic: 118 us -> 45.7 us
  Pallas kernels: 0 us -> 71.5 us
  local copies, waits for them, and re-layouts: 103 us -> 39 us
  waiting for transfers between devices: 214 us -> 167 us
  between operations: 10.1 us -> 23.9 us
    dot_general x6 -> x1, matrix products: 84.6 us -> 0.94 us  [body(): lax.dot_general(feature_rows, small[:, :2 * width // 128].reshape(chips,...]
    pallas_call x0 -> x20, Pallas kernels: none -> 71.5 us  [the longest x4 27.1 us: attend_back(): pl.pallas_call(attend_back_kernel, grid=(pairs,), in_specs=[pl.BlockSpec(...]
    ppermute x67 -> x47, waiting for transfers between devices: 214 us -> 167 us  [the longest x12 71.6 us: shift_z(): return lax.ppermute(v, 'z', [(i, (i + k) % depth) for i in range(depth)])]
    convert_element_type x12 -> x5, other arithmetic: 34.2 us -> 4.89 us  [the longest x1 2.28 us: body(): branch = middle_grad.astype(b16)]
    slice x31 -> x13, local copies, waits for them, and re-layouts: 23.6 us -> 3.58 us  [the longest x1 0.91 us: body(): small[:, :2 * width // 128].reshape(chips, -1)]
    convert_element_type x13 -> x1, other arithmetic: 17 us -> 1.64 us  [add_low(): return (a.astype(f32) + b.astype(f32)).astype(a.dtype)]
    dynamic_slice x12 -> x2, local copies, waits for them, and re-layouts: 14.3 us -> 0.61 us  [pick(): return lax.dynamic_index_in_dim(v, index, axis, False)]
    reduce_sum x3 -> x6, other arithmetic: 15.5 us -> 4.39 us  [the longest x2 1.27 us: body(): jnp.sum(feature_core.astype(f32)[:, None, :, None] * time_parts, axis=(0,...]
  transfers between devices with their start and end apart: 67 -> 50, of which waited for: 21 -> 24; matrix products, arithmetic and copies ran while one was open for 46% -> 18% of each run, Pallas kernels for 0% -> 15%
where the time goes in v2:
time: 480 us; the launch traced here: 475 us
  waiting for transfers between devices  167 us (35%)
  Pallas kernels  71.5 us (15%)
  starting transfers between devices  67.9 us (14%)
  matrix products  59.6 us (12%)
  other arithmetic  45.7 us (10%)
  local copies, waits for them, and re-layouts  39 us (8%)
  between operations  23.9 us (5%)
    ppermute x12, waiting for transfers between devices, shift_z(): return lax.ppermute(v, 'z', [(i, (i + k) % depth) for i in range(depth)])  71.6 us
    ppermute x12, waiting for transfers between devices, swap_x(): return lax.ppermute(v, 'x', [(0, 1), (1, 0)])  66.1 us
    dot_general x11, matrix products, dot(): lax.dot_general(a, b, (((da,), (db,)), ((), ())), preferred_element_type=...  58.6 us
    pallas_call x4, Pallas kernels, attend_back(): pl.pallas_call(attend_back_kernel, grid=(pairs,), in_specs=[pl.BlockSpec(...  27.1 us
    ppermute x8, waiting for transfers between devices, swap_y(): return lax.ppermute(v, 'y', [(0, 1), (1, 0)])  25.9 us
    ppermute x12, starting transfers between devices, shift_z(): return lax.ppermute(v, 'z', [(i, (i + k) % depth) for i in range(depth)])  22.6 us
    pallas_call x2, Pallas kernels, attend(): pl.pallas_call(attend_kernel, grid=(pairs,), in_specs=[pl.BlockSpec((toke...  20.9 us
    unnamed x145, local copies, waits for them, and re-layouts  17.9 us
  transfers between devices with their start and end apart: 50, of which 24 were waited for; matrix products, arithmetic and copies ran while one was open for 18% of the time, Pallas kernels for 15%

profile of v2, /device:TPU:9, one launch (start us, length us, event | category | flops | bytes accessed | tf_op | source)
XLA Modules:
  0.0 474.7 jit_solution(3887854580278675054)
XLA Ops:
  24.0 2.5 collective-permute-start.4
  30.1 11.8 %collective-permute-done.4.refs_2_ = bf16[64,1920]{1,0:T(8,128)(2,1)S(1)} collective-permute-done((bf16[64,1920]{1,0:T(8,128)(2,1)S(1)}, bf16[64,1920]{1,0:T(8,128)(2,1)S(1)}, u32[]{:S(2)}, u32[]{:S(2)}) %collective-permute-start.4) | collective-permute-done | bytes 245792 | tf_op jit(solution)/shard_map/ppermute | solution.py:34
  41.9 5.3 %collective-permute-done.3.refs_1_ = bf16[64,1920]{1,0:T(8,128)(2,1)S(1)} collective-permute-done((bf16[64,1920]{1,0:T(8,128)(2,1)S(1)}, bf16[64,1920]{1,0:T(8,128)(2,1)S(1)}, u32[]{:S(2)}, u32[]{:S(2)}) %collective-permute-start.3) | collective-permute-done | bytes 245792 | tf_op jit(solution)/shard_map/ppermute | solution.py:34
  52.6 5.2 %collective-permute-done.8.refs_1_ = bf16[64,2560]{1,0:T(8,128)(2,1)S(1)} collective-permute-done((bf16[64,2560]{1,0:T(8,128)(2,1)S(1)}, bf16[64,2560]{1,0:T(8,128)(2,1)S(1)}, u32[]{:S(2)}, u32[]{:S(2)}) %collective-permute-start.8) | collective-permute-done | bytes 327712 | tf_op jit(solution)/shard_map/ppermute | solution.py:34
  65.2 3.0 collective-permute-start.9
  70.5 3.5 collective-permute-start.15
  74.0 10.3 %collective-permute-done.11.refs_4_ = bf16[2,4,32,1920]{3,2,1,0:T(8,128)(2,1)S(1)} collective-permute-done((bf16[2,4,32,1920]{3,2,1,0:T(8,128)(2,1)}, bf16[2,4,32,1920]{3,2,1,0:T(8,128)(2,1)S(1)}, u32[]{:S(2)}, u32[]{:S(2)}) %collective-permute-start.11) | collective-permute-done | bytes 983072 | tf_op jit(solution)/shard_map/ppermute | solution.py:29
  88.8 3.7 collective-permute-done.9.refs_2_
  100.7 8.3 %project.1 = (bf16[1024,1024]{1,0:T(8,128)(2,1)S(1)}, f32[1024,1536]{1,0:T(8,128)}) custom-call(bf16[1024,1024]{1,0:T(8,128)(2,1)S(1)} %pad_maximum_fusion.2.source, f32[1,1024]{1,0:T(1,128)S(1)} %get-tuple-element.236.scale, f32[1,1024]{1,0:T(1,128)S(1)} %get-tuple-element.235.shift, bf16[1024,1536]{1,0:T(8,128)(2,1)} %bitcast.135), custom_call_target="tpu_custom_call" | custom-call | flops 1 | bytes 1 | tf_op jit(solution)/shard_map/project/pallas_call | solution.py:382
  109.0 7.5 %collective-permute-done.13.refs_2_ = bf16[4,32,2560]{2,1,0:T(8,128)(2,1)} collective-permute-done((bf16[4,32,2560]{2,1,0:T(8,128)(2,1)S(1)}, bf16[4,32,2560]{2,1,0:T(8,128)(2,1)}, u32[]{:S(2)}, u32[]{:S(2)}) %collective-permute-start.13) | collective-permute-done | bytes 655392 | tf_op jit(solution)/shard_map/ppermute | solution.py:25
  116.4 2.3 pad_maximum_fusion.6
  120.0 2.3 pad_maximum_fusion.7
  125.3 10.4 %attend.2 = (bf16[1024,768]{1,0:T(8,128)(2,1)S(1)}, bf16[1024,256]{1,0:T(8,128)(2,1)S(1)}, f32[2,2,1024]{2,1,0:T(2,128)S(1)}) custom-call(f32[1024,1536]{1,0:T(8,128)} %get-tuple-element.129.project_in, f32[1024,128]{1,0:T(8,128)S(1)} %copy.100.cos_in, f32[1024,128]{1,0:T(8,128)S(1)} %copy.101.sin_in), custom_call_target="tpu_custom_call" | custom-call | flops 1 | bytes 1 | tf_op jit(solution)/shard_map/attend/pallas_call | solution.py:479
  136.8 10.6 %attend.3 = (bf16[1024,768]{1,0:T(8,128)(2,1)S(1)}, bf16[1024,256]{1,0:T(8,128)(2,1)S(1)}, f32[2,2,1024]{2,1,0:T(2,128)S(1)}) custom-call(f32[1024,1536]{1,0:T(8,128)} %get-tuple-element.129.project_in, f32[1024,128]{1,0:T(8,128)S(1)} %copy.100.cos_in, f32[1024,128]{1,0:T(8,128)S(1)} %copy.101.sin_in, bf16[1024,256]{1,0:T(8,128)(2,1)S(1)} %get-tuple-element.132.refs_0_), custom_call_target="tpu_custom_call" | custom-call | flops 1 | bytes 1 | tf_op jit(solution)/shard_map/attend/pallas_call | solution.py:479
  147.4 14.8 %collective-permute-done.17.refs_4_ = bf16[2,4,32,2560]{3,2,1,0:T(8,128)(2,1)} collective-permute-done((bf16[2,4,32,2560]{3,2,1,0:T(8,128)(2,1)}, bf16[2,4,32,2560]{3,2,1,0:T(8,128)(2,1)}, u32[]{:S(2)}, u32[]{:S(2)}) %collective-permute-start.17) | collective-permute-done | bytes 1310752 | tf_op jit(solution)/shard_map/ppermute | solution.py:29
  162.2 4.2 collective-permute-done.19.refs_5_
  166.3 2.5 move.12
  168.8 2.8 collective-permute-start.20
  175.8 2.6 fusion.56
  180.6 2.3 collective-permute-done.21
  183.9 8.6 %multiply_convert_fusion = (bf16[1024,2048]{1,0:T(8,128)(2,1)}, f32[1024,2048]{1,0:T(8,128)}) fusion(f32[2048]{0:T(1024)S(1)} %dynamic-slice_bitcast_fusion.6, bf16[1024,2048]{1,0:T(8,128)(2,1)S(1)} %bitcast.158, bf16[512,1024]{1,0:T(8,128)(2,1)S(1)} %collective-permute-done.21, bf16[512,1024]{1,0:T(8,128)(2,1)S(1)} %add_convert_fusion.1), kind=kOutput, calls=%fused_computation.8 | convolution fusion | flops 4311744512 | bytes 18882560 | tf_op jit(solution)/shard_map/dot_general | solution.py:417
  192.5 7.5 %fusion.57 = f32[1024,1024]{1,0:T(8,128)S(1)} fusion(bf16[1024,2048]{1,0:T(8,128)(2,1)} %get-tuple-element.246, bf16[2048,1024]{1,0:T(8,128)(2,1)} %all-gather.2.cloned.1.call-done), kind=kOutput, calls=%fused_computation.180 | convolution fusion | flops 4294967296 | bytes 12582912 | tf_op jit(solution)/shard_map/dot_general | solution.py:417
  204.4 4.9 %fusion.17 = (f32[]{:T(128)}, f32[512,1024]{1,0:T(8,128)S(1)}, bf16[512,1024]{1,0:T(8,128)(2,1)}) fusion(f32[512]{0:T(512)S(1)} %get-tuple-element.199, bf16[256,1152]{1,0:T(8,128)(2,1)} %copy-done.47, bf16[256,1152]{1,0:T(8,128)(2,1)S(1)} %copy-done.43, f32[512,1024]{1,0:T(8,128)} %copy-done.27, f32[1024]{0:T(1024)S(1)} %add.257, ...), kind=kLoop, calls=%fused_computation.30 | loop fusion | flops 6815743 | bytes 9574404 | tf_op jit(solution)/shard_map/reduce_sum | solution.py:803
  214.0 6.3 %convolution_convert_fusion.2 = bf16[2048,1024]{1,0:T(8,128)(2,1)} fusion(bf16[1024,2048]{1,0:T(8,128)(2,1)S(1)} %copy-done.67, bf16[512,1024]{1,0:T(8,128)(2,1)S(1)} %collective-permute-done.24, bf16[512,1024]{1,0:T(8,128)(2,1)S(1)} %get-tuple-element.206), kind=kOutput, calls=%fused_computation.13 | convolution fusion | flops 4301258752 | bytes 10485760 | tf_op jit(solution)/shard_map/dot_general | solution.py:417
  222.8 10.1 %convert_reduce_fusion = (f32[2048]{0:T(1024)S(1)}, bf16[1024,2048]{1,0:T(8,128)(2,1)S(1)}) fusion(f32[1024,2048]{1,0:T(8,128)} %get-tuple-element.247, f32[2048]{0:T(1024)S(1)} %dynamic-slice_bitcast_fusion.6, bf16[1024,1024]{1,0:T(8,128)(2,1)S(1)} %pad_maximum_fusion.4, bf16[2048,1024]{1,0:T(8,128)(2,1)S(1)} %copy-done.64), kind=kOutput, calls=%fused_computation.7 | convolution fusion | flops 4322228224 | bytes 18890752 | tf_op jit(solution)/shard_map/dot_general | solution.py:417
  232.9 4.5 fusion.58
  240.1 7.5 %convolution_convert_fusion.1 = bf16[1024,2048]{1,0:T(8,128)(2,1)S(1)} fusion(bf16[1024,1024]{1,0:T(8,128)(2,1)} %pad_maximum_fusion.3, bf16[1024,2048]{1,0:T(8,128)(2,1)} %copy-done.66), kind=kOutput, calls=%fused_computation.12 | convolution fusion | flops 4297064448 | bytes 10485760 | tf_op jit(solution)/shard_map/dot_general | solution.py:417
  253.4 2.3 fusion.49
  259.8 2.5 convolution_convert_fusion.3
  265.2 6.6 %attend_back.4.refs_0_ = bf16[1024,384]{1,0:T(8,128)(2,1)S(1)} custom-call(bf16[1024,768]{1,0:T(8,128)(2,1)S(1)} %copy-done.3, bf16[1024,512]{1,0:T(8,128)(2,1)S(1)} %pad_maximum_fusion.11.grad_in, f32[2,2,1024]{2,1,0:T(2,128)S(1)} %get-tuple-element.148.log_in, f32[1024,128]{1,0:T(8,128)S(1)} %copy.100.cos_in, f32[1024,128]{1,0:T(8,128)S(1)} %copy.101.sin_in), custom_call_target="tpu_custom_call" | custom-call | flops 1 | bytes 1 | tf_op jit(solution)/shard_map/attend_back/pallas_call | solution.py:545
  273.3 6.8 %attend_back.5.refs_0_ = bf16[1024,384]{1,0:T(8,128)(2,1)S(1)} custom-call(bf16[1024,768]{1,0:T(8,128)(2,1)S(1)} %copy-done.4, bf16[1024,512]{1,0:T(8,128)(2,1)S(1)} %pad_maximum_fusion.11.grad_in, f32[2,2,1024]{2,1,0:T(2,128)S(1)} %get-tuple-element.148.log_in, f32[1024,128]{1,0:T(8,128)S(1)} %copy.100.cos_in, f32[1024,128]{1,0:T(8,128)S(1)} %copy.101.sin_in, ...), custom_call_target="tpu_custom_call" | custom-call | flops 1 | bytes 1 | tf_op jit(solution)/shard_map/attend_back/pallas_call | solution.py:545
  280.8 6.6 %attend_back.6.refs_0_ = bf16[1024,384]{1,0:T(8,128)(2,1)S(1)} custom-call(bf16[1024,768]{1,0:T(8,128)(2,1)S(1)} %copy-done.6, bf16[1024,512]{1,0:T(8,128)(2,1)S(1)} %pad_maximum_fusion.11.grad_in, f32[2,2,1024]{2,1,0:T(2,128)S(1)} %get-tuple-element.152.log_in, f32[1024,128]{1,0:T(8,128)S(1)} %copy.100.cos_in, f32[1024,128]{1,0:T(8,128)S(1)} %copy.101.sin_in, ...), custom_call_target="tpu_custom_call" | custom-call | flops 1 | bytes 1 | tf_op jit(solution)/shard_map/attend_back/pallas_call | solution.py:545
  290.8 7.0 %attend_back.7 = bf16[1024,384]{1,0:T(8,128)(2,1)S(1)} custom-call(bf16[1024,768]{1,0:T(8,128)(2,1)S(1)} %copy-done.6, bf16[1024,512]{1,0:T(8,128)(2,1)S(1)} %pad_maximum_fusion.11.grad_in, f32[2,2,1024]{2,1,0:T(2,128)S(1)} %get-tuple-element.152.log_in, f32[1024,128]{1,0:T(8,128)S(1)} %copy.100.cos_in, f32[1024,128]{1,0:T(8,128)S(1)} %copy.101.sin_in, ...), custom_call_target="tpu_custom_call" | custom-call | flops 1 | bytes 1 | tf_op jit(solution)/shard_map/attend_back/pallas_call | solution.py:545
  299.4 4.3 convolution_convert_fusion
  308.3 3.4 fusion.59
  312.1 29.0 %collective-permute-done.31.low_got = bf16[4,32,2048]{2,1,0:T(8,128)(2,1)S(1)} collective-permute-done((bf16[4,32,2048]{2,1,0:T(8,128)(2,1)S(1)}, bf16[4,32,2048]{2,1,0:T(8,128)(2,1)S(1)}, u32[]{:S(2)}, u32[]{:S(2)}) %collective-permute-start.31) | collective-permute-done | bytes 524320 | tf_op jit(solution)/shard_map/ppermute | solution.py:25
  343.6 3.2 collective-permute-start.44
  350.6 2.5 collective-permute-start.34
  354.0 23.4 %collective-permute-done.44 = bf16[64,2048]{1,0:T(8,128)(2,1)S(1)} collective-permute-done((bf16[64,2048]{1,0:T(8,128)(2,1)S(1)}, bf16[64,2048]{1,0:T(8,128)(2,1)S(1)}, u32[]{:S(2)}, u32[]{:S(2)}) %collective-permute-start.44) | collective-permute-done | bytes 262176 | tf_op jit(solution)/shard_map/ppermute | solution.py:34
  377.4 2.5 collective-permute-done.45
  383.9 20.6 %collective-permute-done.34.top = bf16[4,2,32,2048]{3,2,1,0:T(8,128)(2,1)S(1)} collective-permute-done((bf16[4,2,32,2048]{3,2,1,0:T(8,128)(2,1)S(1)}, bf16[4,2,32,2048]{3,2,1,0:T(8,128)(2,1)S(1)}, u32[]{:S(2)}, u32[]{:S(2)}) %collective-permute-start.34) | collective-permute-done | bytes 1048608 | tf_op jit(solution)/shard_map/ppermute | solution.py:25
  405.5 2.3 collective-permute-start.38
  411.5 6.4 %all-to-all-start = ((f32[16,64,128]{2,1,0:T(8,128)}), f32[16,64,128]{2,1,0:T(8,128)}, u32[]{:S(2)}, u32[]{:S(2)}) async-start(f32[16,64,128]{2,1,0:T(8,128)} %broadcast_in_dim.11), calls=%async_computation | async-start | bytes 1048576 | tf_op jit(solution)/shard_map/all_to_all | solution.py:165
  420.2 2.3 reshape.271
  424.6 6.2 %collective-permute-start.40 = (bf16[64,2048]{1,0:T(8,128)(2,1)S(1)}, bf16[64,2048]{1,0:T(8,128)(2,1)S(1)}, u32[]{:S(2)}, u32[]{:S(2)}) collective-permute-start(bf16[64,2048]{1,0:T(8,128)(2,1)S(1)} %get-tuple-element.184), channel_id=1, source_target_pairs={{0,16},{8,24},{16,0},{24,8},{1,17},{9,25},{17,1},{25,9},{2,18},{10... | collective-permute-start | bytes 786440 | tf_op jit(solution)/shard_map/ppermute | solution.py:34
  430.7 2.8 collective-permute-done.36
  437.1 14.2 %collective-permute-done.40 = bf16[64,2048]{1,0:T(8,128)(2,1)S(1)} collective-permute-done((bf16[64,2048]{1,0:T(8,128)(2,1)S(1)}, bf16[64,2048]{1,0:T(8,128)(2,1)S(1)}, u32[]{:S(2)}, u32[]{:S(2)}) %collective-permute-start.40) | collective-permute-done | bytes 262176 | tf_op jit(solution)/shard_map/ppermute | solution.py:34
  451.2 2.5 collective-permute-done.41
  (364 shorter events, 128.4 us)
Async XLA Ops:
  7.3 185.2 %all-gather.2.cloned.1.call-start = ((), (), s32[]{:S(2)}) async-start(), calls=%async_computation.2 | async-start | bytes 4456448 | tf_op jit(solution)/shard_map/all_gather | solution.py:689
  9.5 14.2 %collective-permute-start.1 = (bf16[256,1024]{1,0:T(8,128)(2,1)S(1)}, bf16[256,1024]{1,0:T(8,128)(2,1)S(1)}, u32[]{:S(2)}, u32[]{:S(2)}) collective-permute-start(bf16[256,1024]{1,0:T(8,128)(2,1)S(1)} %get-tuple-element.225), channel_id=1, source_target_pairs={{0,2},{2,0},{1,3},{3,1},{4,6},{6,4},{5,7},{7,5},{8,10},{10,8},{9,1... | collective-permute-start | bytes 1572872 | tf_op jit(solution)/shard_map/ppermute | solution.py:25
  23.7 25.5 %collective-permute-start.2 = (bf16[256,1152]{1,0:T(8,128)(2,1)S(1)}, bf16[256,1152]{1,0:T(8,128)(2,1)S(1)}, u32[]{:S(2)}, u32[]{:S(2)}) collective-permute-start(bf16[256,1152]{1,0:T(8,128)(2,1)S(1)} %get-tuple-element.109), channel_id=1, source_target_pairs={{0,2},{2,0},{1,3},{3,1},{4,6},{6,4},{5,7},{7,5},{8,10},{10,8},{9,1... | collective-permute-start | bytes 1769480 | tf_op jit(solution)/shard_map/ppermute | solution.py:25
  24.0 6.1 %collective-permute-start.5 = (bf16[64,1920]{1,0:T(8,128)(2,1)S(1)}, bf16[64,1920]{1,0:T(8,128)(2,1)S(1)}, u32[]{:S(2)}, u32[]{:S(2)}) collective-permute-start(bf16[64,1920]{1,0:T(8,128)(2,1)S(1)} %bitcast.151), channel_id=1, source_target_pairs={{0,24},{8,0},{16,8},{24,16},{1,25},{9,1},{17,9},{25,17},{2,26},{10... | collective-permute-start | bytes 737288 | tf_op jit(solution)/shard_map/ppermute | solution.py:34
  24.0 17.9 %collective-permute-start.4 = (bf16[64,1920]{1,0:T(8,128)(2,1)S(1)}, bf16[64,1920]{1,0:T(8,128)(2,1)S(1)}, u32[]{:S(2)}, u32[]{:S(2)}) collective-permute-start(bf16[64,1920]{1,0:T(8,128)(2,1)S(1)} %bitcast.152), channel_id=1, source_target_pairs={{0,16},{8,24},{16,0},{24,8},{1,17},{9,25},{17,1},{25,9},{2,18},{10... | collective-permute-start | bytes 737288 | tf_op jit(solution)/shard_map/ppermute | solution.py:34
  26.5 20.7 %collective-permute-start.3 = (bf16[64,1920]{1,0:T(8,128)(2,1)S(1)}, bf16[64,1920]{1,0:T(8,128)(2,1)S(1)}, u32[]{:S(2)}, u32[]{:S(2)}) collective-permute-start(bf16[64,1920]{1,0:T(8,128)(2,1)S(1)} %bitcast.153), channel_id=1, source_target_pairs={{0,8},{8,16},{16,24},{24,0},{1,9},{9,17},{17,25},{25,1},{2,10},{10... | collective-permute-start | bytes 737288 | tf_op jit(solution)/shard_map/ppermute | solution.py:34
  47.8 11.5 %collective-permute-start.7 = (bf16[4,32,1920]{2,1,0:T(8,128)(2,1)S(1)}, bf16[4,32,1920]{2,1,0:T(8,128)(2,1)S(1)}, u32[]{:S(2)}, u32[]{:S(2)}) collective-permute-start(bf16[4,32,1920]{2,1,0:T(8,128)(2,1)S(1)} %get-tuple-element.117.refs_1_), channel_id=1, source_target_pairs={{0,4},{4,0},{1,5},{5,1},{2,6},{6,2},{3,7},{7,3},{8,12},{12,8},{9,1... | collective-permute-start | bytes 1474568 | tf_op jit(solution)/shard_map/ppermute | solution.py:29
  49.1 11.1 %collective-permute-start.6 = (bf16[4,32,1920]{2,1,0:T(8,128)(2,1)S(1)}, bf16[4,32,1920]{2,1,0:T(8,128)(2,1)S(1)}, u32[]{:S(2)}, u32[]{:S(2)}) collective-permute-start(bf16[4,32,1920]{2,1,0:T(8,128)(2,1)S(1)} %get-tuple-element.119.refs_0_), channel_id=1, source_target_pairs={{0,2},{2,0},{1,3},{3,1},{4,6},{6,4},{5,7},{7,5},{8,10},{10,8},{9,1... | collective-permute-start | bytes 1474568 | tf_op jit(solution)/shard_map/ppermute | solution.py:25
  50.4 7.4 %collective-permute-start.8 = (bf16[64,2560]{1,0:T(8,128)(2,1)S(1)}, bf16[64,2560]{1,0:T(8,128)(2,1)S(1)}, u32[]{:S(2)}, u32[]{:S(2)}) collective-permute-start(bf16[64,2560]{1,0:T(8,128)(2,1)S(1)} %bitcast.147), channel_id=1, source_target_pairs={{0,8},{8,16},{16,24},{24,0},{1,9},{9,17},{17,25},{25,1},{2,10},{10... | collective-permute-start | bytes 983048 | tf_op jit(solution)/shard_map/ppermute | solution.py:34
  61.4 22.9 %collective-permute-start.11 = (bf16[2,4,32,1920]{3,2,1,0:T(8,128)(2,1)}, bf16[2,4,32,1920]{3,2,1,0:T(8,128)(2,1)S(1)}, u32[]{:S(2)}, u32[]{:S(2)}) collective-permute-start(bf16[2,4,32,1920]{3,2,1,0:T(8,128)(2,1)} %pad_maximum_fusion.13), channel_id=1, source_target_pairs={{0,4},{4,0},{1,5},{5,1},{2,6},{6,2},{3,7},{7,3},{8,12},{12,8},{9,1... | collective-permute-start | bytes 2949128 | tf_op jit(solution)/shard_map/ppermute | solution.py:29
  62.7 22.7 %collective-permute-start.12 = (bf16[2,4,32,1920]{3,2,1,0:T(8,128)(2,1)}, bf16[2,4,32,1920]{3,2,1,0:T(8,128)(2,1)S(1)}, u32[]{:S(2)}, u32[]{:S(2)}) collective-permute-start(bf16[2,4,32,1920]{3,2,1,0:T(8,128)(2,1)} %pad_maximum_fusion.14), channel_id=1, source_target_pairs={{0,2},{2,0},{1,3},{3,1},{4,6},{6,4},{5,7},{7,5},{8,10},{10,8},{9,1... | collective-permute-start | bytes 2949128 | tf_op jit(solution)/shard_map/ppermute | solution.py:25
  64.7 400.0 %reduce-scatter.2.cloned.1.call-start = ((), (), s32[]{:S(2)}) async-start(), calls=%async_computation.3 | async-start | bytes 4456448 | tf_op jit(solution)/shard_map/reduce_scatter | solution.py:818
  64.8 23.2 %collective-permute-start.10 = (bf16[64,2560]{1,0:T(8,128)(2,1)}, bf16[64,2560]{1,0:T(8,128)(2,1)S(1)}, u32[]{:S(2)}, u32[]{:S(2)}) collective-permute-start(bf16[64,2560]{1,0:T(8,128)(2,1)} %bitcast.148), channel_id=1, source_target_pairs={{0,24},{8,0},{16,8},{24,16},{1,25},{9,1},{17,9},{25,17},{2,26},{10... | collective-permute-start | bytes 983048 | tf_op jit(solution)/shard_map/ppermute | solution.py:34
  65.2 27.3 %collective-permute-start.9 = (bf16[64,2560]{1,0:T(8,128)(2,1)}, bf16[64,2560]{1,0:T(8,128)(2,1)S(1)}, u32[]{:S(2)}, u32[]{:S(2)}) collective-permute-start(bf16[64,2560]{1,0:T(8,128)(2,1)} %bitcast.149), channel_id=1, source_target_pairs={{0,16},{8,24},{16,0},{24,8},{1,17},{9,25},{17,1},{25,9},{2,18},{10... | collective-permute-start | bytes 983048 | tf_op jit(solution)/shard_map/ppermute | solution.py:34
  70.5 28.3 %collective-permute-start.15 = (bf16[512,1024]{1,0:T(8,128)(2,1)}, bf16[512,1024]{1,0:T(8,128)(2,1)}, u32[]{:S(2)}, u32[]{:S(2)}) collective-permute-start(bf16[512,1024]{1,0:T(8,128)(2,1)} %pad_maximum_fusion.9), channel_id=1, source_target_pairs={{0,1},{1,0},{2,3},{3,2},{4,5},{5,4},{6,7},{7,6},{8,9},{9,8},{10,11... | collective-permute-start | bytes 3145736 | tf_op jit(solution)/shard_map/ppermute | solution.py:21
  93.7 22.7 %collective-permute-start.13 = (bf16[4,32,2560]{2,1,0:T(8,128)(2,1)S(1)}, bf16[4,32,2560]{2,1,0:T(8,128)(2,1)}, u32[]{:S(2)}, u32[]{:S(2)}) collective-permute-start(bf16[4,32,2560]{2,1,0:T(8,128)(2,1)S(1)} %get-tuple-element.122.refs_0_), channel_id=1, source_target_pairs={{0,2},{2,0},{1,3},{3,1},{4,6},{6,4},{5,7},{7,5},{8,10},{10,8},{9,1... | collective-permute-start | bytes 1966088 | tf_op jit(solution)/shard_map/ppermute | solution.py:25
  95.0 21.5 %collective-permute-start.14 = (bf16[4,32,2560]{2,1,0:T(8,128)(2,1)S(1)}, bf16[4,32,2560]{2,1,0:T(8,128)(2,1)}, u32[]{:S(2)}, u32[]{:S(2)}) collective-permute-start(bf16[4,32,2560]{2,1,0:T(8,128)(2,1)S(1)} %get-tuple-element.123.refs_1_), channel_id=1, source_target_pairs={{0,4},{4,0},{1,5},{5,1},{2,6},{6,2},{3,7},{7,3},{8,12},{12,8},{9,1... | collective-permute-start | bytes 1966088 | tf_op jit(solution)/shard_map/ppermute | solution.py:29
  97.7 2.9 collective-permute-start.16
  118.7 43.5 %collective-permute-start.17 = (bf16[2,4,32,2560]{3,2,1,0:T(8,128)(2,1)}, bf16[2,4,32,2560]{3,2,1,0:T(8,128)(2,1)}, u32[]{:S(2)}, u32[]{:S(2)}) collective-permute-start(bf16[2,4,32,2560]{3,2,1,0:T(8,128)(2,1)} %pad_maximum_fusion.6), channel_id=1, source_target_pairs={{0,4},{4,0},{1,5},{5,1},{2,6},{6,2},{3,7},{7,3},{8,12},{12,8},{9,1... | collective-permute-start | bytes 3932168 | tf_op jit(solution)/shard_map/ppermute | solution.py:29
  122.3 44.1 %collective-permute-start.19 = (bf16[2,4,32,2560]{3,2,1,0:T(8,128)(2,1)}, bf16[2,4,32,2560]{3,2,1,0:T(8,128)(2,1)}, u32[]{:S(2)}, u32[]{:S(2)}) collective-permute-start(bf16[2,4,32,2560]{3,2,1,0:T(8,128)(2,1)} %pad_maximum_fusion.7), channel_id=1, source_target_pairs={{0,2},{2,0},{1,3},{3,1},{4,6},{6,4},{5,7},{7,5},{8,10},{10,8},{9,1... | collective-permute-start | bytes 3932168 | tf_op jit(solution)/shard_map/ppermute | solution.py:25
  168.8 5.4 %collective-permute-start.20 = (bf16[16,64,512]{2,1,0:T(8,128)(2,1)S(1)}, bf16[16,64,512]{2,1,0:T(8,128)(2,1)S(1)}, u32[]{:S(2)}, u32[]{:S(2)}) collective-permute-start(bf16[16,64,512]{2,1,0:T(8,128)(2,1)S(1)} %bitcast.145), channel_id=1, source_target_pairs={{0,1},{1,0},{2,3},{3,2},{4,5},{5,4},{6,7},{7,6},{8,9},{9,8},{10,11... | collective-permute-start | bytes 3145736 | tf_op jit(solution)/shard_map/ppermute | solution.py:21
  172.8 3.0 collective-permute-start.18
  201.1 3.3 collective-permute-start.22
  209.7 3.3 collective-permute-start.24
  239.6 11.1 %collective-permute-start.25 = (bf16[512,1024]{1,0:T(8,128)(2,1)S(1)}, bf16[512,1024]{1,0:T(8,128)(2,1)S(1)}, u32[]{:S(2)}, u32[]{:S(2)}) collective-permute-start(bf16[512,1024]{1,0:T(8,128)(2,1)S(1)} %slice.254), channel_id=1, source_target_pairs={{0,1},{1,0},{2,3},{3,2},{4,5},{5,4},{6,7},{7,6},{8,9},{9,8},{10,11... | collective-permute-start | bytes 3145736 | tf_op jit(solution)/shard_map/ppermute | solution.py:21
  250.5 37.0 %collective-permute-start.28 = (bf16[4,2,32,2048]{3,2,1,0:T(8,128)(2,1)}, bf16[4,2,32,2048]{3,2,1,0:T(8,128)(2,1)}, u32[]{:S(2)}, u32[]{:S(2)}) collective-permute-start(bf16[4,2,32,2048]{3,2,1,0:T(8,128)(2,1)} %get-tuple-element.150), channel_id=1, source_target_pairs={{0,4},{4,0},{1,5},{5,1},{2,6},{6,2},{3,7},{7,3},{8,12},{12,8},{9,1... | collective-permute-start | bytes 3145736 | tf_op jit(solution)/shard_map/ppermute | solution.py:29
  251.9 35.6 %collective-permute-start.27 = (bf16[4,2,32,2048]{3,2,1,0:T(8,128)(2,1)}, bf16[4,2,32,2048]{3,2,1,0:T(8,128)(2,1)}, u32[]{:S(2)}, u32[]{:S(2)}) collective-permute-start(bf16[4,2,32,2048]{3,2,1,0:T(8,128)(2,1)} %get-tuple-element.149), channel_id=1, source_target_pairs={{0,2},{2,0},{1,3},{3,1},{4,6},{6,4},{5,7},{7,5},{8,10},{10,8},{9,1... | collective-permute-start | bytes 3145736 | tf_op jit(solution)/shard_map/ppermute | solution.py:25
  257.2 6.7 %collective-permute-start.26 = (bf16[512,512]{1,0:T(8,128)(2,1)S(1)}, bf16[512,512]{1,0:T(8,128)(2,1)S(1)}, u32[]{:S(2)}, u32[]{:S(2)}) collective-permute-start(bf16[512,512]{1,0:T(8,128)(2,1)S(1)} %get-tuple-element.145), channel_id=1, source_target_pairs={{0,1},{1,0},{2,3},{3,2},{4,5},{5,4},{6,7},{7,6},{8,9},{9,8},{10,11... | collective-permute-start | bytes 1572872 | tf_op jit(solution)/shard_map/ppermute | solution.py:21
  259.4 89.0 %collective-permute-start.23 = (bf16[256,1024]{1,0:T(8,128)(2,1)}, bf16[256,1024]{1,0:T(8,128)(2,1)}, u32[]{:S(2)}, u32[]{:S(2)}) collective-permute-start(bf16[256,1024]{1,0:T(8,128)(2,1)} %slice.193), channel_id=1, source_target_pairs={{0,2},{2,0},{1,3},{3,1},{4,6},{6,4},{5,7},{7,5},{8,10},{10,8},{9,1... | collective-permute-start | bytes 1572872 | tf_op jit(solution)/shard_map/ppermute | solution.py:25
  280.1 23.7 %collective-permute-start.29 = (bf16[16,32,1024]{2,1,0:T(8,128)(2,1)}, bf16[16,32,1024]{2,1,0:T(8,128)(2,1)}, u32[]{:S(2)}, u32[]{:S(2)}) collective-permute-start(bf16[16,32,1024]{2,1,0:T(8,128)(2,1)} %get-tuple-element.159), channel_id=1, source_target_pairs={{0,1},{1,0},{2,3},{3,2},{4,5},{5,4},{6,7},{7,6},{8,9},{9,8},{10,11... | collective-permute-start | bytes 3145736 | tf_op jit(solution)/shard_map/ppermute | solution.py:21
  289.5 22.6 %collective-permute-start.30 = (bf16[4,32,2048]{2,1,0:T(8,128)(2,1)S(1)}, bf16[4,32,2048]{2,1,0:T(8,128)(2,1)S(1)}, u32[]{:S(2)}, u32[]{:S(2)}) collective-permute-start(bf16[4,32,2048]{2,1,0:T(8,128)(2,1)S(1)} %get-tuple-element.162), channel_id=1, source_target_pairs={{0,4},{4,0},{1,5},{5,1},{2,6},{6,2},{3,7},{7,3},{8,12},{12,8},{9,1... | collective-permute-start | bytes 1572872 | tf_op jit(solution)/shard_map/ppermute | solution.py:29
  306.2 34.9 %collective-permute-start.31 = (bf16[4,32,2048]{2,1,0:T(8,128)(2,1)S(1)}, bf16[4,32,2048]{2,1,0:T(8,128)(2,1)S(1)}, u32[]{:S(2)}, u32[]{:S(2)}) collective-permute-start(bf16[4,32,2048]{2,1,0:T(8,128)(2,1)S(1)} %get-tuple-element.163), channel_id=1, source_target_pairs={{0,2},{2,0},{1,3},{3,1},{4,6},{6,4},{5,7},{7,5},{8,10},{10,8},{9,1... | collective-permute-start | bytes 1572872 | tf_op jit(solution)/shard_map/ppermute | solution.py:25
  341.1 12.1 %collective-permute-start.32 = (bf16[512,1024]{1,0:T(8,128)(2,1)S(1)}, bf16[512,1024]{1,0:T(8,128)(2,1)S(1)}, u32[]{:S(2)}, u32[]{:S(2)}) collective-permute-start(bf16[512,1024]{1,0:T(8,128)(2,1)S(1)} %slice.253), channel_id=1, source_target_pairs={{0,1},{1,0},{2,3},{3,2},{4,5},{5,4},{6,7},{7,6},{8,9},{9,8},{10,11... | collective-permute-start | bytes 3145736 | tf_op jit(solution)/shard_map/ppermute | solution.py:21
  343.6 10.4 %collective-permute-start.43 = (bf16[64,2048]{1,0:T(8,128)(2,1)S(1)}, bf16[64,2048]{1,0:T(8,128)(2,1)S(1)}, u32[]{:S(2)}, u32[]{:S(2)}) collective-permute-start(bf16[64,2048]{1,0:T(8,128)(2,1)S(1)} %get-tuple-element.187), channel_id=1, source_target_pairs={{0,8},{8,16},{16,24},{24,0},{1,9},{9,17},{17,25},{25,1},{2,10},{10... | collective-permute-start | bytes 786440 | tf_op jit(solution)/shard_map/ppermute | solution.py:34
  343.6 33.8 %collective-permute-start.44 = (bf16[64,2048]{1,0:T(8,128)(2,1)S(1)}, bf16[64,2048]{1,0:T(8,128)(2,1)S(1)}, u32[]{:S(2)}, u32[]{:S(2)}) collective-permute-start(bf16[64,2048]{1,0:T(8,128)(2,1)S(1)} %get-tuple-element.188), channel_id=1, source_target_pairs={{0,16},{8,24},{16,0},{24,8},{1,17},{9,25},{17,1},{25,9},{2,18},{10... | collective-permute-start | bytes 786440 | tf_op jit(solution)/shard_map/ppermute | solution.py:34
  346.9 33.0 %collective-permute-start.45 = (bf16[64,2048]{1,0:T(8,128)(2,1)S(1)}, bf16[64,2048]{1,0:T(8,128)(2,1)S(1)}, u32[]{:S(2)}, u32[]{:S(2)}) collective-permute-start(bf16[64,2048]{1,0:T(8,128)(2,1)S(1)} %get-tuple-element.189), channel_id=1, source_target_pairs={{0,24},{8,0},{16,8},{24,16},{1,25},{9,1},{17,9},{25,17},{2,26},{10... | collective-permute-start | bytes 786440 | tf_op jit(solution)/shard_map/ppermute | solution.py:34
  350.6 53.9 %collective-permute-start.34 = (bf16[4,2,32,2048]{3,2,1,0:T(8,128)(2,1)S(1)}, bf16[4,2,32,2048]{3,2,1,0:T(8,128)(2,1)S(1)}, u32[]{:S(2)}, u32[]{:S(2)}) collective-permute-start(bf16[4,2,32,2048]{3,2,1,0:T(8,128)(2,1)S(1)} %get-tuple-element.171), channel_id=1, source_target_pairs={{0,2},{2,0},{1,3},{3,1},{4,6},{6,4},{5,7},{7,5},{8,10},{10,8},{9,1... | collective-permute-start | bytes 3145736 | tf_op jit(solution)/shard_map/ppermute | solution.py:25
  353.1 51.3 %collective-permute-start.35 = (bf16[4,2,32,2048]{3,2,1,0:T(8,128)(2,1)S(1)}, bf16[4,2,32,2048]{3,2,1,0:T(8,128)(2,1)S(1)}, u32[]{:S(2)}, u32[]{:S(2)}) collective-permute-start(bf16[4,2,32,2048]{3,2,1,0:T(8,128)(2,1)S(1)} %get-tuple-element.174), channel_id=1, source_target_pairs={{0,4},{4,0},{1,5},{5,1},{2,6},{6,2},{3,7},{7,3},{8,12},{12,8},{9,1... | collective-permute-start | bytes 3145736 | tf_op jit(solution)/shard_map/ppermute | solution.py:29
  382.0 25.9 %collective-permute-start.33 = (f32[41,128]{1,0:T(8,128)S(1)}, f32[41,128]{1,0:T(8,128)S(1)}, u32[]{:S(2)}, u32[]{:S(2)}) collective-permute-start(f32[41,128]{1,0:T(8,128)S(1)} %bitcast.173), channel_id=1, source_target_pairs={{0,1},{1,0},{2,3},{3,2},{4,5},{5,4},{6,7},{7,6},{8,9},{9,8},{10,11... | collective-permute-start | bytes 62984 | tf_op jit(solution)/shard_map/ppermute | solution.py:21
  382.9 35.0 %collective-permute-start.46 = (f32[32,16,128]{2,1,0:T(8,128)S(1)}, f32[32,16,128]{2,1,0:T(8,128)}, u32[]{:S(2)}, u32[]{:S(2)}) collective-permute-start(f32[32,16,128]{2,1,0:T(8,128)S(1)} %dynamic-slice_bitcast_fusion.4), channel_id=1, source_target_pairs={{0,1},{1,0},{2,3},{3,2},{4,5},{5,4},{6,7},{7,6},{8,9},{9,8},{10,11... | collective-permute-start | bytes 786440 | tf_op jit(solution)/shard_map/ppermute | solution.py:21
  405.5 17.0 %collective-permute-start.38 = (bf16[4,32,2048]{2,1,0:T(8,128)(2,1)S(1)}, bf16[4,32,2048]{2,1,0:T(8,128)(2,1)S(1)}, u32[]{:S(2)}, u32[]{:S(2)}) collective-permute-start(bf16[4,32,2048]{2,1,0:T(8,128)(2,1)S(1)} %get-tuple-element.181), channel_id=1, source_target_pairs={{0,2},{2,0},{1,3},{3,1},{4,6},{6,4},{5,7},{7,5},{8,10},{10,8},{9,1... | collective-permute-start | bytes 1572872 | tf_op jit(solution)/shard_map/ppermute | solution.py:25
  408.7 24.8 %collective-permute-start.36 = (bf16[256,1024]{1,0:T(8,128)(2,1)}, bf16[256,1024]{1,0:T(8,128)(2,1)}, u32[]{:S(2)}, u32[]{:S(2)}) collective-permute-start(bf16[256,1024]{1,0:T(8,128)(2,1)} %slice.256), channel_id=1, source_target_pairs={{0,2},{2,0},{1,3},{3,1},{4,6},{6,4},{5,7},{7,5},{8,10},{10,8},{9,1... | collective-permute-start | bytes 1572872 | tf_op jit(solution)/shard_map/ppermute | solution.py:25
  408.8 13.7 %collective-permute-start.37 = (bf16[4,32,2048]{2,1,0:T(8,128)(2,1)S(1)}, bf16[4,32,2048]{2,1,0:T(8,128)(2,1)S(1)}, u32[]{:S(2)}, u32[]{:S(2)}) collective-permute-start(bf16[4,32,2048]{2,1,0:T(8,128)(2,1)S(1)} %get-tuple-element.180), channel_id=1, source_target_pairs={{0,4},{4,0},{1,5},{5,1},{2,6},{6,2},{3,7},{7,3},{8,12},{12,8},{9,1... | collective-permute-start | bytes 1572872 | tf_op jit(solution)/shard_map/ppermute | solution.py:29
  411.5 44.7 %all-to-all-start = ((f32[16,64,128]{2,1,0:T(8,128)}), f32[16,64,128]{2,1,0:T(8,128)}, u32[]{:S(2)}, u32[]{:S(2)}) async-start(f32[16,64,128]{2,1,0:T(8,128)} %broadcast_in_dim.11), calls=%async_computation | async-start | bytes 1048576 | tf_op jit(solution)/shard_map/all_to_all | solution.py:165
  423.3 13.8 %collective-permute-start.39 = (bf16[64,2048]{1,0:T(8,128)(2,1)S(1)}, bf16[64,2048]{1,0:T(8,128)(2,1)S(1)}, u32[]{:S(2)}, u32[]{:S(2)}) collective-permute-start(bf16[64,2048]{1,0:T(8,128)(2,1)S(1)} %get-tuple-element.183), channel_id=1, source_target_pairs={{0,8},{8,16},{16,24},{24,0},{1,9},{9,17},{17,25},{25,1},{2,10},{10... | collective-permute-start | bytes 786440 | tf_op jit(solution)/shard_map/ppermute | solution.py:34
  424.6 26.7 %collective-permute-start.40 = (bf16[64,2048]{1,0:T(8,128)(2,1)S(1)}, bf16[64,2048]{1,0:T(8,128)(2,1)S(1)}, u32[]{:S(2)}, u32[]{:S(2)}) collective-permute-start(bf16[64,2048]{1,0:T(8,128)(2,1)S(1)} %get-tuple-element.184), channel_id=1, source_target_pairs={{0,16},{8,24},{16,0},{24,8},{1,17},{9,25},{17,1},{25,9},{2,18},{10... | collective-permute-start | bytes 786440 | tf_op jit(solution)/shard_map/ppermute | solution.py:34
  430.7 23.0 %collective-permute-start.41 = (bf16[64,2048]{1,0:T(8,128)(2,1)S(1)}, bf16[64,2048]{1,0:T(8,128)(2,1)S(1)}, u32[]{:S(2)}, u32[]{:S(2)}) collective-permute-start(bf16[64,2048]{1,0:T(8,128)(2,1)S(1)} %get-tuple-element.185), channel_id=1, source_target_pairs={{0,24},{8,0},{16,8},{24,16},{1,25},{9,1},{17,9},{25,17},{2,26},{10... | collective-permute-start | bytes 786440 | tf_op jit(solution)/shard_map/ppermute | solution.py:34
  454.5 4.6 collective-permute-start.42
  (70 other events, 548.8 us)
Sparse Core Ops, SparseCore 0:
  64.9 107.0 all-gather.1
  272.0 136.4 reduce-scatter.1

commit v3 on v2

--- a/solution.py
+++ b/solution.py
@@ -308,26 +308,31 @@
     )(where, parts.reshape(depth, 2, 2, 2, half, cols), got[0], got[1])
 
 
-def scatter_far(keep, got, where, tiled):
+def scatter_far(keep, got, where, tiled, ordered=False):
     x, c, y, z, depth = place()
     half, cols = keep[0].shape[1:]
     if not tiled:
         both = jnp.concatenate([add_low(k, g) for k, g in zip(keep, got)], axis=1)
-        return [pick(both, (z + k) % depth) for k in range(depth)]
+        return [both] if ordered else [pick(both, (z + k) % depth) for k in range(depth)]
 
     def kernel(where, top, low, top_got, low_got, *outs):
+        if ordered:
+            outs[0][:, :half] = add_low(top[...], top_got[...])
+            outs[0][:, half:] = add_low(low[...], low_got[...])
+            return
         for k in range(depth):
             at = lax.rem(where[3] + k, depth)
             outs[k][:half] = add_low(top[at], top_got[at])
             outs[k][half:] = add_low(low[at], low_got[at])
 
     near = pl.BlockSpec(memory_space=pltpu.VMEM)
-    shape = jax.ShapeDtypeStruct((2 * half, cols), keep[0].dtype)
+    shape = jax.ShapeDtypeStruct(((depth,) if ordered else ()) + (2 * half, cols), keep[0].dtype)
+    count = 1 if ordered else depth
     return pl.pallas_call(
         kernel,
         in_specs=[pl.BlockSpec(memory_space=pltpu.SMEM)] + [near] * 4,
-        out_specs=[near] * depth,
-        out_shape=[shape] * depth,
+        out_specs=[near] * count,
+        out_shape=[shape] * count,
         compiler_params=pltpu.CompilerParams(vmem_limit_bytes=32 << 20),
         cost_estimate=little,
         name="scatter_far",
@@ -350,8 +355,11 @@
     def far(self):
         self.got = [swap_y(self.got[0]), swap_x(self.got[1])]
 
-    def add_far(self):
-        self.got = list(scatter_far(self.keep, self.got, self.where, self.tiled))
+    def add_far(self, ordered=False):
+        self.got = list(scatter_far(self.keep, self.got, self.where, self.tiled, ordered))
+
+    def scatter_along(self):
+        self.got = [lax.psum_scatter(self.got[0], "z", scatter_dimension=0, tiled=True)[0]]
 
     def along(self):
         self.got = [self.got[0]] + [shift_z(v, k) for k, v in enumerate(self.got) if k]
@@ -361,8 +369,51 @@
 
 
 def gather_small(v):
-    chips = 4 * lax.axis_size("z")
-    return exchange(jnp.broadcast_to(v, (chips,) + v.shape), ("z", "y", "x"))
+    x, c, y, z, depth = place()
+    pieces = [v] + [shift_z(v, k) for k in range(1, depth)]
+    stack = jnp.zeros((depth,) + v.shape, v.dtype)
+    for k in range(depth):
+        stack = lax.dynamic_update_slice(stack, pieces[k][None], ((z - k) % depth, 0, 0))
+    other = swap_x(stack)
+    pair = jnp.stack([jnp.where(x == 0, stack, other), jnp.where(x == 0, other, stack)], axis=1)
+    other = swap_y(pair)
+    quad = jnp.stack([jnp.where(y == 0, pair, other), jnp.where(y == 0, other, pair)], axis=1)
+    return quad.reshape((4 * depth,) + v.shape)
+
+
+def finish(place_of, small, features, wide, rows, ff_rows):
+    chips = small.shape[0]
+    te_rows = features.shape[0]
+    blocks = wide // 128
+    starts = [0, blocks, 3 * blocks // 2, 2 * blocks, 5 * blocks // 2 + 1]
+    sizes = [2 * rows, rows, rows, rows, ff_rows]
+
+    def kernel(where, small, features, time_out, *refs):
+        outs, loss_out, sums = refs[:5], refs[5], refs[6]
+        sums[...] = jnp.sum(small[...], axis=0)
+        for n in range(blocks):
+            total = features[:, :1] * small[0, n : n + 1]
+            for k in range(1, chips):
+                total += features[:, k : k + 1] * small[k, n : n + 1]
+            time_out[:, n * 128 : (n + 1) * 128] = total
+        for start, size, out, at in zip(starts, sizes, outs, (0, 0, 0, 0, 1)):
+            first = where[at] * size
+            row = sums[pl.ds(start + first // 128, 1)]
+            out[...] = pltpu.roll(row, lax.rem(128 - lax.rem(first, 128), 128), 1)[:, :size]
+        loss_out[...] = sums[5 * blocks // 2 : 5 * blocks // 2 + 1, :1]
+
+    near = pl.BlockSpec(memory_space=pltpu.VMEM)
+    lines = [jax.ShapeDtypeStruct((1, n), f32) for n in sizes + [1]]
+    made = pl.pallas_call(
+        kernel,
+        in_specs=[pl.BlockSpec(memory_space=pltpu.SMEM), near, near],
+        out_specs=[near] * 7,
+        out_shape=[jax.ShapeDtypeStruct((te_rows, wide), f32)] + lines,
+        scratch_shapes=[pltpu.VMEM(small.shape[1:], f32)],
+        cost_estimate=little,
+        name="finish",
+    )(place_of, small, features)
+    return [made[0]] + [v.reshape(-1) for v in made[1:]]
 
 
 def project_kernel(source, scale, shift, weight, hidden_out, project_out):
@@ -566,14 +617,28 @@
     )(turned, mixture_grad, log_total, cosine, sine, *deps)
 
 
-def prepare_kernel(where, vector, qkv, up, out, time, own, other, out_low, time_low):
+def prepare_kernel(
+    where, steps, bias_time, gain, shift, bias_up, bias_down, mask, qkv, up, out, time,
+    own, other, out_low, time_low, lines,
+):
     c = where[1]
     rows, width = out.shape
+    count = jnp.sum(mask[...].astype(f32), axis=1, keepdims=True)
+    count = jnp.sum(count, axis=0, keepdims=True)
+    high = jnp.floor(count * (1.0 / 256.0))
+    step = steps[where[0]]
+    lane = lax.broadcasted_iota(jnp.int32, (1, 128), 1)
+    numbers = jnp.where(lane == 0, high, count - 256.0 * high)
+    numbers = jnp.where(lane == 2, (step // 32).astype(f32), numbers)
+    numbers = jnp.where(lane == 3, lax.rem(step, 32).astype(f32), numbers)
     half = width // 2
     step = 128
     for there, made in ((c, own), (1 - c, other)):
-        made[:, :128] = jnp.zeros((rows, 128), b16)
-        made[:3, :128] = vector[...].astype(b16)
+        lines[...] = jnp.zeros((rows, 128), f32)
+        for n, v in enumerate((bias_time, gain, shift, bias_up, bias_down)):
+            lines[n : n + 1, : v.shape[1]] = v[...]
+        lines[5:6] = numbers
+        made[:, :128] = lines[...].astype(b16)
         for p in range(half // 128):
             for n in range(3):
                 at = pl.multiple_of(n * width + there * half + p * 128, 128)
@@ -593,14 +658,15 @@
         time_low[n * te_rows : (n + 2) * te_rows] = jnp.concatenate(pair, axis=0).astype(b16)
 
 
-def prepare(where, vector, qkv, up, out, time):
+def prepare(where, steps, vectors, mask, qkv, up, out, time):
     rows, width = out.shape
     cols = 128 + 3 * width // 2 + up.shape[1] // 2
     near = pl.BlockSpec(memory_space=pltpu.VMEM)
     return pl.pallas_call(
         prepare_kernel,
-        in_specs=[pl.BlockSpec(memory_space=pltpu.SMEM)] + [near] * 5,
+        in_specs=[pl.BlockSpec(memory_space=pltpu.SMEM)] * 2 + [near] * 10,
         out_specs=[near] * 4,
+        scratch_shapes=[pltpu.VMEM((rows, 128), f32)],
         out_shape=[
             jax.ShapeDtypeStruct((rows, cols), b16),
             jax.ShapeDtypeStruct((rows, cols), b16),
@@ -609,7 +675,7 @@
         ],
         cost_estimate=little,
         name="prepare",
-    )(where, vector, qkv, up, out, time)
+    )(where, steps, *[v.reshape(1, -1) for v in vectors], mask, qkv, up, out, time)
 
 
 def body(
@@ -631,17 +697,13 @@
     tiled = rows % 32 == 0 and ff_rows % 128 == 0
     where = jnp.stack([x, c, y, z])
 
-    count = jnp.sum(valid_mask)
-    step = pick(time_steps, x)
-    whole_numbers = jnp.stack([count // 256, count % 256, step // 32, step % 32]).astype(f32)
-    vector = jnp.concatenate([time_bias, norm_gain, norm_bias, up_bias, down_bias, whole_numbers])
-    vector = jnp.pad(vector, (0, 384 - vector.shape[0])).reshape(3, 128)
     te_rows = time_weight.shape[0]
     te_folds = 2 * rows // te_rows
     cut = 128 + 3 * half
     if tiled:
         own, other, out_low, time_low = prepare(
-            where, vector, qkv_weight, up_weight, out_weight, time_weight
+            where, time_steps, (time_bias, norm_gain, norm_bias, up_bias, down_bias), valid_mask,
+            qkv_weight, up_weight, out_weight, time_weight,
         )
     else:
 
@@ -651,6 +713,11 @@
         def fold(v, n):
             return jnp.concatenate(jnp.split(v.astype(b16), n, axis=1), axis=0)
 
+        count = jnp.sum(valid_mask)
+        step = pick(time_steps, x)
+        whole_numbers = jnp.stack([count // 256, count % 256, step // 32, step % 32]).astype(f32)
+        vector = jnp.concatenate([time_bias, norm_gain, norm_bias, up_bias, down_bias, whole_numbers])
+        vector = jnp.pad(vector, (0, 384 - vector.shape[0])).reshape(3, 128)
         vector = jnp.pad(vector.astype(b16), ((0, rows - 3), (0, 0)))
         qkv_cut = qkv_weight.reshape(rows, 3, 2, pairs, 128).transpose(0, 3, 2, 1, 4)
         qkv_own, qkv_other = own_other(qkv_cut.reshape(rows, pairs, 2, 3 * 128))
@@ -689,16 +756,13 @@
     down_full = lax.all_gather(down_weight.astype(b16), ("z", "y", "x"), axis=0, tiled=True)
 
     source_far = swap_x(pick(inputs, 1 - x))
-    piece_1, source_far = tie(piece_1, source_far)
     marks = valid_mask.astype(b16)
     target_marks = jnp.concatenate(
         [teacher, jnp.broadcast_to(marks[:, :, None], (seqs, block, 128))], axis=2
     )
-    target_far, source_far = tie(pick(target_marks, 1 - x), source_far)
-    target_far = swap_x(target_far)
     pieces_1 = gather_z(piece_1, tiled)
     stack_1 = stack_z(pieces_1, tiled)
-    target_far, stack_1[0] = tie(target_far, stack_1[0])
+    source_far, stack_1[0] = tie(source_far, stack_1[0])
     piece_2, stack_1[1] = tie(piece_2, stack_1[1])
     pieces_2 = gather_z(piece_2, tiled)
     near_1 = list(gather_near(stack_1))
@@ -721,14 +785,14 @@
     sine = jnp.sin(angles)
     sine = jnp.tile(jnp.concatenate([-sine, sine], axis=1), (1, 2))
 
-    vectors = vectors.reshape(chips, 2, rows, 128)[:, :, :3].reshape(chips, 2, 384)
-    vectors = vectors.astype(f32)
+    vectors = vectors.reshape(chips, 2, rows, 128).astype(f32)
+    packed = vectors[:, :, :3].reshape(chips, 2, 384)
     at = 0
 
     def take(n):
         nonlocal at
-        at += n
-        return vectors[:, :, at - n : at]
+        at += 1 if tiled else n
+        return vectors[:, :, at - 1, :n] if tiled else packed[:, :, at - n : at]
 
     bias_time = take(time_bias.shape[0]).reshape(2 * width)
     gain = take(rows).reshape(width)
@@ -757,6 +821,8 @@
     turned_a, mixed_a, log_a = attend(project, cosine, sine, 0, ahead)
     turned_b, mixed_b, log_b = attend(project, cosine, sine, ahead, pairs - ahead, (mixed_a,))
     far_2[0], mixed_a, mixed_b = tie(far_2[0], mixed_a, mixed_b)
+    target_far, far_2[1] = tie(pick(target_marks, 1 - x), far_2[1])
+    target_far = swap_x(target_far)
     up_full, out_half = assemble(near_2, far_2, [0, ff, ff + half], tiled)
     up_full = up_full.reshape(width, ff)
     out_far = swap_core(out_half)
@@ -793,6 +859,7 @@
     flat = 0.5 * (1.0 + lax.erf(inner * (2.0**-0.5)))
     active = (inner * flat).astype(b16)
     slope = flat + inner * jnp.exp(-0.5 * inner * inner) * ((2.0 * math.pi) ** -0.5)
+    active, target_far = tie(active, target_far)
     down = dot(active, down_full, 1, 0)
     result = middle + (down[:mine] + swap_core(down[mine:].astype(b16)).astype(f32) + bias_down)
 
@@ -803,27 +870,25 @@
     loss_part = jnp.sum(mark * differ * differ)
     result_grad = 2.0 * mark * differ * factor
 
-    def spread_out(v):
-        far = swap_x(v[block:].astype(b16)).astype(v.dtype)
-        near = v[:block]
-        return jnp.stack([jnp.where(x == 0, near, far), jnp.where(x == 0, far, near)])
-
     down_in = result_grad.astype(b16)
     down_in_all = jnp.concatenate([down_in, swap_core(down_in)], axis=0)
     near_axes = ("y", "x")
     result_low = result.astype(b16)
-    result_far = swap_x(result_low[block:])
     down_term = dot(active, down_in_all, 0, 0).astype(b16)
-    down_in_all, down_term = tie(down_in_all, down_term)
-    down_sum = lax.psum_scatter(down_term, ("z", "y", "x"), scatter_dimension=0, tiled=True)
+    down_sum = Scatter(down_term.reshape(chips, -1, width), where, tiled)
+    down_in_all, down_sum.got[0] = tie(down_in_all, down_sum.got[0])
+    down_sum.near()
     inner_grad = (dot(down_in_all, down_full, 1, 1) * slope).astype(b16)
     second_part = dot(inner_grad, up_full, 1, 1)
     second_send, second_all = tie(second_part[mine:].astype(b16), second_all)
     second_got = swap_core(second_send)
     up_term = dot(second_all, inner_grad, 0, 0).astype(b16)
     up_sum = Scatter(up_term.reshape(chips, -1, ff), where, tiled)
-    second_got, up_sum.got[0] = tie(second_got, up_sum.got[0])
+    second_got, up_sum.got[0], *down_sum.got = tie(second_got, up_sum.got[0], *down_sum.got)
     up_sum.near()
+    down_sum.add_near()
+    second_got, down_sum.got[0] = tie(second_got, down_sum.got[0])
+    down_sum.far()
     second_grad = second_part[:mine] + second_got.astype(f32)
     middle_grad = result_grad + norm_back(second_grad * gain, n2, rate2)
     branch = middle_grad.astype(b16)
@@ -847,7 +912,12 @@
         return attend_back(turned, log, mixture_grad, cosine, sine, at, p, 1, deps)
 
     grads = [pair_back(0, ())]
-    for p in range(1, pairs - 1):
+    grads.append(pair_back(1, (grads[-1],)))
+    down_sum.got[0], down_sum.got[1], grads[-1] = tie(down_sum.got[0], down_sum.got[1], grads[-1])
+    down_sum.add_far(True)
+    grads[-1], down_sum.got[0] = tie(grads[-1], down_sum.got[0])
+    down_sum.scatter_along()
+    for p in range(2, pairs - 1):
         grads.append(pair_back(p, (grads[-1],)))
     up_sum.got[0], up_sum.got[1], grads[-1] = tie(up_sum.got[0], up_sum.got[1], grads[-1])
     up_sum.add_near()
@@ -866,17 +936,11 @@
         hidden_part[mine:].astype(b16), hidden_part[:mine], *up_sum.got
     )
     hidden_got = swap_core(hidden_got)
-    up_sum.add_far()
+    up_sum.add_far(True)
     up_sum.got[0], hidden_got = tie(up_sum.got[0], hidden_got)
-    up_sum.along()
+    up_sum.scatter_along()
     hidden_grad = hidden_keep + hidden_got.astype(f32)
     n1, rate1 = stats(source_low.astype(f32))
-    activations = jnp.stack(
-        [
-            jnp.where(x == 0, result_low[:block], result_far),
-            jnp.where(x == 0, result_far, result_low[:block]),
-        ]
-    )
     input_grad = middle_grad + norm_back(hidden_grad * scale, n1, rate1)
 
     small = jnp.concatenate(
@@ -900,31 +964,27 @@
     fill = jnp.zeros((-(small.shape[0] + up_bias_part.shape[0]) % 8, 128), f32)
     small = jnp.concatenate([small, up_bias_part, fill], axis=0)
     small = gather_small(small)
-    input_grad = spread_out(input_grad)
     up_sum = up_sum.total()
     last_sum.add_far()
+    input_far, result_far, last_sum.got[1] = tie(
+        input_grad[block:].astype(b16), result_low[block:], last_sum.got[1]
+    )
     last_sum.along()
-    last_sum = last_sum.total()
-    down_sum = down_sum.astype(f32)
+    input_far = swap_x(input_far).astype(f32)
+    result_far = swap_x(result_far)
+
+    def spread_out(near, far):
+        return jnp.stack([jnp.where(x == 0, near, far), jnp.where(x == 0, far, near)])
+
+    activations = spread_out(result_low[:block], result_far)
+    input_grad = spread_out(input_grad[:block], input_far)
+    down_sum = down_sum.total()
     index = 2 * k_chip + c
     feature_rows = lax.dynamic_slice_in_dim(features, index * te_rows, te_rows, 1).astype(f32)
-    time_sum = lax.dot_general(
-        feature_rows,
-        small[:, : 2 * width // 128].reshape(chips, -1),
-        (((0,), (0,)), ((), ())),
-        precision=highest,
-    )
-    sums = jnp.sum(small, axis=0).reshape(-1)
-
-    def share(start, size, index):
-        return lax.dynamic_slice_in_dim(sums[start:], index * size, size, 0)
-
-    time_bias_sum = share(0, 2 * rows, index)
-    gain_sum = share(2 * width, rows, index)
-    shift_sum = share(3 * width, rows, index)
-    down_bias_sum = share(4 * width, rows, index)
-    up_bias_sum = share(5 * width + 128, ff_rows, k_chip)
-    loss = (sums[5 * width] / (valid_total * width)).reshape(1)
+    time_sum, time_bias_sum, gain_sum, shift_sum, down_bias_sum, up_bias_sum, loss_sum = finish(
+        jnp.stack([index, k_chip]), small, feature_rows.T, 2 * width, rows, ff_rows
+    )
+    loss = (loss_sum[0] / (valid_total * width)).reshape(1)
 
     def columns(total, inner_size):
         total = total.reshape(2, rows, -1, inner_size)
@@ -934,6 +994,12 @@
             [jnp.where(c == 0, near, far), jnp.where(c == 0, far, near)], axis=2
         ).reshape(rows, -1)
 
+    up_sum = columns(up_sum, ff_rows)
+    others = (activations, input_grad, up_sum, down_sum, time_sum, loss)
+    tied = tie(*last_sum.got, *others)
+    last_sum.got = tied[: -len(others)]
+    activations, input_grad, up_sum, down_sum, time_sum, loss = tied[-len(others) :]
+    last_sum = last_sum.total()
     out_sum = last_sum[:, qkv_cols:]
     out_sum = jnp.concatenate([out_sum[:rows], out_sum[rows:]], axis=1)
     qkv_sum = last_sum[:, :qkv_cols].reshape(2 * rows, pairs, 3, 128)
@@ -944,7 +1010,7 @@
         input_grad,
         columns(qkv_sum, half),
         out_sum,
-        columns(up_sum, ff_rows),
+        up_sum,
         down_sum,
         time_sum,
         time_bias_sum,

time: 480 us -> 458 us (0.954)
  waiting for transfers between devices: 167 us -> 124 us
  other arithmetic: 45.7 us -> 60.3 us
  Pallas kernels: 71.5 us -> 83.4 us
  local copies, waits for them, and re-layouts: 39 us -> 47.8 us
  between operations: 23.9 us -> 18.4 us
  starting transfers between devices: 67.9 us -> 62.7 us
    ppermute x12, waiting for transfers between devices: 71.6 us -> 31.6 us  [shift_z(): return lax.ppermute(v, 'z', [(i, (i + k) % depth) for i in range(depth)])]
    ppermute x8 -> x11, waiting for transfers between devices: 25.9 us -> 12.2 us  [swap_y(): return lax.ppermute(v, 'y', [(0, 1), (1, 0)])]
    ppermute x12 -> x15, waiting for transfers between devices: 66.1 us -> 77 us  [swap_x(): return lax.ppermute(v, 'x', [(0, 1), (1, 0)])]
    unnamed x145 -> x173, local copies, waits for them, and re-layouts: 17.9 us -> 27.6 us
    ppermute x12, starting transfers between devices: 22.6 us -> 13.3 us  [shift_z(): return lax.ppermute(v, 'z', [(i, (i + k) % depth) for i in range(depth)])]
    ppermute x15, starting transfers between devices: 16.1 us -> 24.9 us  [swap_core(): return lax.ppermute(v, 'core', [(0, 1), (1, 0)])]
    all_to_all x1 -> x0, starting transfers between devices: 6.37 us -> none  [exchange(): return lax.all_to_all(v, axes, 0, 0, tiled=True)]
    another operation x2 -> x4, other arithmetic: 2.76 us -> 8.6 us  [spread_out(): jnp.stack([jnp.where(x == 0, near, far), jnp.where(x == 0, far, near)])]
  transfers between devices with their start and end apart: 50 -> 56, of which waited for: 24 -> 27; matrix products, arithmetic and copies ran while one was open for 18% -> 22% of each run, Pallas kernels for 15% -> 18%
where the time goes in v3:
time: 458 us; the launch traced here: 452 us
  waiting for transfers between devices  124 us (27%)
  Pallas kernels  83.4 us (18%)
  starting transfers between devices  62.7 us (14%)
  other arithmetic  60.3 us (13%)
  matrix products  55.7 us (12%)
  local copies, waits for them, and re-layouts  47.8 us (10%)
  between operations  18.4 us (4%)
    ppermute x15, waiting for transfers between devices, swap_x(): return lax.ppermute(v, 'x', [(0, 1), (1, 0)])  77 us
    dot_general x11, matrix products, dot(): lax.dot_general(a, b, (((da,), (db,)), ((), ())), preferred_element_type=...  55.7 us
    ppermute x12, waiting for transfers between devices, shift_z(): return lax.ppermute(v, 'z', [(i, (i + k) % depth) for i in range(depth)])  31.6 us
    unnamed x173, local copies, waits for them, and re-layouts  27.6 us
    pallas_call x4, Pallas kernels, attend_back(): pl.pallas_call(attend_back_kernel, grid=(pairs,), in_specs=[pl.BlockSpec(...  27 us
    ppermute x15, starting transfers between devices, swap_core(): return lax.ppermute(v, 'core', [(0, 1), (1, 0)])  24.9 us
    pallas_call x2, Pallas kernels, attend(): pl.pallas_call(attend_kernel, grid=(pairs,), in_specs=[pl.BlockSpec((toke...  21.1 us
    ppermute x15, starting transfers between devices, swap_x(): return lax.ppermute(v, 'x', [(0, 1), (1, 0)])  18 us
  transfers between devices with their start and end apart: 56, of which 27 were waited for; matrix products, arithmetic and copies ran while one was open for 22% of the time, Pallas kernels for 18%

profile of v3, /device:TPU:9, one launch (start us, length us, event | category | flops | bytes accessed | tf_op | source)
XLA Modules:
  0.0 452.1 jit_solution(11766440244860322291)
XLA Ops:
  23.9 3.4 collective-permute-done.2.refs_1_
  27.3 14.9 %collective-permute-done.3.refs_2_ = bf16[64,1920]{1,0:T(8,128)(2,1)S(1)} collective-permute-done((bf16[64,1920]{1,0:T(8,128)(2,1)S(1)}, bf16[64,1920]{1,0:T(8,128)(2,1)S(1)}, u32[]{:S(2)}, u32[]{:S(2)}) %collective-permute-start.3) | collective-permute-done | bytes 245792 | tf_op jit(solution)/shard_map/ppermute | solution.py:34
  42.2 2.5 collective-permute-done.4.refs_3_
  46.9 8.4 %collective-permute-done.8.refs_1_ = bf16[64,2560]{1,0:T(8,128)(2,1)S(1)} collective-permute-done((bf16[64,2560]{1,0:T(8,128)(2,1)}, bf16[64,2560]{1,0:T(8,128)(2,1)S(1)}, u32[]{:S(2)}, u32[]{:S(2)}) %collective-permute-start.8) | collective-permute-done | bytes 327712 | tf_op jit(solution)/shard_map/ppermute | solution.py:34
  55.3 2.4 collective-permute-done.7.refs_3_
  64.9 2.7 collective-permute-start.5
  67.6 15.9 %collective-permute-done.10.refs_5_ = bf16[2,4,32,1920]{3,2,1,0:T(8,128)(2,1)S(1)} collective-permute-done((bf16[2,4,32,1920]{3,2,1,0:T(8,128)(2,1)}, bf16[2,4,32,1920]{3,2,1,0:T(8,128)(2,1)S(1)}, u32[]{:S(2)}, u32[]{:S(2)}) %collective-permute-start.10) | collective-permute-done | bytes 983072 | tf_op jit(solution)/shard_map/ppermute | solution.py:25
  94.2 2.9 collective-permute-start.11
  99.8 8.3 %project.1 = (bf16[1024,1024]{1,0:T(8,128)(2,1)S(1)}, f32[1024,1536]{1,0:T(8,128)}) custom-call(bf16[1024,1024]{1,0:T(8,128)(2,1)S(1)} %pad_maximum_fusion.2.source, f32[1,1024]{1,0:T(1,128)S(1)} %get-tuple-element.302.scale, f32[1,1024]{1,0:T(1,128)S(1)} %get-tuple-element.301.shift, bf16[1024,1536]{1,0:T(8,128)(2,1)} %bitcast.161), custom_call_target="tpu_custom_call" | custom-call | flops 1 | bytes 1 | tf_op jit(solution)/shard_map/project/pallas_call | solution.py:433
  120.0 2.3 fusion.26
  122.3 10.3 %attend.2 = (bf16[1024,768]{1,0:T(8,128)(2,1)S(1)}, bf16[1024,256]{1,0:T(8,128)(2,1)S(1)}, f32[2,2,1024]{2,1,0:T(2,128)S(1)}) custom-call(f32[1024,1536]{1,0:T(8,128)} %get-tuple-element.155.project_in, f32[1024,128]{1,0:T(8,128)S(1)} %copy.122.cos_in, f32[1024,128]{1,0:T(8,128)S(1)} %copy.123.sin_in), custom_call_target="tpu_custom_call" | custom-call | flops 1 | bytes 1 | tf_op jit(solution)/shard_map/attend/pallas_call | solution.py:530
  133.8 10.7 %attend.3 = (bf16[1024,768]{1,0:T(8,128)(2,1)S(1)}, bf16[1024,256]{1,0:T(8,128)(2,1)S(1)}, f32[2,2,1024]{2,1,0:T(2,128)S(1)}) custom-call(f32[1024,1536]{1,0:T(8,128)} %get-tuple-element.155.project_in, f32[1024,128]{1,0:T(8,128)S(1)} %copy.122.cos_in, f32[1024,128]{1,0:T(8,128)S(1)} %copy.123.sin_in, bf16[1024,256]{1,0:T(8,128)(2,1)S(1)} %get-tuple-element.160.refs_0_), custom_call_target="tpu_custom_call" | custom-call | flops 1 | bytes 1 | tf_op jit(solution)/shard_map/attend/pallas_call | solution.py:530
  144.6 6.5 %collective-permute-done.16.refs_4_ = bf16[2,4,32,2560]{3,2,1,0:T(8,128)(2,1)} collective-permute-done((bf16[2,4,32,2560]{3,2,1,0:T(8,128)(2,1)}, bf16[2,4,32,2560]{3,2,1,0:T(8,128)(2,1)}, u32[]{:S(2)}, u32[]{:S(2)}) %collective-permute-start.16) | collective-permute-done | bytes 1310752 | tf_op jit(solution)/shard_map/ppermute | solution.py:29
  151.0 7.6 %collective-permute-done.18.refs_5_ = bf16[2,4,32,2560]{3,2,1,0:T(8,128)(2,1)} collective-permute-done((bf16[2,4,32,2560]{3,2,1,0:T(8,128)(2,1)}, bf16[2,4,32,2560]{3,2,1,0:T(8,128)(2,1)}, u32[]{:S(2)}, u32[]{:S(2)}) %collective-permute-start.18) | collective-permute-done | bytes 1310752 | tf_op jit(solution)/shard_map/ppermute | solution.py:25
  158.6 2.5 move.13
  161.1 5.0 %collective-permute-start.19 = (bf16[16,64,512]{2,1,0:T(8,128)(2,1)S(1)}, bf16[16,64,512]{2,1,0:T(8,128)(2,1)S(1)}, u32[]{:S(2)}, u32[]{:S(2)}) collective-permute-start(bf16[16,64,512]{2,1,0:T(8,128)(2,1)S(1)} %bitcast.171), channel_id=1, source_target_pairs={{0,1},{1,0},{2,3},{3,2},{4,5},{5,4},{6,7},{7,6},{8,9},{9,8},{10,11... | collective-permute-start | bytes 3145736 | tf_op jit(solution)/shard_map/ppermute | solution.py:21
  170.2 2.6 fusion.49
  176.6 8.8 %multiply_convert_fusion = (bf16[1024,2048]{1,0:T(8,128)(2,1)}, f32[1024,2048]{1,0:T(8,128)}) fusion(f32[2048]{0:T(1024)S(1)} %bitcast.202, bf16[1024,2048]{1,0:T(8,128)(2,1)S(1)} %bitcast.183, bf16[512,1024]{1,0:T(8,128)(2,1)S(1)} %collective-permute-done.20, bf16[512,1024]{1,0:T(8,128)(2,1)S(1)} %add_convert_fusion.1), kind=kOutput, calls=%fused_computation.8 | convolution fusion | flops 4311744512 | bytes 18882560 | tf_op jit(solution)/shard_map/dot_general | solution.py:468
  185.4 4.4 collective-permute-done.21
  189.8 7.5 %fusion.50 = f32[1024,1024]{1,0:T(8,128)S(1)} fusion(bf16[1024,2048]{1,0:T(8,128)(2,1)} %get-tuple-element.169, bf16[2048,1024]{1,0:T(8,128)(2,1)} %all-gather.2.cloned.1.call-done), kind=kOutput, calls=%fused_computation.183 | convolution fusion | flops 4294967296 | bytes 12582912 | tf_op jit(solution)/shard_map/dot_general | solution.py:468
  204.7 4.9 %fusion.17 = (f32[]{:T(128)}, f32[512,1024]{1,0:T(8,128)S(1)}, bf16[512,1024]{1,0:T(8,128)(2,1)}) fusion(f32[512]{0:T(512)S(1)} %get-tuple-element.262, bf16[256,1152]{1,0:T(8,128)(2,1)} %collective-permute-done.21, bf16[256,1152]{1,0:T(8,128)(2,1)S(1)} %copy-done.64, f32[512,1024]{1,0:T(8,128)} %copy-done.49, f32[1024]{0:T(1024)S(1)} %add.248, ...), kind=kLoop, calls=%fused_computation.30 | loop fusion | flops 6815743 | bytes 9574404 | tf_op jit(solution)/shard_map/reduce_sum | solution.py:870
  213.3 5.0 %convolution_convert_fusion.2 = bf16[2048,1024]{1,0:T(8,128)(2,1)S(1)} fusion(bf16[1024,2048]{1,0:T(8,128)(2,1)S(1)} %copy-done.78, bf16[512,1024]{1,0:T(8,128)(2,1)S(1)} %collective-permute-done.23, bf16[512,1024]{1,0:T(8,128)(2,1)S(1)} %get-tuple-element.271), kind=kOutput, calls=%fused_computation.13 | convolution fusion | flops 4301258752 | bytes 10485760 | tf_op jit(solution)/shard_map/dot_general | solution.py:468
  218.2 2.4 move.15
  223.1 8.0 %convert_reduce_fusion = (f32[2048]{0:T(1024)S(1)}, bf16[1024,2048]{1,0:T(8,128)(2,1)S(1)}) fusion(f32[1024,2048]{1,0:T(8,128)S(1)} %bitcast.215, f32[2048]{0:T(1024)S(1)} %bitcast.203, bf16[1024,1024]{1,0:T(8,128)(2,1)S(1)} %pad_maximum_fusion.4, bf16[2048,1024]{1,0:T(8,128)(2,1)S(1)} %copy-done.76), kind=kOutput, calls=%fused_computation.7 | convolution fusion | flops 4322228224 | bytes 18890752 | tf_op jit(solution)/shard_map/dot_general | solution.py:468
  231.1 4.5 %fusion.51 = f32[1024,1024]{1,0:T(8,128)S(1)} fusion(bf16[1024,2048]{1,0:T(8,128)(2,1)S(1)} %get-tuple-element.313, bf16[1024,2048]{1,0:T(8,128)(2,1)S(1)} %bitcast.184), kind=kOutput, calls=%fused_computation.184 | convolution fusion | flops 4294967296 | bytes 12582912 | tf_op jit(solution)/shard_map/dot_general | solution.py:468
  238.6 7.4 %convolution_convert_fusion.1 = bf16[1024,2048]{1,0:T(8,128)(2,1)S(1)} fusion(bf16[1024,1024]{1,0:T(8,128)(2,1)} %pad_maximum_fusion.3, bf16[1024,2048]{1,0:T(8,128)(2,1)} %copy-done.77), kind=kOutput, calls=%fused_computation.12 | convolution fusion | flops 4297064448 | bytes 10485760 | tf_op jit(solution)/shard_map/dot_general | solution.py:468
  250.5 11.0 %collective-permute-done.25.top = bf16[4,2,64,1024]{3,2,1,0:T(8,128)(2,1)S(1)} collective-permute-done((bf16[4,2,64,1024]{3,2,1,0:T(8,128)(2,1)}, bf16[4,2,64,1024]{3,2,1,0:T(8,128)(2,1)S(1)}, u32[]{:S(2)}, u32[]{:S(2)}) %collective-permute-start.25) | collective-permute-done | bytes 1048608 | tf_op jit(solution)/shard_map/ppermute | solution.py:25
  266.2 2.4 multiply_reduce_fusion
  270.6 3.5 fusion.44
  279.3 2.9 convolution_convert_fusion.3
  285.4 6.6 %attend_back.4.refs_0_ = bf16[1024,384]{1,0:T(8,128)(2,1)S(1)} custom-call(bf16[1024,768]{1,0:T(8,128)(2,1)S(1)} %copy-done.9, bf16[1024,512]{1,0:T(8,128)(2,1)S(1)} %pad_maximum_fusion.10.grad_in, f32[2,2,1024]{2,1,0:T(2,128)S(1)} %get-tuple-element.185.log_in, f32[1024,128]{1,0:T(8,128)S(1)} %copy.122.cos_in, f32[1024,128]{1,0:T(8,128)S(1)} %copy.123.sin_in), custom_call_target="tpu_custom_call" | custom-call | flops 1 | bytes 1 | tf_op jit(solution)/shard_map/attend_back/pallas_call | solution.py:596
  292.0 7.0 %attend_back.5.refs_0_ = bf16[1024,384]{1,0:T(8,128)(2,1)S(1)} custom-call(bf16[1024,768]{1,0:T(8,128)(2,1)S(1)} %copy-done.9, bf16[1024,512]{1,0:T(8,128)(2,1)S(1)} %pad_maximum_fusion.10.grad_in, f32[2,2,1024]{2,1,0:T(2,128)S(1)} %get-tuple-element.185.log_in, f32[1024,128]{1,0:T(8,128)S(1)} %copy.122.cos_in, f32[1024,128]{1,0:T(8,128)S(1)} %copy.123.sin_in, ...), custom_call_target="tpu_custom_call" | custom-call | flops 1 | bytes 1 | tf_op jit(solution)/shard_map/attend_back/pallas_call | solution.py:596
  299.0 4.3 collective-permute-done.29.low_got
  305.1 2.8 collective-permute-start.32
  309.4 6.6 %attend_back.6.refs_0_ = bf16[1024,384]{1,0:T(8,128)(2,1)S(1)} custom-call(bf16[1024,768]{1,0:T(8,128)(2,1)S(1)} %copy-done.11, bf16[1024,512]{1,0:T(8,128)(2,1)S(1)} %pad_maximum_fusion.10.grad_in, f32[2,2,1024]{2,1,0:T(2,128)S(1)} %get-tuple-element.197.log_in, f32[1024,128]{1,0:T(8,128)S(1)} %copy.122.cos_in, f32[1024,128]{1,0:T(8,128)S(1)} %copy.123.sin_in, ...), custom_call_target="tpu_custom_call" | custom-call | flops 1 | bytes 1 | tf_op jit(solution)/shard_map/attend_back/pallas_call | solution.py:596
  318.9 6.8 %attend_back.7 = bf16[1024,384]{1,0:T(8,128)(2,1)S(1)} custom-call(bf16[1024,768]{1,0:T(8,128)(2,1)S(1)} %copy-done.12, bf16[1024,512]{1,0:T(8,128)(2,1)S(1)} %pad_maximum_fusion.10.grad_in, f32[2,2,1024]{2,1,0:T(2,128)S(1)} %get-tuple-element.197.log_in, f32[1024,128]{1,0:T(8,128)S(1)} %copy.122.cos_in, f32[1024,128]{1,0:T(8,128)S(1)} %copy.123.sin_in, ...), custom_call_target="tpu_custom_call" | custom-call | flops 1 | bytes 1 | tf_op jit(solution)/shard_map/attend_back/pallas_call | solution.py:596
  327.3 4.3 convolution_convert_fusion
  338.0 3.4 fusion.52
  345.0 2.8 collective-permute-done.35.low_got
  356.3 3.4 fusion.15
  361.0 4.2 fusion.14
  365.2 10.5 %collective-permute-done.33.top = bf16[4,2,32,2048]{3,2,1,0:T(8,128)(2,1)S(1)} collective-permute-done((bf16[4,2,32,2048]{3,2,1,0:T(8,128)(2,1)}, bf16[4,2,32,2048]{3,2,1,0:T(8,128)(2,1)S(1)}, u32[]{:S(2)}, u32[]{:S(2)}) %collective-permute-start.33) | collective-permute-done | bytes 1048608 | tf_op jit(solution)/shard_map/ppermute | solution.py:25
  379.7 4.9 %collective-permute-start.48 = (f32[64,128]{1,0:T(8,128)S(1)}, f32[64,128]{1,0:T(8,128)S(1)}, u32[]{:S(2)}, u32[]{:S(2)}) collective-permute-start(f32[64,128]{1,0:T(8,128)S(1)} %get-tuple-element.267), channel_id=1, source_target_pairs={{0,16},{8,24},{16,0},{24,8},{1,17},{9,25},{17,1},{25,9},{2,18},{10... | collective-permute-start | bytes 98312 | tf_op jit(solution)/shard_map/ppermute | solution.py:34
  395.9 6.6 %collective-permute-done.40.low_got = bf16[4,32,2048]{2,1,0:T(8,128)(2,1)S(1)} collective-permute-done((bf16[4,32,2048]{2,1,0:T(8,128)(2,1)}, bf16[4,32,2048]{2,1,0:T(8,128)(2,1)S(1)}, u32[]{:S(2)}, u32[]{:S(2)}) %collective-permute-start.40) | collective-permute-done | bytes 524320 | tf_op jit(solution)/shard_map/ppermute | solution.py:25
  411.1 2.7 collective-permute-start.42
  416.1 9.0 %collective-permute-done.45 = bf16[256,1024]{1,0:T(8,128)(2,1)} collective-permute-done((bf16[256,1024]{1,0:T(8,128)(2,1)}, bf16[256,1024]{1,0:T(8,128)(2,1)}, u32[]{:S(2)}, u32[]{:S(2)}) %collective-permute-start.45) | collective-permute-done | bytes 524320 | tf_op jit(solution)/shard_map/ppermute | solution.py:25
  425.0 2.6 fusion.21
  428.9 4.9 %collective-permute-start.46 = (f32[32,16,128]{2,1,0:T(8,128)S(1)}, f32[32,16,128]{2,1,0:T(8,128)S(1)}, u32[]{:S(2)}, u32[]{:S(2)}) collective-permute-start(f32[32,16,128]{2,1,0:T(8,128)S(1)} %dynamic-slice_bitcast_fusion.4), channel_id=1, source_target_pairs={{0,1},{1,0},{2,3},{3,2},{4,5},{5,4},{6,7},{7,6},{8,9},{9,8},{10,11... | collective-permute-start | bytes 786440 | tf_op jit(solution)/shard_map/ppermute | solution.py:21
  (399 shorter events, 158.6 us)
Async XLA Ops:
  7.2 182.6 %all-gather.2.cloned.1.call-start = ((), (), s32[]{:S(2)}) async-start(), calls=%async_computation.2 | async-start | bytes 4456448 | tf_op jit(solution)/shard_map/all_gather | solution.py:756
  9.3 37.3 %collective-permute-start = (bf16[256,1024]{1,0:T(8,128)(2,1)S(1)}, bf16[256,1024]{1,0:T(8,128)(2,1)S(1)}, u32[]{:S(2)}, u32[]{:S(2)}) collective-permute-start(bf16[256,1024]{1,0:T(8,128)(2,1)S(1)} %get-tuple-element.290), channel_id=1, source_target_pairs={{0,2},{2,0},{1,3},{3,1},{4,6},{6,4},{5,7},{7,5},{8,10},{10,8},{9,1... | collective-permute-start | bytes 1572872 | tf_op jit(solution)/shard_map/ppermute | solution.py:25
  20.1 7.2 %collective-permute-start.2 = (bf16[64,1920]{1,0:T(8,128)(2,1)S(1)}, bf16[64,1920]{1,0:T(8,128)(2,1)S(1)}, u32[]{:S(2)}, u32[]{:S(2)}) collective-permute-start(bf16[64,1920]{1,0:T(8,128)(2,1)S(1)} %bitcast.177), channel_id=1, source_target_pairs={{0,8},{8,16},{16,24},{24,0},{1,9},{9,17},{17,25},{25,1},{2,10},{10... | collective-permute-start | bytes 737288 | tf_op jit(solution)/shard_map/ppermute | solution.py:34
  21.4 20.8 %collective-permute-start.3 = (bf16[64,1920]{1,0:T(8,128)(2,1)S(1)}, bf16[64,1920]{1,0:T(8,128)(2,1)S(1)}, u32[]{:S(2)}, u32[]{:S(2)}) collective-permute-start(bf16[64,1920]{1,0:T(8,128)(2,1)S(1)} %bitcast.178), channel_id=1, source_target_pairs={{0,16},{8,24},{16,0},{24,8},{1,17},{9,25},{17,1},{25,9},{2,18},{10... | collective-permute-start | bytes 737288 | tf_op jit(solution)/shard_map/ppermute | solution.py:34
  22.4 22.3 %collective-permute-start.4 = (bf16[64,1920]{1,0:T(8,128)(2,1)S(1)}, bf16[64,1920]{1,0:T(8,128)(2,1)S(1)}, u32[]{:S(2)}, u32[]{:S(2)}) collective-permute-start(bf16[64,1920]{1,0:T(8,128)(2,1)S(1)} %bitcast.179), channel_id=1, source_target_pairs={{0,24},{8,0},{16,8},{24,16},{1,25},{9,1},{17,9},{25,17},{2,26},{10... | collective-permute-start | bytes 737288 | tf_op jit(solution)/shard_map/ppermute | solution.py:34
  45.3 12.4 %collective-permute-start.7 = (bf16[4,32,1920]{2,1,0:T(8,128)(2,1)S(1)}, bf16[4,32,1920]{2,1,0:T(8,128)(2,1)S(1)}, u32[]{:S(2)}, u32[]{:S(2)}) collective-permute-start(bf16[4,32,1920]{2,1,0:T(8,128)(2,1)S(1)} %get-tuple-element.142.refs_1_), channel_id=1, source_target_pairs={{0,4},{4,0},{1,5},{5,1},{2,6},{6,2},{3,7},{7,3},{8,12},{12,8},{9,1... | collective-permute-start | bytes 1474568 | tf_op jit(solution)/shard_map/ppermute | solution.py:29
  46.6 12.0 %collective-permute-start.6 = (bf16[4,32,1920]{2,1,0:T(8,128)(2,1)S(1)}, bf16[4,32,1920]{2,1,0:T(8,128)(2,1)S(1)}, u32[]{:S(2)}, u32[]{:S(2)}) collective-permute-start(bf16[4,32,1920]{2,1,0:T(8,128)(2,1)S(1)} %get-tuple-element.139.refs_0_), channel_id=1, source_target_pairs={{0,2},{2,0},{1,3},{3,1},{4,6},{6,4},{5,7},{7,5},{8,10},{10,8},{9,1... | collective-permute-start | bytes 1474568 | tf_op jit(solution)/shard_map/ppermute | solution.py:25
  46.9 8.4 %collective-permute-start.8 = (bf16[64,2560]{1,0:T(8,128)(2,1)}, bf16[64,2560]{1,0:T(8,128)(2,1)S(1)}, u32[]{:S(2)}, u32[]{:S(2)}) collective-permute-start(bf16[64,2560]{1,0:T(8,128)(2,1)} %bitcast.12.refs_0_), channel_id=1, source_target_pairs={{0,8},{8,16},{16,24},{24,0},{1,9},{9,17},{17,25},{25,1},{2,10},{10... | collective-permute-start | bytes 983048 | tf_op jit(solution)/shard_map/ppermute | solution.py:34
  59.7 23.8 %collective-permute-start.10 = (bf16[2,4,32,1920]{3,2,1,0:T(8,128)(2,1)}, bf16[2,4,32,1920]{3,2,1,0:T(8,128)(2,1)S(1)}, u32[]{:S(2)}, u32[]{:S(2)}) collective-permute-start(bf16[2,4,32,1920]{3,2,1,0:T(8,128)(2,1)} %pad_maximum_fusion.14), channel_id=1, source_target_pairs={{0,2},{2,0},{1,3},{3,1},{4,6},{6,4},{5,7},{7,5},{8,10},{10,8},{9,1... | collective-permute-start | bytes 2949128 | tf_op jit(solution)/shard_map/ppermute | solution.py:25
  61.0 23.5 %collective-permute-start.9 = (bf16[2,4,32,1920]{3,2,1,0:T(8,128)(2,1)}, bf16[2,4,32,1920]{3,2,1,0:T(8,128)(2,1)S(1)}, u32[]{:S(2)}, u32[]{:S(2)}) collective-permute-start(bf16[2,4,32,1920]{3,2,1,0:T(8,128)(2,1)} %pad_maximum_fusion.13), channel_id=1, source_target_pairs={{0,4},{4,0},{1,5},{5,1},{2,6},{6,2},{3,7},{7,3},{8,12},{12,8},{9,1... | collective-permute-start | bytes 2949128 | tf_op jit(solution)/shard_map/ppermute | solution.py:29
  61.4 27.2 %collective-permute-start.12 = (bf16[64,2560]{1,0:T(8,128)(2,1)}, bf16[64,2560]{1,0:T(8,128)(2,1)}, u32[]{:S(2)}, u32[]{:S(2)}) collective-permute-start(bf16[64,2560]{1,0:T(8,128)(2,1)} %bitcast.12.refs_0_), channel_id=1, source_target_pairs={{0,16},{8,24},{16,0},{24,8},{1,17},{9,25},{17,1},{25,9},{2,18},{10... | collective-permute-start | bytes 983048 | tf_op jit(solution)/shard_map/ppermute | solution.py:34
  61.4 27.5 %collective-permute-start.13 = (bf16[64,2560]{1,0:T(8,128)(2,1)}, bf16[64,2560]{1,0:T(8,128)(2,1)}, u32[]{:S(2)}, u32[]{:S(2)}) collective-permute-start(bf16[64,2560]{1,0:T(8,128)(2,1)} %bitcast.12.refs_0_), channel_id=1, source_target_pairs={{0,24},{8,0},{16,8},{24,16},{1,25},{9,1},{17,9},{25,17},{2,26},{10... | collective-permute-start | bytes 983048 | tf_op jit(solution)/shard_map/ppermute | solution.py:34
  62.6 342.8 %reduce-scatter.5.cloned.1.call-start = ((), (), s32[]{:S(2)}) async-start(), calls=%async_computation.4 | async-start | bytes 1310720 | tf_op jit(solution)/shard_map/reduce_scatter | solution.py:362
  64.9 32.2 %collective-permute-start.5 = (bf16[512,1024]{1,0:T(8,128)(2,1)}, bf16[512,1024]{1,0:T(8,128)(2,1)}, u32[]{:S(2)}, u32[]{:S(2)}) collective-permute-start(bf16[512,1024]{1,0:T(8,128)(2,1)} %pad_maximum_fusion.9), channel_id=1, source_target_pairs={{0,1},{1,0},{2,3},{3,2},{4,5},{5,4},{6,7},{7,6},{8,9},{9,8},{10,11... | collective-permute-start | bytes 3145736 | tf_op jit(solution)/shard_map/ppermute | solution.py:21
  90.7 19.7 %collective-permute-start.14 = (bf16[4,32,2560]{2,1,0:T(8,128)(2,1)S(1)}, bf16[4,32,2560]{2,1,0:T(8,128)(2,1)}, u32[]{:S(2)}, u32[]{:S(2)}) collective-permute-start(bf16[4,32,2560]{2,1,0:T(8,128)(2,1)S(1)} %get-tuple-element.152.refs_0_), channel_id=1, source_target_pairs={{0,2},{2,0},{1,3},{3,1},{4,6},{6,4},{5,7},{7,5},{8,10},{10,8},{9,1... | collective-permute-start | bytes 1966088 | tf_op jit(solution)/shard_map/ppermute | solution.py:25
  91.9 18.5 %collective-permute-start.15 = (bf16[4,32,2560]{2,1,0:T(8,128)(2,1)S(1)}, bf16[4,32,2560]{2,1,0:T(8,128)(2,1)}, u32[]{:S(2)}, u32[]{:S(2)}) collective-permute-start(bf16[4,32,2560]{2,1,0:T(8,128)(2,1)S(1)} %get-tuple-element.153.refs_1_), channel_id=1, source_target_pairs={{0,4},{4,0},{1,5},{5,1},{2,6},{6,2},{3,7},{7,3},{8,12},{12,8},{9,1... | collective-permute-start | bytes 1966088 | tf_op jit(solution)/shard_map/ppermute | solution.py:29
  94.2 5.5 %collective-permute-start.11 = (f32[16,128]{1,0:T(8,128)S(1)}, f32[16,128]{1,0:T(8,128)S(1)}, u32[]{:S(2)}, u32[]{:S(2)}) collective-permute-start(f32[16,128]{1,0:T(8,128)S(1)} %reshape.287), channel_id=1, source_target_pairs={{0,1},{1,0},{2,3},{3,2},{4,5},{5,4},{6,7},{7,6},{8,9},{9,8},{10,11... | collective-permute-start | bytes 24584 | tf_op jit(solution)/shard_map/ppermute | solution.py:21
  112.6 38.4 %collective-permute-start.16 = (bf16[2,4,32,2560]{3,2,1,0:T(8,128)(2,1)}, bf16[2,4,32,2560]{3,2,1,0:T(8,128)(2,1)}, u32[]{:S(2)}, u32[]{:S(2)}) collective-permute-start(bf16[2,4,32,2560]{3,2,1,0:T(8,128)(2,1)} %pad_maximum_fusion.6), channel_id=1, source_target_pairs={{0,4},{4,0},{1,5},{5,1},{2,6},{6,2},{3,7},{7,3},{8,12},{12,8},{9,1... | collective-permute-start | bytes 3932168 | tf_op jit(solution)/shard_map/ppermute | solution.py:29
  116.4 42.3 %collective-permute-start.18 = (bf16[2,4,32,2560]{3,2,1,0:T(8,128)(2,1)}, bf16[2,4,32,2560]{3,2,1,0:T(8,128)(2,1)}, u32[]{:S(2)}, u32[]{:S(2)}) collective-permute-start(bf16[2,4,32,2560]{3,2,1,0:T(8,128)(2,1)} %pad_maximum_fusion.7), channel_id=1, source_target_pairs={{0,2},{2,0},{1,3},{3,1},{4,6},{6,4},{5,7},{7,5},{8,10},{10,8},{9,1... | collective-permute-start | bytes 3932168 | tf_op jit(solution)/shard_map/ppermute | solution.py:25
  161.1 7.6 %collective-permute-start.19 = (bf16[16,64,512]{2,1,0:T(8,128)(2,1)S(1)}, bf16[16,64,512]{2,1,0:T(8,128)(2,1)S(1)}, u32[]{:S(2)}, u32[]{:S(2)}) collective-permute-start(bf16[16,64,512]{2,1,0:T(8,128)(2,1)S(1)} %bitcast.171), channel_id=1, source_target_pairs={{0,1},{1,0},{2,3},{3,2},{4,5},{5,4},{6,7},{7,6},{8,9},{9,8},{10,11... | collective-permute-start | bytes 3145736 | tf_op jit(solution)/shard_map/ppermute | solution.py:21
  175.1 14.6 %collective-permute-start.21 = (bf16[256,1152]{1,0:T(8,128)(2,1)S(1)}, bf16[256,1152]{1,0:T(8,128)(2,1)}, u32[]{:S(2)}, u32[]{:S(2)}) collective-permute-start(bf16[256,1152]{1,0:T(8,128)(2,1)S(1)} %copy-done.72), channel_id=1, source_target_pairs={{0,2},{2,0},{1,3},{3,1},{4,6},{6,4},{5,7},{7,5},{8,10},{10,8},{9,1... | collective-permute-start | bytes 1769480 | tf_op jit(solution)/shard_map/ppermute | solution.py:25
  237.1 13.5 %collective-permute-start.24 = (bf16[512,1024]{1,0:T(8,128)(2,1)}, bf16[512,1024]{1,0:T(8,128)(2,1)}, u32[]{:S(2)}, u32[]{:S(2)}) collective-permute-start(bf16[512,1024]{1,0:T(8,128)(2,1)} %slice.201), channel_id=1, source_target_pairs={{0,1},{1,0},{2,3},{3,2},{4,5},{5,4},{6,7},{7,6},{8,9},{9,8},{10,11... | collective-permute-start | bytes 3145736 | tf_op jit(solution)/shard_map/ppermute | solution.py:21
  237.1 24.4 %collective-permute-start.25 = (bf16[4,2,64,1024]{3,2,1,0:T(8,128)(2,1)}, bf16[4,2,64,1024]{3,2,1,0:T(8,128)(2,1)S(1)}, u32[]{:S(2)}, u32[]{:S(2)}) collective-permute-start(bf16[4,2,64,1024]{3,2,1,0:T(8,128)(2,1)} %get-tuple-element.175), channel_id=1, source_target_pairs={{0,2},{2,0},{1,3},{3,1},{4,6},{6,4},{5,7},{7,5},{8,10},{10,8},{9,1... | collective-permute-start | bytes 3145736 | tf_op jit(solution)/shard_map/ppermute | solution.py:25
  238.5 24.1 %collective-permute-start.26 = (bf16[4,2,64,1024]{3,2,1,0:T(8,128)(2,1)}, bf16[4,2,64,1024]{3,2,1,0:T(8,128)(2,1)S(1)}, u32[]{:S(2)}, u32[]{:S(2)}) collective-permute-start(bf16[4,2,64,1024]{3,2,1,0:T(8,128)(2,1)} %get-tuple-element.176), channel_id=1, source_target_pairs={{0,4},{4,0},{1,5},{5,1},{2,6},{6,2},{3,7},{7,3},{8,12},{12,8},{9,1... | collective-permute-start | bytes 3145736 | tf_op jit(solution)/shard_map/ppermute | solution.py:29
  249.1 66.9 %collective-permute-start.31 = (bf16[4,2,32,2048]{3,2,1,0:T(8,128)(2,1)}, bf16[4,2,32,2048]{3,2,1,0:T(8,128)(2,1)}, u32[]{:S(2)}, u32[]{:S(2)}) collective-permute-start(bf16[4,2,32,2048]{3,2,1,0:T(8,128)(2,1)} %get-tuple-element.195), channel_id=1, source_target_pairs={{0,4},{4,0},{1,5},{5,1},{2,6},{6,2},{3,7},{7,3},{8,12},{12,8},{9,1... | collective-permute-start | bytes 3145736 | tf_op jit(solution)/shard_map/ppermute | solution.py:29
  268.7 47.3 %collective-permute-start.30 = (bf16[4,2,32,2048]{3,2,1,0:T(8,128)(2,1)}, bf16[4,2,32,2048]{3,2,1,0:T(8,128)(2,1)}, u32[]{:S(2)}, u32[]{:S(2)}) collective-permute-start(bf16[4,2,32,2048]{3,2,1,0:T(8,128)(2,1)} %get-tuple-element.194), channel_id=1, source_target_pairs={{0,2},{2,0},{1,3},{3,1},{4,6},{6,4},{5,7},{7,5},{8,10},{10,8},{9,1... | collective-permute-start | bytes 3145736 | tf_op jit(solution)/shard_map/ppermute | solution.py:25
  276.4 7.4 %collective-permute-start.27 = (bf16[512,512]{1,0:T(8,128)(2,1)}, bf16[512,512]{1,0:T(8,128)(2,1)}, u32[]{:S(2)}, u32[]{:S(2)}) collective-permute-start(bf16[512,512]{1,0:T(8,128)(2,1)} %get-tuple-element.182), channel_id=1, source_target_pairs={{0,1},{1,0},{2,3},{3,2},{4,5},{5,4},{6,7},{7,6},{8,9},{9,8},{10,11... | collective-permute-start | bytes 1572872 | tf_op jit(solution)/shard_map/ppermute | solution.py:21
  277.8 21.2 %collective-permute-start.28 = (bf16[4,64,1024]{2,1,0:T(8,128)(2,1)}, bf16[4,64,1024]{2,1,0:T(8,128)(2,1)S(1)}, u32[]{:S(2)}, u32[]{:S(2)}) collective-permute-start(bf16[4,64,1024]{2,1,0:T(8,128)(2,1)} %get-tuple-element.186), channel_id=1, source_target_pairs={{0,4},{4,0},{1,5},{5,1},{2,6},{6,2},{3,7},{7,3},{8,12},{12,8},{9,1... | collective-permute-start | bytes 1572872 | tf_op jit(solution)/shard_map/ppermute | solution.py:29
  277.9 25.5 %collective-permute-start.29 = (bf16[4,64,1024]{2,1,0:T(8,128)(2,1)S(1)}, bf16[4,64,1024]{2,1,0:T(8,128)(2,1)S(1)}, u32[]{:S(2)}, u32[]{:S(2)}) collective-permute-start(bf16[4,64,1024]{2,1,0:T(8,128)(2,1)S(1)} %copy-done.48), channel_id=1, source_target_pairs={{0,2},{2,0},{1,3},{3,1},{4,6},{6,4},{5,7},{7,5},{8,10},{10,8},{9,1... | collective-permute-start | bytes 1572872 | tf_op jit(solution)/shard_map/ppermute | solution.py:25
  305.1 26.5 %collective-permute-start.32 = (bf16[16,32,1024]{2,1,0:T(8,128)(2,1)}, bf16[16,32,1024]{2,1,0:T(8,128)(2,1)}, u32[]{:S(2)}, u32[]{:S(2)}) collective-permute-start(bf16[16,32,1024]{2,1,0:T(8,128)(2,1)} %get-tuple-element.203), channel_id=1, source_target_pairs={{0,1},{1,0},{2,3},{3,2},{4,5},{5,4},{6,7},{7,6},{8,9},{9,8},{10,11... | collective-permute-start | bytes 3145736 | tf_op jit(solution)/shard_map/ppermute | solution.py:21
  326.1 18.1 %collective-permute-start.34 = (bf16[4,32,2048]{2,1,0:T(8,128)(2,1)S(1)}, bf16[4,32,2048]{2,1,0:T(8,128)(2,1)S(1)}, u32[]{:S(2)}, u32[]{:S(2)}) collective-permute-start(bf16[4,32,2048]{2,1,0:T(8,128)(2,1)S(1)} %get-tuple-element.207), channel_id=1, source_target_pairs={{0,4},{4,0},{1,5},{5,1},{2,6},{6,2},{3,7},{7,3},{8,12},{12,8},{9,1... | collective-permute-start | bytes 1572872 | tf_op jit(solution)/shard_map/ppermute | solution.py:29
  334.3 13.6 %collective-permute-start.35 = (bf16[4,32,2048]{2,1,0:T(8,128)(2,1)S(1)}, bf16[4,32,2048]{2,1,0:T(8,128)(2,1)S(1)}, u32[]{:S(2)}, u32[]{:S(2)}) collective-permute-start(bf16[4,32,2048]{2,1,0:T(8,128)(2,1)S(1)} %get-tuple-element.208), channel_id=1, source_target_pairs={{0,2},{2,0},{1,3},{3,1},{4,6},{6,4},{5,7},{7,5},{8,10},{10,8},{9,1... | collective-permute-start | bytes 1572872 | tf_op jit(solution)/shard_map/ppermute | solution.py:25
  348.7 7.5 %collective-permute-start.36 = (bf16[512,1024]{1,0:T(8,128)(2,1)}, bf16[512,1024]{1,0:T(8,128)(2,1)}, u32[]{:S(2)}, u32[]{:S(2)}) collective-permute-start(bf16[512,1024]{1,0:T(8,128)(2,1)} %slice.200), channel_id=1, source_target_pairs={{0,1},{1,0},{2,3},{3,2},{4,5},{5,4},{6,7},{7,6},{8,9},{9,8},{10,11... | collective-permute-start | bytes 3145736 | tf_op jit(solution)/shard_map/ppermute | solution.py:21
  350.3 77.4 %reduce-scatter.3.cloned.1.call-start = ((), (), s32[]{:S(2)}) async-start(), calls=%async_computation.3 | async-start | bytes 1310720 | tf_op jit(solution)/shard_map/reduce_scatter | solution.py:362
  350.5 25.2 %collective-permute-start.33 = (bf16[4,2,32,2048]{3,2,1,0:T(8,128)(2,1)}, bf16[4,2,32,2048]{3,2,1,0:T(8,128)(2,1)S(1)}, u32[]{:S(2)}, u32[]{:S(2)}) collective-permute-start(bf16[4,2,32,2048]{3,2,1,0:T(8,128)(2,1)} %get-tuple-element.205), channel_id=1, source_target_pairs={{0,2},{2,0},{1,3},{3,1},{4,6},{6,4},{5,7},{7,5},{8,10},{10,8},{9,1... | collective-permute-start | bytes 3145736 | tf_op jit(solution)/shard_map/ppermute | solution.py:25
  352.0 24.8 %collective-permute-start.37 = (bf16[4,2,32,2048]{3,2,1,0:T(8,128)(2,1)}, bf16[4,2,32,2048]{3,2,1,0:T(8,128)(2,1)S(1)}, u32[]{:S(2)}, u32[]{:S(2)}) collective-permute-start(bf16[4,2,32,2048]{3,2,1,0:T(8,128)(2,1)} %copy-done.44), channel_id=1, source_target_pairs={{0,4},{4,0},{1,5},{5,1},{2,6},{6,2},{3,7},{7,3},{8,12},{12,8},{9,1... | collective-permute-start | bytes 3145736 | tf_op jit(solution)/shard_map/ppermute | solution.py:29
  360.3 19.1 %collective-permute-start.38 = (f32[41,128]{1,0:T(8,128)S(1)}, f32[41,128]{1,0:T(8,128)S(1)}, u32[]{:S(2)}, u32[]{:S(2)}) collective-permute-start(f32[41,128]{1,0:T(8,128)S(1)} %bitcast.197), channel_id=1, source_target_pairs={{0,1},{1,0},{2,3},{3,2},{4,5},{5,4},{6,7},{7,6},{8,9},{9,8},{10,11... | collective-permute-start | bytes 62984 | tf_op jit(solution)/shard_map/ppermute | solution.py:21
  379.6 6.4 %collective-permute-start.47 = (f32[64,128]{1,0:T(8,128)S(1)}, f32[64,128]{1,0:T(8,128)S(1)}, u32[]{:S(2)}, u32[]{:S(2)}) collective-permute-start(f32[64,128]{1,0:T(8,128)S(1)} %get-tuple-element.267), channel_id=1, source_target_pairs={{0,8},{8,16},{16,24},{24,0},{1,9},{9,17},{17,25},{25,1},{2,10},{10... | collective-permute-start | bytes 98312 | tf_op jit(solution)/shard_map/ppermute | solution.py:34
  379.7 6.5 %collective-permute-start.48 = (f32[64,128]{1,0:T(8,128)S(1)}, f32[64,128]{1,0:T(8,128)S(1)}, u32[]{:S(2)}, u32[]{:S(2)}) collective-permute-start(f32[64,128]{1,0:T(8,128)S(1)} %get-tuple-element.267), channel_id=1, source_target_pairs={{0,16},{8,24},{16,0},{24,8},{1,17},{9,25},{17,1},{25,9},{2,18},{10... | collective-permute-start | bytes 98312 | tf_op jit(solution)/shard_map/ppermute | solution.py:34
  388.8 13.6 %collective-permute-start.40 = (bf16[4,32,2048]{2,1,0:T(8,128)(2,1)}, bf16[4,32,2048]{2,1,0:T(8,128)(2,1)S(1)}, u32[]{:S(2)}, u32[]{:S(2)}) collective-permute-start(bf16[4,32,2048]{2,1,0:T(8,128)(2,1)} %copy-done.46), channel_id=1, source_target_pairs={{0,2},{2,0},{1,3},{3,1},{4,6},{6,4},{5,7},{7,5},{8,10},{10,8},{9,1... | collective-permute-start | bytes 1572872 | tf_op jit(solution)/shard_map/ppermute | solution.py:25
  390.3 12.2 %collective-permute-start.39 = (bf16[4,32,2048]{2,1,0:T(8,128)(2,1)}, bf16[4,32,2048]{2,1,0:T(8,128)(2,1)S(1)}, u32[]{:S(2)}, u32[]{:S(2)}) collective-permute-start(bf16[4,32,2048]{2,1,0:T(8,128)(2,1)} %copy-done.45), channel_id=1, source_target_pairs={{0,4},{4,0},{1,5},{5,1},{2,6},{6,2},{3,7},{7,3},{8,12},{12,8},{9,1... | collective-permute-start | bytes 1572872 | tf_op jit(solution)/shard_map/ppermute | solution.py:29
  392.3 14.9 %collective-permute-start.51 = (f32[4,2,64,128]{3,2,1,0:T(8,128)S(1)}, f32[4,2,64,128]{3,2,1,0:T(8,128)S(1)}, u32[]{:S(2)}, u32[]{:S(2)}) collective-permute-start(f32[4,2,64,128]{3,2,1,0:T(8,128)S(1)} %pad_maximum_fusion.19), channel_id=1, source_target_pairs={{0,4},{4,0},{1,5},{5,1},{2,6},{6,2},{3,7},{7,3},{8,12},{12,8},{9,1... | collective-permute-start | bytes 786440 | tf_op jit(solution)/shard_map/ppermute | solution.py:29
  403.3 10.5 %collective-permute-start.44 = (bf16[256,1024]{1,0:T(8,128)(2,1)}, bf16[256,1024]{1,0:T(8,128)(2,1)}, u32[]{:S(2)}, u32[]{:S(2)}) collective-permute-start(bf16[256,1024]{1,0:T(8,128)(2,1)} %slice.155), channel_id=1, source_target_pairs={{0,2},{2,0},{1,3},{3,1},{4,6},{6,4},{5,7},{7,5},{8,10},{10,8},{9,1... | collective-permute-start | bytes 1572872 | tf_op jit(solution)/shard_map/ppermute | solution.py:25
  407.2 17.8 %collective-permute-start.45 = (bf16[256,1024]{1,0:T(8,128)(2,1)}, bf16[256,1024]{1,0:T(8,128)(2,1)}, u32[]{:S(2)}, u32[]{:S(2)}) collective-permute-start(bf16[256,1024]{1,0:T(8,128)(2,1)} %slice.203), channel_id=1, source_target_pairs={{0,2},{2,0},{1,3},{3,1},{4,6},{6,4},{5,7},{7,5},{8,10},{10,8},{9,1... | collective-permute-start | bytes 1572872 | tf_op jit(solution)/shard_map/ppermute | solution.py:25
  411.0 28.3 %collective-permute-start.41 = (bf16[64,2048]{1,0:T(8,128)(2,1)S(1)}, bf16[64,2048]{1,0:T(8,128)(2,1)}, u32[]{:S(2)}, u32[]{:S(2)}) collective-permute-start(bf16[64,2048]{1,0:T(8,128)(2,1)S(1)} %get-tuple-element.226), channel_id=1, source_target_pairs={{0,8},{8,16},{16,24},{24,0},{1,9},{9,17},{17,25},{25,1},{2,10},{10... | collective-permute-start | bytes 786440 | tf_op jit(solution)/shard_map/ppermute | solution.py:34
  411.1 28.2 %collective-permute-start.42 = (bf16[64,2048]{1,0:T(8,128)(2,1)S(1)}, bf16[64,2048]{1,0:T(8,128)(2,1)}, u32[]{:S(2)}, u32[]{:S(2)}) collective-permute-start(bf16[64,2048]{1,0:T(8,128)(2,1)S(1)} %get-tuple-element.227), channel_id=1, source_target_pairs={{0,16},{8,24},{16,0},{24,8},{1,17},{9,25},{17,1},{25,9},{2,18},{10... | collective-permute-start | bytes 786440 | tf_op jit(solution)/shard_map/ppermute | solution.py:34
  413.8 25.5 %collective-permute-start.43 = (bf16[64,2048]{1,0:T(8,128)(2,1)S(1)}, bf16[64,2048]{1,0:T(8,128)(2,1)}, u32[]{:S(2)}, u32[]{:S(2)}) collective-permute-start(bf16[64,2048]{1,0:T(8,128)(2,1)S(1)} %get-tuple-element.228), channel_id=1, source_target_pairs={{0,24},{8,0},{16,8},{24,16},{1,25},{9,1},{17,9},{25,17},{2,26},{10... | collective-permute-start | bytes 786440 | tf_op jit(solution)/shard_map/ppermute | solution.py:34
  428.9 8.6 %collective-permute-start.46 = (f32[32,16,128]{2,1,0:T(8,128)S(1)}, f32[32,16,128]{2,1,0:T(8,128)S(1)}, u32[]{:S(2)}, u32[]{:S(2)}) collective-permute-start(f32[32,16,128]{2,1,0:T(8,128)S(1)} %dynamic-slice_bitcast_fusion.4), channel_id=1, source_target_pairs={{0,1},{1,0},{2,3},{3,2},{4,5},{5,4},{6,7},{7,6},{8,9},{9,8},{10,11... | collective-permute-start | bytes 786440 | tf_op jit(solution)/shard_map/ppermute | solution.py:21
  (89 other events, 440.2 us)
Sparse Core Ops, SparseCore 0:
  62.7 104.6 all-gather.1
  350.4 27.7 reduce-scatter.4
  380.6 27.2 reduce-scatter.2

commit v4 on v3

--- a/solution.py
+++ b/solution.py
@@ -880,15 +880,17 @@
     down_sum.near()
     inner_grad = (dot(down_in_all, down_full, 1, 1) * slope).astype(b16)
     second_part = dot(inner_grad, up_full, 1, 1)
-    second_send, second_all = tie(second_part[mine:].astype(b16), second_all)
+    second_send, second_all, *down_sum.got = tie(
+        second_part[mine:].astype(b16), second_all, *down_sum.got
+    )
     second_got = swap_core(second_send)
+    down_sum.add_near()
+    second_all, down_sum.got[0] = tie(second_all, down_sum.got[0])
+    down_sum.far()
     up_term = dot(second_all, inner_grad, 0, 0).astype(b16)
     up_sum = Scatter(up_term.reshape(chips, -1, ff), where, tiled)
-    second_got, up_sum.got[0], *down_sum.got = tie(second_got, up_sum.got[0], *down_sum.got)
+    second_got, up_sum.got[0] = tie(second_got, up_sum.got[0])
     up_sum.near()
-    down_sum.add_near()
-    second_got, down_sum.got[0] = tie(second_got, down_sum.got[0])
-    down_sum.far()
     second_grad = second_part[:mine] + second_got.astype(f32)
     middle_grad = result_grad + norm_back(second_grad * gain, n2, rate2)
     branch = middle_grad.astype(b16)

time: 458 us -> 453 us (0.989)
    ppermute x15, starting transfers between devices: 18 us -> 12.9 us  [swap_x(): return lax.ppermute(v, 'x', [(0, 1), (1, 0)])]
    unnamed x173 -> x177, local copies, waits for them, and re-layouts: 27.6 us -> 29.8 us
  transfers between devices with their start and end apart: 56 -> 56, of which waited for: 27 -> 28; matrix products, arithmetic and copies ran while one was open for 22% -> 24% of each run, Pallas kernels for 18% -> 18%
where the time goes in v4:
time: 453 us; the launch traced here: 447 us
  waiting for transfers between devices  124 us (27%)
  Pallas kernels  81.5 us (18%)
  other arithmetic  60.5 us (13%)
  starting transfers between devices  59.1 us (13%)
  matrix products  53.2 us (12%)
  local copies, waits for them, and re-layouts  50 us (11%)
  between operations  18.6 us (4%)
    ppermute x15, waiting for transfers between devices, swap_x(): return lax.ppermute(v, 'x', [(0, 1), (1, 0)])  73.7 us
    dot_general x11, matrix products, dot(): lax.dot_general(a, b, (((da,), (db,)), ((), ())), preferred_element_type=...  53.2 us
    ppermute x12, waiting for transfers between devices, shift_z(): return lax.ppermute(v, 'z', [(i, (i + k) % depth) for i in range(depth)])  31.5 us
    unnamed x177, local copies, waits for them, and re-layouts  29.8 us
    pallas_call x4, Pallas kernels, attend_back(): pl.pallas_call(attend_back_kernel, grid=(pairs,), in_specs=[pl.BlockSpec(...  26.8 us
    ppermute x15, starting transfers between devices, swap_core(): return lax.ppermute(v, 'core', [(0, 1), (1, 0)])  22.8 us
    pallas_call x2, Pallas kernels, attend(): pl.pallas_call(attend_kernel, grid=(pairs,), in_specs=[pl.BlockSpec((toke...  20.9 us
    ppermute x11, waiting for transfers between devices, swap_y(): return lax.ppermute(v, 'y', [(0, 1), (1, 0)])  16 us
  transfers between devices with their start and end apart: 56, of which 28 were waited for; matrix products, arithmetic and copies ran while one was open for 24% of the time, Pallas kernels for 18%

profile of v4, /device:TPU:9, one launch (start us, length us, event | category | flops | bytes accessed | tf_op | source)
XLA Modules:
  0.0 447.0 jit_solution(898277368581447615)
XLA Ops:
  23.9 3.4 collective-permute-done.2.refs_1_
  27.3 14.9 %collective-permute-done.3.refs_2_ = bf16[64,1920]{1,0:T(8,128)(2,1)S(1)} collective-permute-done((bf16[64,1920]{1,0:T(8,128)(2,1)S(1)}, bf16[64,1920]{1,0:T(8,128)(2,1)S(1)}, u32[]{:S(2)}, u32[]{:S(2)}) %collective-permute-start.3) | collective-permute-done | bytes 245792 | tf_op jit(solution)/shard_map/ppermute | solution.py:34
  42.2 2.5 collective-permute-done.4.refs_3_
  46.9 8.4 %collective-permute-done.8.refs_1_ = bf16[64,2560]{1,0:T(8,128)(2,1)S(1)} collective-permute-done((bf16[64,2560]{1,0:T(8,128)(2,1)}, bf16[64,2560]{1,0:T(8,128)(2,1)S(1)}, u32[]{:S(2)}, u32[]{:S(2)}) %collective-permute-start.8) | collective-permute-done | bytes 327712 | tf_op jit(solution)/shard_map/ppermute | solution.py:34
  55.3 2.4 collective-permute-done.7.refs_3_
  64.9 2.7 collective-permute-start.5
  67.6 15.9 %collective-permute-done.10.refs_5_ = bf16[2,4,32,1920]{3,2,1,0:T(8,128)(2,1)S(1)} collective-permute-done((bf16[2,4,32,1920]{3,2,1,0:T(8,128)(2,1)}, bf16[2,4,32,1920]{3,2,1,0:T(8,128)(2,1)S(1)}, u32[]{:S(2)}, u32[]{:S(2)}) %collective-permute-start.10) | collective-permute-done | bytes 983072 | tf_op jit(solution)/shard_map/ppermute | solution.py:25
  94.2 2.9 collective-permute-start.11
  99.8 8.6 %project.1 = (bf16[1024,1024]{1,0:T(8,128)(2,1)S(1)}, f32[1024,1536]{1,0:T(8,128)}) custom-call(bf16[1024,1024]{1,0:T(8,128)(2,1)S(1)} %pad_maximum_fusion.2.source, f32[1,1024]{1,0:T(1,128)S(1)} %get-tuple-element.302.scale, f32[1,1024]{1,0:T(1,128)S(1)} %get-tuple-element.301.shift, bf16[1024,1536]{1,0:T(8,128)(2,1)} %bitcast.161), custom_call_target="tpu_custom_call" | custom-call | flops 1 | bytes 1 | tf_op jit(solution)/shard_map/project/pallas_call | solution.py:433
  110.4 2.3 pad_maximum_fusion.6
  114.1 2.3 pad_maximum_fusion.7
  120.0 2.3 fusion.26
  122.3 10.3 %attend.2 = (bf16[1024,768]{1,0:T(8,128)(2,1)S(1)}, bf16[1024,256]{1,0:T(8,128)(2,1)S(1)}, f32[2,2,1024]{2,1,0:T(2,128)S(1)}) custom-call(f32[1024,1536]{1,0:T(8,128)} %get-tuple-element.155.project_in, f32[1024,128]{1,0:T(8,128)S(1)} %copy.122.cos_in, f32[1024,128]{1,0:T(8,128)S(1)} %copy.123.sin_in), custom_call_target="tpu_custom_call" | custom-call | flops 1 | bytes 1 | tf_op jit(solution)/shard_map/attend/pallas_call | solution.py:530
  133.8 10.5 %attend.3 = (bf16[1024,768]{1,0:T(8,128)(2,1)S(1)}, bf16[1024,256]{1,0:T(8,128)(2,1)S(1)}, f32[2,2,1024]{2,1,0:T(2,128)S(1)}) custom-call(f32[1024,1536]{1,0:T(8,128)} %get-tuple-element.155.project_in, f32[1024,128]{1,0:T(8,128)S(1)} %copy.122.cos_in, f32[1024,128]{1,0:T(8,128)S(1)} %copy.123.sin_in, bf16[1024,256]{1,0:T(8,128)(2,1)S(1)} %get-tuple-element.160.refs_0_), custom_call_target="tpu_custom_call" | custom-call | flops 1 | bytes 1 | tf_op jit(solution)/shard_map/attend/pallas_call | solution.py:530
  144.3 6.6 %collective-permute-done.16.refs_4_ = bf16[2,4,32,2560]{3,2,1,0:T(8,128)(2,1)} collective-permute-done((bf16[2,4,32,2560]{3,2,1,0:T(8,128)(2,1)}, bf16[2,4,32,2560]{3,2,1,0:T(8,128)(2,1)}, u32[]{:S(2)}, u32[]{:S(2)}) %collective-permute-start.16) | collective-permute-done | bytes 1310752 | tf_op jit(solution)/shard_map/ppermute | solution.py:29
  151.0 7.7 %collective-permute-done.18.refs_5_ = bf16[2,4,32,2560]{3,2,1,0:T(8,128)(2,1)} collective-permute-done((bf16[2,4,32,2560]{3,2,1,0:T(8,128)(2,1)}, bf16[2,4,32,2560]{3,2,1,0:T(8,128)(2,1)}, u32[]{:S(2)}, u32[]{:S(2)}) %collective-permute-start.18) | collective-permute-done | bytes 1310752 | tf_op jit(solution)/shard_map/ppermute | solution.py:25
  158.7 2.5 move.13
  161.2 5.0 %collective-permute-start.19 = (bf16[16,64,512]{2,1,0:T(8,128)(2,1)S(1)}, bf16[16,64,512]{2,1,0:T(8,128)(2,1)S(1)}, u32[]{:S(2)}, u32[]{:S(2)}) collective-permute-start(bf16[16,64,512]{2,1,0:T(8,128)(2,1)S(1)} %bitcast.171), channel_id=1, source_target_pairs={{0,1},{1,0},{2,3},{3,2},{4,5},{5,4},{6,7},{7,6},{8,9},{9,8},{10,11... | collective-permute-start | bytes 3145736 | tf_op jit(solution)/shard_map/ppermute | solution.py:21
  170.2 2.6 fusion.49
  176.7 8.8 %multiply_convert_fusion = (bf16[1024,2048]{1,0:T(8,128)(2,1)}, f32[1024,2048]{1,0:T(8,128)}) fusion(f32[2048]{0:T(1024)S(1)} %bitcast.202, bf16[1024,2048]{1,0:T(8,128)(2,1)S(1)} %bitcast.183, bf16[512,1024]{1,0:T(8,128)(2,1)S(1)} %collective-permute-done.20, bf16[512,1024]{1,0:T(8,128)(2,1)S(1)} %add_convert_fusion.1), kind=kOutput, calls=%fused_computation.8 | convolution fusion | flops 4311744512 | bytes 18882560 | tf_op jit(solution)/shard_map/dot_general | solution.py:468
  185.4 4.4 collective-permute-done.21
  189.8 7.5 %fusion.50 = f32[1024,1024]{1,0:T(8,128)S(1)} fusion(bf16[1024,2048]{1,0:T(8,128)(2,1)} %get-tuple-element.169, bf16[2048,1024]{1,0:T(8,128)(2,1)} %all-gather.2.cloned.1.call-done), kind=kOutput, calls=%fused_computation.183 | convolution fusion | flops 4294967296 | bytes 12582912 | tf_op jit(solution)/shard_map/dot_general | solution.py:468
  204.8 4.9 %fusion.17 = (f32[]{:T(128)}, f32[512,1024]{1,0:T(8,128)S(1)}, bf16[512,1024]{1,0:T(8,128)(2,1)}) fusion(f32[512]{0:T(512)S(1)} %get-tuple-element.262, bf16[256,1152]{1,0:T(8,128)(2,1)} %collective-permute-done.21, bf16[256,1152]{1,0:T(8,128)(2,1)S(1)} %copy-done.64, f32[512,1024]{1,0:T(8,128)} %copy-done.49, f32[1024]{0:T(1024)S(1)} %add.248, ...), kind=kLoop, calls=%fused_computation.30 | loop fusion | flops 6815743 | bytes 9574404 | tf_op jit(solution)/shard_map/reduce_sum | solution.py:870
  213.3 5.0 %convolution_convert_fusion.2 = bf16[2048,1024]{1,0:T(8,128)(2,1)S(1)} fusion(bf16[1024,2048]{1,0:T(8,128)(2,1)S(1)} %copy-done.80, bf16[512,1024]{1,0:T(8,128)(2,1)S(1)} %collective-permute-done.23, bf16[512,1024]{1,0:T(8,128)(2,1)S(1)} %get-tuple-element.271), kind=kOutput, calls=%fused_computation.13 | convolution fusion | flops 4301258752 | bytes 10485760 | tf_op jit(solution)/shard_map/dot_general | solution.py:468
  222.5 8.1 %convert_reduce_fusion = (f32[2048]{0:T(1024)S(1)}, bf16[1024,2048]{1,0:T(8,128)(2,1)S(1)}) fusion(f32[1024,2048]{1,0:T(8,128)S(1)} %bitcast.215, f32[2048]{0:T(1024)S(1)} %bitcast.203, bf16[1024,1024]{1,0:T(8,128)(2,1)S(1)} %pad_maximum_fusion.4, bf16[2048,1024]{1,0:T(8,128)(2,1)S(1)} %copy-done.77), kind=kOutput, calls=%fused_computation.7 | convolution fusion | flops 4322228224 | bytes 18890752 | tf_op jit(solution)/shard_map/dot_general | solution.py:468
  230.5 4.5 %fusion.51 = f32[1024,1024]{1,0:T(8,128)S(1)} fusion(bf16[1024,2048]{1,0:T(8,128)(2,1)S(1)} %get-tuple-element.313, bf16[1024,2048]{1,0:T(8,128)(2,1)S(1)} %bitcast.184), kind=kOutput, calls=%fused_computation.184 | convolution fusion | flops 4294967296 | bytes 12582912 | tf_op jit(solution)/shard_map/dot_general | solution.py:468
  236.4 8.9 %collective-permute-done.24.top = bf16[4,2,64,1024]{3,2,1,0:T(8,128)(2,1)S(1)} collective-permute-done((bf16[4,2,64,1024]{3,2,1,0:T(8,128)(2,1)S(1)}, bf16[4,2,64,1024]{3,2,1,0:T(8,128)(2,1)S(1)}, u32[]{:S(2)}, u32[]{:S(2)}) %collective-permute-start.24) | collective-permute-done | bytes 1048608 | tf_op jit(solution)/shard_map/ppermute | solution.py:25
  253.3 4.9 %convolution_convert_fusion.1 = bf16[1024,2048]{1,0:T(8,128)(2,1)S(1)} fusion(bf16[1024,1024]{1,0:T(8,128)(2,1)S(1)} %copy-done.70, bf16[1024,2048]{1,0:T(8,128)(2,1)S(1)} %copy-done.79), kind=kOutput, calls=%fused_computation.12 | convolution fusion | flops 4297064448 | bytes 10485760 | tf_op jit(solution)/shard_map/dot_general | solution.py:468
  261.4 2.4 multiply_reduce_fusion
  264.0 3.7 fusion.44
  273.1 2.9 convolution_convert_fusion.3
  279.1 6.6 %attend_back.4.refs_0_ = bf16[1024,384]{1,0:T(8,128)(2,1)S(1)} custom-call(bf16[1024,768]{1,0:T(8,128)(2,1)S(1)} %copy-done.9, bf16[1024,512]{1,0:T(8,128)(2,1)S(1)} %pad_maximum_fusion.10.grad_in, f32[2,2,1024]{2,1,0:T(2,128)S(1)} %get-tuple-element.185.log_in, f32[1024,128]{1,0:T(8,128)S(1)} %copy.122.cos_in, f32[1024,128]{1,0:T(8,128)S(1)} %copy.123.sin_in), custom_call_target="tpu_custom_call" | custom-call | flops 1 | bytes 1 | tf_op jit(solution)/shard_map/attend_back/pallas_call | solution.py:596
  285.8 6.8 %attend_back.5.refs_0_ = bf16[1024,384]{1,0:T(8,128)(2,1)S(1)} custom-call(bf16[1024,768]{1,0:T(8,128)(2,1)S(1)} %copy-done.9, bf16[1024,512]{1,0:T(8,128)(2,1)S(1)} %pad_maximum_fusion.10.grad_in, f32[2,2,1024]{2,1,0:T(2,128)S(1)} %get-tuple-element.185.log_in, f32[1024,128]{1,0:T(8,128)S(1)} %copy.122.cos_in, f32[1024,128]{1,0:T(8,128)S(1)} %copy.123.sin_in, ...), custom_call_target="tpu_custom_call" | custom-call | flops 1 | bytes 1 | tf_op jit(solution)/shard_map/attend_back/pallas_call | solution.py:596
  292.6 4.7 %collective-permute-done.28.top_got = bf16[4,64,1024]{2,1,0:T(8,128)(2,1)S(1)} collective-permute-done((bf16[4,64,1024]{2,1,0:T(8,128)(2,1)}, bf16[4,64,1024]{2,1,0:T(8,128)(2,1)S(1)}, u32[]{:S(2)}, u32[]{:S(2)}) %collective-permute-start.28) | collective-permute-done | bytes 524320 | tf_op jit(solution)/shard_map/ppermute | solution.py:29
  297.3 2.8 collective-permute-done.29.low_got
  304.1 6.6 %attend_back.6.refs_0_ = bf16[1024,384]{1,0:T(8,128)(2,1)S(1)} custom-call(bf16[1024,768]{1,0:T(8,128)(2,1)S(1)} %copy-done.11, bf16[1024,512]{1,0:T(8,128)(2,1)S(1)} %pad_maximum_fusion.10.grad_in, f32[2,2,1024]{2,1,0:T(2,128)S(1)} %get-tuple-element.197.log_in, f32[1024,128]{1,0:T(8,128)S(1)} %copy.122.cos_in, f32[1024,128]{1,0:T(8,128)S(1)} %copy.123.sin_in, ...), custom_call_target="tpu_custom_call" | custom-call | flops 1 | bytes 1 | tf_op jit(solution)/shard_map/attend_back/pallas_call | solution.py:596
  313.7 6.8 %attend_back.7 = bf16[1024,384]{1,0:T(8,128)(2,1)S(1)} custom-call(bf16[1024,768]{1,0:T(8,128)(2,1)S(1)} %copy-done.12, bf16[1024,512]{1,0:T(8,128)(2,1)S(1)} %pad_maximum_fusion.10.grad_in, f32[2,2,1024]{2,1,0:T(2,128)S(1)} %get-tuple-element.197.log_in, f32[1024,128]{1,0:T(8,128)S(1)} %copy.122.cos_in, f32[1024,128]{1,0:T(8,128)S(1)} %copy.123.sin_in, ...), custom_call_target="tpu_custom_call" | custom-call | flops 1 | bytes 1 | tf_op jit(solution)/shard_map/attend_back/pallas_call | solution.py:596
  322.1 4.3 convolution_convert_fusion
  333.2 3.4 fusion.52
  350.6 3.4 fusion.15
  355.4 4.1 fusion.14
  359.5 11.0 %collective-permute-done.33.top = bf16[4,2,32,2048]{3,2,1,0:T(8,128)(2,1)S(1)} collective-permute-done((bf16[4,2,32,2048]{3,2,1,0:T(8,128)(2,1)}, bf16[4,2,32,2048]{3,2,1,0:T(8,128)(2,1)S(1)}, u32[]{:S(2)}, u32[]{:S(2)}) %collective-permute-start.33) | collective-permute-done | bytes 1048608 | tf_op jit(solution)/shard_map/ppermute | solution.py:25
  373.4 5.0 %collective-permute-start.48 = (f32[64,128]{1,0:T(8,128)S(1)}, f32[64,128]{1,0:T(8,128)S(1)}, u32[]{:S(2)}, u32[]{:S(2)}) collective-permute-start(f32[64,128]{1,0:T(8,128)S(1)} %get-tuple-element.267), channel_id=1, source_target_pairs={{0,16},{8,24},{16,0},{24,8},{1,17},{9,25},{17,1},{25,9},{2,18},{10... | collective-permute-start | bytes 98312 | tf_op jit(solution)/shard_map/ppermute | solution.py:34
  390.2 7.6 %collective-permute-done.40.low_got = bf16[4,32,2048]{2,1,0:T(8,128)(2,1)S(1)} collective-permute-done((bf16[4,32,2048]{2,1,0:T(8,128)(2,1)}, bf16[4,32,2048]{2,1,0:T(8,128)(2,1)S(1)}, u32[]{:S(2)}, u32[]{:S(2)}) %collective-permute-start.40) | collective-permute-done | bytes 524320 | tf_op jit(solution)/shard_map/ppermute | solution.py:25
  405.8 2.7 collective-permute-start.42
  411.3 9.0 %collective-permute-done.45 = bf16[256,1024]{1,0:T(8,128)(2,1)} collective-permute-done((bf16[256,1024]{1,0:T(8,128)(2,1)}, bf16[256,1024]{1,0:T(8,128)(2,1)}, u32[]{:S(2)}, u32[]{:S(2)}) %collective-permute-start.45) | collective-permute-done | bytes 524320 | tf_op jit(solution)/shard_map/ppermute | solution.py:25
  420.3 2.7 fusion.21
  424.2 4.4 collective-permute-start.46
  (403 shorter events, 156.9 us)
Async XLA Ops:
  7.2 182.6 %all-gather.2.cloned.1.call-start = ((), (), s32[]{:S(2)}) async-start(), calls=%async_computation.2 | async-start | bytes 4456448 | tf_op jit(solution)/shard_map/all_gather | solution.py:756
  9.3 37.3 %collective-permute-start = (bf16[256,1024]{1,0:T(8,128)(2,1)S(1)}, bf16[256,1024]{1,0:T(8,128)(2,1)S(1)}, u32[]{:S(2)}, u32[]{:S(2)}) collective-permute-start(bf16[256,1024]{1,0:T(8,128)(2,1)S(1)} %get-tuple-element.290), channel_id=1, source_target_pairs={{0,2},{2,0},{1,3},{3,1},{4,6},{6,4},{5,7},{7,5},{8,10},{10,8},{9,1... | collective-permute-start | bytes 1572872 | tf_op jit(solution)/shard_map/ppermute | solution.py:25
  20.1 7.2 %collective-permute-start.2 = (bf16[64,1920]{1,0:T(8,128)(2,1)S(1)}, bf16[64,1920]{1,0:T(8,128)(2,1)S(1)}, u32[]{:S(2)}, u32[]{:S(2)}) collective-permute-start(bf16[64,1920]{1,0:T(8,128)(2,1)S(1)} %bitcast.177), channel_id=1, source_target_pairs={{0,8},{8,16},{16,24},{24,0},{1,9},{9,17},{17,25},{25,1},{2,10},{10... | collective-permute-start | bytes 737288 | tf_op jit(solution)/shard_map/ppermute | solution.py:34
  21.4 20.8 %collective-permute-start.3 = (bf16[64,1920]{1,0:T(8,128)(2,1)S(1)}, bf16[64,1920]{1,0:T(8,128)(2,1)S(1)}, u32[]{:S(2)}, u32[]{:S(2)}) collective-permute-start(bf16[64,1920]{1,0:T(8,128)(2,1)S(1)} %bitcast.178), channel_id=1, source_target_pairs={{0,16},{8,24},{16,0},{24,8},{1,17},{9,25},{17,1},{25,9},{2,18},{10... | collective-permute-start | bytes 737288 | tf_op jit(solution)/shard_map/ppermute | solution.py:34
  22.4 22.3 %collective-permute-start.4 = (bf16[64,1920]{1,0:T(8,128)(2,1)S(1)}, bf16[64,1920]{1,0:T(8,128)(2,1)S(1)}, u32[]{:S(2)}, u32[]{:S(2)}) collective-permute-start(bf16[64,1920]{1,0:T(8,128)(2,1)S(1)} %bitcast.179), channel_id=1, source_target_pairs={{0,24},{8,0},{16,8},{24,16},{1,25},{9,1},{17,9},{25,17},{2,26},{10... | collective-permute-start | bytes 737288 | tf_op jit(solution)/shard_map/ppermute | solution.py:34
  45.3 12.4 %collective-permute-start.7 = (bf16[4,32,1920]{2,1,0:T(8,128)(2,1)S(1)}, bf16[4,32,1920]{2,1,0:T(8,128)(2,1)S(1)}, u32[]{:S(2)}, u32[]{:S(2)}) collective-permute-start(bf16[4,32,1920]{2,1,0:T(8,128)(2,1)S(1)} %get-tuple-element.142.refs_1_), channel_id=1, source_target_pairs={{0,4},{4,0},{1,5},{5,1},{2,6},{6,2},{3,7},{7,3},{8,12},{12,8},{9,1... | collective-permute-start | bytes 1474568 | tf_op jit(solution)/shard_map/ppermute | solution.py:29
  46.6 12.0 %collective-permute-start.6 = (bf16[4,32,1920]{2,1,0:T(8,128)(2,1)S(1)}, bf16[4,32,1920]{2,1,0:T(8,128)(2,1)S(1)}, u32[]{:S(2)}, u32[]{:S(2)}) collective-permute-start(bf16[4,32,1920]{2,1,0:T(8,128)(2,1)S(1)} %get-tuple-element.139.refs_0_), channel_id=1, source_target_pairs={{0,2},{2,0},{1,3},{3,1},{4,6},{6,4},{5,7},{7,5},{8,10},{10,8},{9,1... | collective-permute-start | bytes 1474568 | tf_op jit(solution)/shard_map/ppermute | solution.py:25
  46.9 8.4 %collective-permute-start.8 = (bf16[64,2560]{1,0:T(8,128)(2,1)}, bf16[64,2560]{1,0:T(8,128)(2,1)S(1)}, u32[]{:S(2)}, u32[]{:S(2)}) collective-permute-start(bf16[64,2560]{1,0:T(8,128)(2,1)} %bitcast.12.refs_0_), channel_id=1, source_target_pairs={{0,8},{8,16},{16,24},{24,0},{1,9},{9,17},{17,25},{25,1},{2,10},{10... | collective-permute-start | bytes 983048 | tf_op jit(solution)/shard_map/ppermute | solution.py:34
  59.7 23.8 %collective-permute-start.10 = (bf16[2,4,32,1920]{3,2,1,0:T(8,128)(2,1)}, bf16[2,4,32,1920]{3,2,1,0:T(8,128)(2,1)S(1)}, u32[]{:S(2)}, u32[]{:S(2)}) collective-permute-start(bf16[2,4,32,1920]{3,2,1,0:T(8,128)(2,1)} %pad_maximum_fusion.14), channel_id=1, source_target_pairs={{0,2},{2,0},{1,3},{3,1},{4,6},{6,4},{5,7},{7,5},{8,10},{10,8},{9,1... | collective-permute-start | bytes 2949128 | tf_op jit(solution)/shard_map/ppermute | solution.py:25
  61.1 23.5 %collective-permute-start.9 = (bf16[2,4,32,1920]{3,2,1,0:T(8,128)(2,1)}, bf16[2,4,32,1920]{3,2,1,0:T(8,128)(2,1)S(1)}, u32[]{:S(2)}, u32[]{:S(2)}) collective-permute-start(bf16[2,4,32,1920]{3,2,1,0:T(8,128)(2,1)} %pad_maximum_fusion.13), channel_id=1, source_target_pairs={{0,4},{4,0},{1,5},{5,1},{2,6},{6,2},{3,7},{7,3},{8,12},{12,8},{9,1... | collective-permute-start | bytes 2949128 | tf_op jit(solution)/shard_map/ppermute | solution.py:29
  61.4 27.2 %collective-permute-start.12 = (bf16[64,2560]{1,0:T(8,128)(2,1)}, bf16[64,2560]{1,0:T(8,128)(2,1)}, u32[]{:S(2)}, u32[]{:S(2)}) collective-permute-start(bf16[64,2560]{1,0:T(8,128)(2,1)} %bitcast.12.refs_0_), channel_id=1, source_target_pairs={{0,16},{8,24},{16,0},{24,8},{1,17},{9,25},{17,1},{25,9},{2,18},{10... | collective-permute-start | bytes 983048 | tf_op jit(solution)/shard_map/ppermute | solution.py:34
  61.4 27.6 %collective-permute-start.13 = (bf16[64,2560]{1,0:T(8,128)(2,1)}, bf16[64,2560]{1,0:T(8,128)(2,1)}, u32[]{:S(2)}, u32[]{:S(2)}) collective-permute-start(bf16[64,2560]{1,0:T(8,128)(2,1)} %bitcast.12.refs_0_), channel_id=1, source_target_pairs={{0,24},{8,0},{16,8},{24,16},{1,25},{9,1},{17,9},{25,17},{2,26},{10... | collective-permute-start | bytes 983048 | tf_op jit(solution)/shard_map/ppermute | solution.py:34
  62.6 336.1 %reduce-scatter.5.cloned.1.call-start = ((), (), s32[]{:S(2)}) async-start(), calls=%async_computation.4 | async-start | bytes 1310720 | tf_op jit(solution)/shard_map/reduce_scatter | solution.py:362
  64.9 32.2 %collective-permute-start.5 = (bf16[512,1024]{1,0:T(8,128)(2,1)}, bf16[512,1024]{1,0:T(8,128)(2,1)}, u32[]{:S(2)}, u32[]{:S(2)}) collective-permute-start(bf16[512,1024]{1,0:T(8,128)(2,1)} %pad_maximum_fusion.9), channel_id=1, source_target_pairs={{0,1},{1,0},{2,3},{3,2},{4,5},{5,4},{6,7},{7,6},{8,9},{9,8},{10,11... | collective-permute-start | bytes 3145736 | tf_op jit(solution)/shard_map/ppermute | solution.py:21
  90.7 19.7 %collective-permute-start.14 = (bf16[4,32,2560]{2,1,0:T(8,128)(2,1)S(1)}, bf16[4,32,2560]{2,1,0:T(8,128)(2,1)}, u32[]{:S(2)}, u32[]{:S(2)}) collective-permute-start(bf16[4,32,2560]{2,1,0:T(8,128)(2,1)S(1)} %get-tuple-element.152.refs_0_), channel_id=1, source_target_pairs={{0,2},{2,0},{1,3},{3,1},{4,6},{6,4},{5,7},{7,5},{8,10},{10,8},{9,1... | collective-permute-start | bytes 1966088 | tf_op jit(solution)/shard_map/ppermute | solution.py:25
  91.9 18.5 %collective-permute-start.15 = (bf16[4,32,2560]{2,1,0:T(8,128)(2,1)S(1)}, bf16[4,32,2560]{2,1,0:T(8,128)(2,1)}, u32[]{:S(2)}, u32[]{:S(2)}) collective-permute-start(bf16[4,32,2560]{2,1,0:T(8,128)(2,1)S(1)} %get-tuple-element.153.refs_1_), channel_id=1, source_target_pairs={{0,4},{4,0},{1,5},{5,1},{2,6},{6,2},{3,7},{7,3},{8,12},{12,8},{9,1... | collective-permute-start | bytes 1966088 | tf_op jit(solution)/shard_map/ppermute | solution.py:29
  94.2 5.5 %collective-permute-start.11 = (f32[16,128]{1,0:T(8,128)S(1)}, f32[16,128]{1,0:T(8,128)S(1)}, u32[]{:S(2)}, u32[]{:S(2)}) collective-permute-start(f32[16,128]{1,0:T(8,128)S(1)} %reshape.287), channel_id=1, source_target_pairs={{0,1},{1,0},{2,3},{3,2},{4,5},{5,4},{6,7},{7,6},{8,9},{9,8},{10,11... | collective-permute-start | bytes 24584 | tf_op jit(solution)/shard_map/ppermute | solution.py:21
  112.7 38.3 %collective-permute-start.16 = (bf16[2,4,32,2560]{3,2,1,0:T(8,128)(2,1)}, bf16[2,4,32,2560]{3,2,1,0:T(8,128)(2,1)}, u32[]{:S(2)}, u32[]{:S(2)}) collective-permute-start(bf16[2,4,32,2560]{3,2,1,0:T(8,128)(2,1)} %pad_maximum_fusion.6), channel_id=1, source_target_pairs={{0,4},{4,0},{1,5},{5,1},{2,6},{6,2},{3,7},{7,3},{8,12},{12,8},{9,1... | collective-permute-start | bytes 3932168 | tf_op jit(solution)/shard_map/ppermute | solution.py:29
  116.4 42.3 %collective-permute-start.18 = (bf16[2,4,32,2560]{3,2,1,0:T(8,128)(2,1)}, bf16[2,4,32,2560]{3,2,1,0:T(8,128)(2,1)}, u32[]{:S(2)}, u32[]{:S(2)}) collective-permute-start(bf16[2,4,32,2560]{3,2,1,0:T(8,128)(2,1)} %pad_maximum_fusion.7), channel_id=1, source_target_pairs={{0,2},{2,0},{1,3},{3,1},{4,6},{6,4},{5,7},{7,5},{8,10},{10,8},{9,1... | collective-permute-start | bytes 3932168 | tf_op jit(solution)/shard_map/ppermute | solution.py:25
  161.2 7.6 %collective-permute-start.19 = (bf16[16,64,512]{2,1,0:T(8,128)(2,1)S(1)}, bf16[16,64,512]{2,1,0:T(8,128)(2,1)S(1)}, u32[]{:S(2)}, u32[]{:S(2)}) collective-permute-start(bf16[16,64,512]{2,1,0:T(8,128)(2,1)S(1)} %bitcast.171), channel_id=1, source_target_pairs={{0,1},{1,0},{2,3},{3,2},{4,5},{5,4},{6,7},{7,6},{8,9},{9,8},{10,11... | collective-permute-start | bytes 3145736 | tf_op jit(solution)/shard_map/ppermute | solution.py:21
  175.2 14.6 %collective-permute-start.21 = (bf16[256,1152]{1,0:T(8,128)(2,1)S(1)}, bf16[256,1152]{1,0:T(8,128)(2,1)}, u32[]{:S(2)}, u32[]{:S(2)}) collective-permute-start(bf16[256,1152]{1,0:T(8,128)(2,1)S(1)} %copy-done.73), channel_id=1, source_target_pairs={{0,2},{2,0},{1,3},{3,1},{4,6},{6,4},{5,7},{7,5},{8,10},{10,8},{9,1... | collective-permute-start | bytes 1769480 | tf_op jit(solution)/shard_map/ppermute | solution.py:25
  220.4 24.9 %collective-permute-start.24 = (bf16[4,2,64,1024]{3,2,1,0:T(8,128)(2,1)S(1)}, bf16[4,2,64,1024]{3,2,1,0:T(8,128)(2,1)S(1)}, u32[]{:S(2)}, u32[]{:S(2)}) collective-permute-start(bf16[4,2,64,1024]{3,2,1,0:T(8,128)(2,1)S(1)} %get-tuple-element.172), channel_id=1, source_target_pairs={{0,2},{2,0},{1,3},{3,1},{4,6},{6,4},{5,7},{7,5},{8,10},{10,8},{9,1... | collective-permute-start | bytes 3145736 | tf_op jit(solution)/shard_map/ppermute | solution.py:25
  222.0 24.5 %collective-permute-start.25 = (bf16[4,2,64,1024]{3,2,1,0:T(8,128)(2,1)S(1)}, bf16[4,2,64,1024]{3,2,1,0:T(8,128)(2,1)S(1)}, u32[]{:S(2)}, u32[]{:S(2)}) collective-permute-start(bf16[4,2,64,1024]{3,2,1,0:T(8,128)(2,1)S(1)} %get-tuple-element.173), channel_id=1, source_target_pairs={{0,4},{4,0},{1,5},{5,1},{2,6},{6,2},{3,7},{7,3},{8,12},{12,8},{9,1... | collective-permute-start | bytes 3145736 | tf_op jit(solution)/shard_map/ppermute | solution.py:29
  246.5 14.7 %collective-permute-start.26 = (bf16[512,1024]{1,0:T(8,128)(2,1)}, bf16[512,1024]{1,0:T(8,128)(2,1)}, u32[]{:S(2)}, u32[]{:S(2)}) collective-permute-start(bf16[512,1024]{1,0:T(8,128)(2,1)} %slice.201), channel_id=1, source_target_pairs={{0,1},{1,0},{2,3},{3,2},{4,5},{5,4},{6,7},{7,6},{8,9},{9,8},{10,11... | collective-permute-start | bytes 3145736 | tf_op jit(solution)/shard_map/ppermute | solution.py:21
  261.1 49.6 %collective-permute-start.31 = (bf16[4,2,32,2048]{3,2,1,0:T(8,128)(2,1)}, bf16[4,2,32,2048]{3,2,1,0:T(8,128)(2,1)}, u32[]{:S(2)}, u32[]{:S(2)}) collective-permute-start(bf16[4,2,32,2048]{3,2,1,0:T(8,128)(2,1)} %get-tuple-element.195), channel_id=1, source_target_pairs={{0,4},{4,0},{1,5},{5,1},{2,6},{6,2},{3,7},{7,3},{8,12},{12,8},{9,1... | collective-permute-start | bytes 3145736 | tf_op jit(solution)/shard_map/ppermute | solution.py:29
  263.8 46.9 %collective-permute-start.30 = (bf16[4,2,32,2048]{3,2,1,0:T(8,128)(2,1)}, bf16[4,2,32,2048]{3,2,1,0:T(8,128)(2,1)}, u32[]{:S(2)}, u32[]{:S(2)}) collective-permute-start(bf16[4,2,32,2048]{3,2,1,0:T(8,128)(2,1)} %get-tuple-element.194), channel_id=1, source_target_pairs={{0,2},{2,0},{1,3},{3,1},{4,6},{6,4},{5,7},{7,5},{8,10},{10,8},{9,1... | collective-permute-start | bytes 3145736 | tf_op jit(solution)/shard_map/ppermute | solution.py:25
  270.0 7.6 %collective-permute-start.27 = (bf16[512,512]{1,0:T(8,128)(2,1)}, bf16[512,512]{1,0:T(8,128)(2,1)}, u32[]{:S(2)}, u32[]{:S(2)}) collective-permute-start(bf16[512,512]{1,0:T(8,128)(2,1)} %get-tuple-element.182), channel_id=1, source_target_pairs={{0,1},{1,0},{2,3},{3,2},{4,5},{5,4},{6,7},{7,6},{8,9},{9,8},{10,11... | collective-permute-start | bytes 1572872 | tf_op jit(solution)/shard_map/ppermute | solution.py:21
  270.3 27.0 %collective-permute-start.28 = (bf16[4,64,1024]{2,1,0:T(8,128)(2,1)}, bf16[4,64,1024]{2,1,0:T(8,128)(2,1)S(1)}, u32[]{:S(2)}, u32[]{:S(2)}) collective-permute-start(bf16[4,64,1024]{2,1,0:T(8,128)(2,1)} %get-tuple-element.186), channel_id=1, source_target_pairs={{0,4},{4,0},{1,5},{5,1},{2,6},{6,2},{3,7},{7,3},{8,12},{12,8},{9,1... | collective-permute-start | bytes 1572872 | tf_op jit(solution)/shard_map/ppermute | solution.py:29
  271.7 28.4 %collective-permute-start.29 = (bf16[4,64,1024]{2,1,0:T(8,128)(2,1)S(1)}, bf16[4,64,1024]{2,1,0:T(8,128)(2,1)S(1)}, u32[]{:S(2)}, u32[]{:S(2)}) collective-permute-start(bf16[4,64,1024]{2,1,0:T(8,128)(2,1)S(1)} %copy-done.48), channel_id=1, source_target_pairs={{0,2},{2,0},{1,3},{3,1},{4,6},{6,4},{5,7},{7,5},{8,10},{10,8},{9,1... | collective-permute-start | bytes 1572872 | tf_op jit(solution)/shard_map/ppermute | solution.py:25
  301.8 24.6 %collective-permute-start.32 = (bf16[16,32,1024]{2,1,0:T(8,128)(2,1)}, bf16[16,32,1024]{2,1,0:T(8,128)(2,1)}, u32[]{:S(2)}, u32[]{:S(2)}) collective-permute-start(bf16[16,32,1024]{2,1,0:T(8,128)(2,1)} %get-tuple-element.203), channel_id=1, source_target_pairs={{0,1},{1,0},{2,3},{3,2},{4,5},{5,4},{6,7},{7,6},{8,9},{9,8},{10,11... | collective-permute-start | bytes 3145736 | tf_op jit(solution)/shard_map/ppermute | solution.py:21
  320.8 18.5 %collective-permute-start.34 = (bf16[4,32,2048]{2,1,0:T(8,128)(2,1)S(1)}, bf16[4,32,2048]{2,1,0:T(8,128)(2,1)S(1)}, u32[]{:S(2)}, u32[]{:S(2)}) collective-permute-start(bf16[4,32,2048]{2,1,0:T(8,128)(2,1)S(1)} %get-tuple-element.207), channel_id=1, source_target_pairs={{0,4},{4,0},{1,5},{5,1},{2,6},{6,2},{3,7},{7,3},{8,12},{12,8},{9,1... | collective-permute-start | bytes 1572872 | tf_op jit(solution)/shard_map/ppermute | solution.py:29
  329.0 13.3 %collective-permute-start.35 = (bf16[4,32,2048]{2,1,0:T(8,128)(2,1)S(1)}, bf16[4,32,2048]{2,1,0:T(8,128)(2,1)S(1)}, u32[]{:S(2)}, u32[]{:S(2)}) collective-permute-start(bf16[4,32,2048]{2,1,0:T(8,128)(2,1)S(1)} %get-tuple-element.208), channel_id=1, source_target_pairs={{0,2},{2,0},{1,3},{3,1},{4,6},{6,4},{5,7},{7,5},{8,10},{10,8},{9,1... | collective-permute-start | bytes 1572872 | tf_op jit(solution)/shard_map/ppermute | solution.py:25
  343.2 7.4 %collective-permute-start.36 = (bf16[512,1024]{1,0:T(8,128)(2,1)}, bf16[512,1024]{1,0:T(8,128)(2,1)}, u32[]{:S(2)}, u32[]{:S(2)}) collective-permute-start(bf16[512,1024]{1,0:T(8,128)(2,1)} %slice.200), channel_id=1, source_target_pairs={{0,1},{1,0},{2,3},{3,2},{4,5},{5,4},{6,7},{7,6},{8,9},{9,8},{10,11... | collective-permute-start | bytes 3145736 | tf_op jit(solution)/shard_map/ppermute | solution.py:21
  345.0 77.9 %reduce-scatter.3.cloned.1.call-start = ((), (), s32[]{:S(2)}) async-start(), calls=%async_computation.3 | async-start | bytes 1310720 | tf_op jit(solution)/shard_map/reduce_scatter | solution.py:362
  345.3 25.2 %collective-permute-start.33 = (bf16[4,2,32,2048]{3,2,1,0:T(8,128)(2,1)}, bf16[4,2,32,2048]{3,2,1,0:T(8,128)(2,1)S(1)}, u32[]{:S(2)}, u32[]{:S(2)}) collective-permute-start(bf16[4,2,32,2048]{3,2,1,0:T(8,128)(2,1)} %get-tuple-element.205), channel_id=1, source_target_pairs={{0,2},{2,0},{1,3},{3,1},{4,6},{6,4},{5,7},{7,5},{8,10},{10,8},{9,1... | collective-permute-start | bytes 3145736 | tf_op jit(solution)/shard_map/ppermute | solution.py:25
  345.5 25.0 %collective-permute-start.37 = (bf16[4,2,32,2048]{3,2,1,0:T(8,128)(2,1)}, bf16[4,2,32,2048]{3,2,1,0:T(8,128)(2,1)S(1)}, u32[]{:S(2)}, u32[]{:S(2)}) collective-permute-start(bf16[4,2,32,2048]{3,2,1,0:T(8,128)(2,1)} %copy-done.44), channel_id=1, source_target_pairs={{0,4},{4,0},{1,5},{5,1},{2,6},{6,2},{3,7},{7,3},{8,12},{12,8},{9,1... | collective-permute-start | bytes 3145736 | tf_op jit(solution)/shard_map/ppermute | solution.py:29
  354.7 18.5 %collective-permute-start.38 = (f32[41,128]{1,0:T(8,128)S(1)}, f32[41,128]{1,0:T(8,128)S(1)}, u32[]{:S(2)}, u32[]{:S(2)}) collective-permute-start(f32[41,128]{1,0:T(8,128)S(1)} %bitcast.197), channel_id=1, source_target_pairs={{0,1},{1,0},{2,3},{3,2},{4,5},{5,4},{6,7},{7,6},{8,9},{9,8},{10,11... | collective-permute-start | bytes 62984 | tf_op jit(solution)/shard_map/ppermute | solution.py:21
  373.3 6.5 %collective-permute-start.47 = (f32[64,128]{1,0:T(8,128)S(1)}, f32[64,128]{1,0:T(8,128)S(1)}, u32[]{:S(2)}, u32[]{:S(2)}) collective-permute-start(f32[64,128]{1,0:T(8,128)S(1)} %get-tuple-element.267), channel_id=1, source_target_pairs={{0,8},{8,16},{16,24},{24,0},{1,9},{9,17},{17,25},{25,1},{2,10},{10... | collective-permute-start | bytes 98312 | tf_op jit(solution)/shard_map/ppermute | solution.py:34
  373.4 6.5 %collective-permute-start.48 = (f32[64,128]{1,0:T(8,128)S(1)}, f32[64,128]{1,0:T(8,128)S(1)}, u32[]{:S(2)}, u32[]{:S(2)}) collective-permute-start(f32[64,128]{1,0:T(8,128)S(1)} %get-tuple-element.267), channel_id=1, source_target_pairs={{0,16},{8,24},{16,0},{24,8},{1,17},{9,25},{17,1},{25,9},{2,18},{10... | collective-permute-start | bytes 98312 | tf_op jit(solution)/shard_map/ppermute | solution.py:34
  383.7 14.1 %collective-permute-start.40 = (bf16[4,32,2048]{2,1,0:T(8,128)(2,1)}, bf16[4,32,2048]{2,1,0:T(8,128)(2,1)S(1)}, u32[]{:S(2)}, u32[]{:S(2)}) collective-permute-start(bf16[4,32,2048]{2,1,0:T(8,128)(2,1)} %copy-done.46), channel_id=1, source_target_pairs={{0,2},{2,0},{1,3},{3,1},{4,6},{6,4},{5,7},{7,5},{8,10},{10,8},{9,1... | collective-permute-start | bytes 1572872 | tf_op jit(solution)/shard_map/ppermute | solution.py:25
  383.9 14.0 %collective-permute-start.39 = (bf16[4,32,2048]{2,1,0:T(8,128)(2,1)}, bf16[4,32,2048]{2,1,0:T(8,128)(2,1)S(1)}, u32[]{:S(2)}, u32[]{:S(2)}) collective-permute-start(bf16[4,32,2048]{2,1,0:T(8,128)(2,1)} %copy-done.45), channel_id=1, source_target_pairs={{0,4},{4,0},{1,5},{5,1},{2,6},{6,2},{3,7},{7,3},{8,12},{12,8},{9,1... | collective-permute-start | bytes 1572872 | tf_op jit(solution)/shard_map/ppermute | solution.py:29
  385.9 16.1 %collective-permute-start.51 = (f32[4,2,64,128]{3,2,1,0:T(8,128)S(1)}, f32[4,2,64,128]{3,2,1,0:T(8,128)S(1)}, u32[]{:S(2)}, u32[]{:S(2)}) collective-permute-start(f32[4,2,64,128]{3,2,1,0:T(8,128)S(1)} %pad_maximum_fusion.19), channel_id=1, source_target_pairs={{0,4},{4,0},{1,5},{5,1},{2,6},{6,2},{3,7},{7,3},{8,12},{12,8},{9,1... | collective-permute-start | bytes 786440 | tf_op jit(solution)/shard_map/ppermute | solution.py:29
  398.6 10.4 %collective-permute-start.44 = (bf16[256,1024]{1,0:T(8,128)(2,1)}, bf16[256,1024]{1,0:T(8,128)(2,1)}, u32[]{:S(2)}, u32[]{:S(2)}) collective-permute-start(bf16[256,1024]{1,0:T(8,128)(2,1)} %slice.155), channel_id=1, source_target_pairs={{0,2},{2,0},{1,3},{3,1},{4,6},{6,4},{5,7},{7,5},{8,10},{10,8},{9,1... | collective-permute-start | bytes 1572872 | tf_op jit(solution)/shard_map/ppermute | solution.py:25
  400.5 19.7 %collective-permute-start.45 = (bf16[256,1024]{1,0:T(8,128)(2,1)}, bf16[256,1024]{1,0:T(8,128)(2,1)}, u32[]{:S(2)}, u32[]{:S(2)}) collective-permute-start(bf16[256,1024]{1,0:T(8,128)(2,1)} %slice.203), channel_id=1, source_target_pairs={{0,2},{2,0},{1,3},{3,1},{4,6},{6,4},{5,7},{7,5},{8,10},{10,8},{9,1... | collective-permute-start | bytes 1572872 | tf_op jit(solution)/shard_map/ppermute | solution.py:25
  405.7 28.3 %collective-permute-start.41 = (bf16[64,2048]{1,0:T(8,128)(2,1)S(1)}, bf16[64,2048]{1,0:T(8,128)(2,1)}, u32[]{:S(2)}, u32[]{:S(2)}) collective-permute-start(bf16[64,2048]{1,0:T(8,128)(2,1)S(1)} %get-tuple-element.226), channel_id=1, source_target_pairs={{0,8},{8,16},{16,24},{24,0},{1,9},{9,17},{17,25},{25,1},{2,10},{10... | collective-permute-start | bytes 786440 | tf_op jit(solution)/shard_map/ppermute | solution.py:34
  405.8 28.3 %collective-permute-start.42 = (bf16[64,2048]{1,0:T(8,128)(2,1)S(1)}, bf16[64,2048]{1,0:T(8,128)(2,1)}, u32[]{:S(2)}, u32[]{:S(2)}) collective-permute-start(bf16[64,2048]{1,0:T(8,128)(2,1)S(1)} %get-tuple-element.227), channel_id=1, source_target_pairs={{0,16},{8,24},{16,0},{24,8},{1,17},{9,25},{17,1},{25,9},{2,18},{10... | collective-permute-start | bytes 786440 | tf_op jit(solution)/shard_map/ppermute | solution.py:34
  408.5 25.6 %collective-permute-start.43 = (bf16[64,2048]{1,0:T(8,128)(2,1)S(1)}, bf16[64,2048]{1,0:T(8,128)(2,1)}, u32[]{:S(2)}, u32[]{:S(2)}) collective-permute-start(bf16[64,2048]{1,0:T(8,128)(2,1)S(1)} %get-tuple-element.228), channel_id=1, source_target_pairs={{0,24},{8,0},{16,8},{24,16},{1,25},{9,1},{17,9},{25,17},{2,26},{10... | collective-permute-start | bytes 786440 | tf_op jit(solution)/shard_map/ppermute | solution.py:34
  424.2 8.1 %collective-permute-start.46 = (f32[32,16,128]{2,1,0:T(8,128)S(1)}, f32[32,16,128]{2,1,0:T(8,128)S(1)}, u32[]{:S(2)}, u32[]{:S(2)}) collective-permute-start(f32[32,16,128]{2,1,0:T(8,128)S(1)} %dynamic-slice_bitcast_fusion.4), channel_id=1, source_target_pairs={{0,1},{1,0},{2,3},{3,2},{4,5},{5,4},{6,7},{7,6},{8,9},{9,8},{10,11... | collective-permute-start | bytes 786440 | tf_op jit(solution)/shard_map/ppermute | solution.py:21
  (91 other events, 456.5 us)
Sparse Core Ops, SparseCore 0:
  62.7 104.6 all-gather.1
  345.2 27.4 reduce-scatter.4
  375.1 28.0 reduce-scatter.2

commit v5 on v4

--- a/solution.py
+++ b/solution.py
@@ -959,7 +959,7 @@
     small_got = swap_core(small)
     last_sum.got[0], input_grad = tie(last_sum.got[0], input_grad)
     last_sum.add_near()
-    small_got, input_grad, last_sum.got[0] = tie(small_got, input_grad, last_sum.got[0])
+    input_grad, last_sum.got[0] = tie(input_grad, last_sum.got[0])
     last_sum.far()
     small = small + small_got
     up_bias_part = jnp.sum(inner_grad.astype(f32), 0).reshape(-1, 128)

time: 453 us -> 444 us (0.980)
    ppermute x15, waiting for transfers between devices: 73.7 us -> 56.3 us  [swap_x(): return lax.ppermute(v, 'x', [(0, 1), (1, 0)])]
    ppermute x11, waiting for transfers between devices: 16 us -> 25.4 us  [swap_y(): return lax.ppermute(v, 'y', [(0, 1), (1, 0)])]
    ppermute x12, waiting for transfers between devices: 31.5 us -> 36.2 us  [shift_z(): return lax.ppermute(v, 'z', [(i, (i + k) % depth) for i in range(depth)])]
  transfers between devices with their start and end apart: 56 -> 56, of which waited for: 28 -> 29; matrix products, arithmetic and copies ran while one was open for 24% -> 24% of each run, Pallas kernels for 18% -> 18%
where the time goes in v5:
time: 444 us; the launch traced here: 439 us
  waiting for transfers between devices  121 us (27%)
  Pallas kernels  81.5 us (18%)
  other arithmetic  59.7 us (13%)
  starting transfers between devices  57.3 us (13%)
  matrix products  53.2 us (12%)
  local copies, waits for them, and re-layouts  47.4 us (11%)
  between operations  18.6 us (4%)
    ppermute x15, waiting for transfers between devices, swap_x(): return lax.ppermute(v, 'x', [(0, 1), (1, 0)])  56.3 us
    dot_general x11, matrix products, dot(): lax.dot_general(a, b, (((da,), (db,)), ((), ())), preferred_element_type=...  53.2 us
    ppermute x12, waiting for transfers between devices, shift_z(): return lax.ppermute(v, 'z', [(i, (i + k) % depth) for i in range(depth)])  36.2 us
    unnamed x177, local copies, waits for them, and re-layouts  28.5 us
    pallas_call x4, Pallas kernels, attend_back(): pl.pallas_call(attend_back_kernel, grid=(pairs,), in_specs=[pl.BlockSpec(...  26.8 us
    ppermute x11, waiting for transfers between devices, swap_y(): return lax.ppermute(v, 'y', [(0, 1), (1, 0)])  25.4 us
    ppermute x15, starting transfers between devices, swap_core(): return lax.ppermute(v, 'core', [(0, 1), (1, 0)])  21.7 us
    pallas_call x2, Pallas kernels, attend(): pl.pallas_call(attend_kernel, grid=(pairs,), in_specs=[pl.BlockSpec((toke...  20.9 us
  transfers between devices with their start and end apart: 56, of which 29 were waited for; matrix products, arithmetic and copies ran while one was open for 24% of the time, Pallas kernels for 18%

profile of v5, /device:TPU:9, one launch (start us, length us, event | category | flops | bytes accessed | tf_op | source)
XLA Modules:
  0.0 439.1 jit_solution(10816004299631060115)
XLA Ops:
  23.9 3.4 collective-permute-done.2.refs_1_
  27.3 14.9 %collective-permute-done.3.refs_2_ = bf16[64,1920]{1,0:T(8,128)(2,1)S(1)} collective-permute-done((bf16[64,1920]{1,0:T(8,128)(2,1)S(1)}, bf16[64,1920]{1,0:T(8,128)(2,1)S(1)}, u32[]{:S(2)}, u32[]{:S(2)}) %collective-permute-start.3) | collective-permute-done | bytes 245792 | tf_op jit(solution)/shard_map/ppermute | solution.py:34
  42.2 2.5 collective-permute-done.4.refs_3_
  46.9 8.4 %collective-permute-done.8.refs_1_ = bf16[64,2560]{1,0:T(8,128)(2,1)S(1)} collective-permute-done((bf16[64,2560]{1,0:T(8,128)(2,1)}, bf16[64,2560]{1,0:T(8,128)(2,1)S(1)}, u32[]{:S(2)}, u32[]{:S(2)}) %collective-permute-start.8) | collective-permute-done | bytes 327712 | tf_op jit(solution)/shard_map/ppermute | solution.py:34
  55.3 2.4 collective-permute-done.7.refs_3_
  64.9 2.7 collective-permute-start.5
  67.6 15.9 %collective-permute-done.10.refs_5_ = bf16[2,4,32,1920]{3,2,1,0:T(8,128)(2,1)S(1)} collective-permute-done((bf16[2,4,32,1920]{3,2,1,0:T(8,128)(2,1)}, bf16[2,4,32,1920]{3,2,1,0:T(8,128)(2,1)S(1)}, u32[]{:S(2)}, u32[]{:S(2)}) %collective-permute-start.10) | collective-permute-done | bytes 983072 | tf_op jit(solution)/shard_map/ppermute | solution.py:25
  94.2 2.9 collective-permute-start.11
  99.8 8.6 %project.1 = (bf16[1024,1024]{1,0:T(8,128)(2,1)S(1)}, f32[1024,1536]{1,0:T(8,128)}) custom-call(bf16[1024,1024]{1,0:T(8,128)(2,1)S(1)} %pad_maximum_fusion.2.source, f32[1,1024]{1,0:T(1,128)S(1)} %get-tuple-element.300.scale, f32[1,1024]{1,0:T(1,128)S(1)} %get-tuple-element.299.shift, bf16[1024,1536]{1,0:T(8,128)(2,1)} %bitcast.161), custom_call_target="tpu_custom_call" | custom-call | flops 1 | bytes 1 | tf_op jit(solution)/shard_map/project/pallas_call | solution.py:433
  110.4 2.3 pad_maximum_fusion.6
  114.1 2.3 pad_maximum_fusion.7
  120.0 2.3 fusion.26
  122.3 10.3 %attend.2 = (bf16[1024,768]{1,0:T(8,128)(2,1)S(1)}, bf16[1024,256]{1,0:T(8,128)(2,1)S(1)}, f32[2,2,1024]{2,1,0:T(2,128)S(1)}) custom-call(f32[1024,1536]{1,0:T(8,128)} %get-tuple-element.154.project_in, f32[1024,128]{1,0:T(8,128)S(1)} %copy.122.cos_in, f32[1024,128]{1,0:T(8,128)S(1)} %copy.123.sin_in), custom_call_target="tpu_custom_call" | custom-call | flops 1 | bytes 1 | tf_op jit(solution)/shard_map/attend/pallas_call | solution.py:530
  133.8 10.5 %attend.3 = (bf16[1024,768]{1,0:T(8,128)(2,1)S(1)}, bf16[1024,256]{1,0:T(8,128)(2,1)S(1)}, f32[2,2,1024]{2,1,0:T(2,128)S(1)}) custom-call(f32[1024,1536]{1,0:T(8,128)} %get-tuple-element.154.project_in, f32[1024,128]{1,0:T(8,128)S(1)} %copy.122.cos_in, f32[1024,128]{1,0:T(8,128)S(1)} %copy.123.sin_in, bf16[1024,256]{1,0:T(8,128)(2,1)S(1)} %get-tuple-element.159.refs_0_), custom_call_target="tpu_custom_call" | custom-call | flops 1 | bytes 1 | tf_op jit(solution)/shard_map/attend/pallas_call | solution.py:530
  144.3 6.6 %collective-permute-done.16.refs_4_ = bf16[2,4,32,2560]{3,2,1,0:T(8,128)(2,1)} collective-permute-done((bf16[2,4,32,2560]{3,2,1,0:T(8,128)(2,1)}, bf16[2,4,32,2560]{3,2,1,0:T(8,128)(2,1)}, u32[]{:S(2)}, u32[]{:S(2)}) %collective-permute-start.16) | collective-permute-done | bytes 1310752 | tf_op jit(solution)/shard_map/ppermute | solution.py:29
  151.0 7.7 %collective-permute-done.18.refs_5_ = bf16[2,4,32,2560]{3,2,1,0:T(8,128)(2,1)} collective-permute-done((bf16[2,4,32,2560]{3,2,1,0:T(8,128)(2,1)}, bf16[2,4,32,2560]{3,2,1,0:T(8,128)(2,1)}, u32[]{:S(2)}, u32[]{:S(2)}) %collective-permute-start.18) | collective-permute-done | bytes 1310752 | tf_op jit(solution)/shard_map/ppermute | solution.py:25
  158.7 2.5 move.13
  161.2 5.0 %collective-permute-start.19 = (bf16[16,64,512]{2,1,0:T(8,128)(2,1)S(1)}, bf16[16,64,512]{2,1,0:T(8,128)(2,1)S(1)}, u32[]{:S(2)}, u32[]{:S(2)}) collective-permute-start(bf16[16,64,512]{2,1,0:T(8,128)(2,1)S(1)} %bitcast.171), channel_id=1, source_target_pairs={{0,1},{1,0},{2,3},{3,2},{4,5},{5,4},{6,7},{7,6},{8,9},{9,8},{10,11... | collective-permute-start | bytes 3145736 | tf_op jit(solution)/shard_map/ppermute | solution.py:21
  170.2 2.6 fusion.49
  176.7 8.7 %multiply_convert_fusion = (bf16[1024,2048]{1,0:T(8,128)(2,1)}, f32[1024,2048]{1,0:T(8,128)}) fusion(f32[2048]{0:T(1024)S(1)} %bitcast.202, bf16[1024,2048]{1,0:T(8,128)(2,1)S(1)} %bitcast.183, bf16[512,1024]{1,0:T(8,128)(2,1)S(1)} %collective-permute-done.20, bf16[512,1024]{1,0:T(8,128)(2,1)S(1)} %add_convert_fusion.1), kind=kOutput, calls=%fused_computation.8 | convolution fusion | flops 4311744512 | bytes 18882560 | tf_op jit(solution)/shard_map/dot_general | solution.py:468
  185.4 4.5 %collective-permute-done.21 = bf16[256,1152]{1,0:T(8,128)(2,1)} collective-permute-done((bf16[256,1152]{1,0:T(8,128)(2,1)S(1)}, bf16[256,1152]{1,0:T(8,128)(2,1)}, u32[]{:S(2)}, u32[]{:S(2)}) %collective-permute-start.21) | collective-permute-done | bytes 589856 | tf_op jit(solution)/shard_map/ppermute | solution.py:25
  189.8 7.5 %fusion.50 = f32[1024,1024]{1,0:T(8,128)S(1)} fusion(bf16[1024,2048]{1,0:T(8,128)(2,1)} %get-tuple-element.168, bf16[2048,1024]{1,0:T(8,128)(2,1)} %all-gather.2.cloned.1.call-done), kind=kOutput, calls=%fused_computation.183 | convolution fusion | flops 4294967296 | bytes 12582912 | tf_op jit(solution)/shard_map/dot_general | solution.py:468
  204.8 4.9 %fusion.17 = (f32[]{:T(128)}, f32[512,1024]{1,0:T(8,128)S(1)}, bf16[512,1024]{1,0:T(8,128)(2,1)}) fusion(f32[512]{0:T(512)S(1)} %get-tuple-element.260, bf16[256,1152]{1,0:T(8,128)(2,1)} %collective-permute-done.21, bf16[256,1152]{1,0:T(8,128)(2,1)S(1)} %copy-done.62, f32[512,1024]{1,0:T(8,128)} %copy-done.47, f32[1024]{0:T(1024)S(1)} %add.248, ...), kind=kLoop, calls=%fused_computation.30 | loop fusion | flops 6815743 | bytes 9574404 | tf_op jit(solution)/shard_map/reduce_sum | solution.py:870
  213.3 4.9 %convolution_convert_fusion.2 = bf16[2048,1024]{1,0:T(8,128)(2,1)S(1)} fusion(bf16[1024,2048]{1,0:T(8,128)(2,1)S(1)} %copy-done.80, bf16[512,1024]{1,0:T(8,128)(2,1)S(1)} %collective-permute-done.23, bf16[512,1024]{1,0:T(8,128)(2,1)S(1)} %get-tuple-element.269), kind=kOutput, calls=%fused_computation.13 | convolution fusion | flops 4301258752 | bytes 10485760 | tf_op jit(solution)/shard_map/dot_general | solution.py:468
  222.5 8.1 %convert_reduce_fusion = (f32[2048]{0:T(1024)S(1)}, bf16[1024,2048]{1,0:T(8,128)(2,1)S(1)}) fusion(f32[1024,2048]{1,0:T(8,128)S(1)} %bitcast.215, f32[2048]{0:T(1024)S(1)} %bitcast.203, bf16[1024,1024]{1,0:T(8,128)(2,1)S(1)} %pad_maximum_fusion.4, bf16[2048,1024]{1,0:T(8,128)(2,1)S(1)} %copy-done.77), kind=kOutput, calls=%fused_computation.7 | convolution fusion | flops 4322228224 | bytes 18890752 | tf_op jit(solution)/shard_map/dot_general | solution.py:468
  230.5 4.5 %fusion.51 = f32[1024,1024]{1,0:T(8,128)S(1)} fusion(bf16[1024,2048]{1,0:T(8,128)(2,1)S(1)} %get-tuple-element.311, bf16[1024,2048]{1,0:T(8,128)(2,1)S(1)} %bitcast.184), kind=kOutput, calls=%fused_computation.184 | convolution fusion | flops 4294967296 | bytes 12582912 | tf_op jit(solution)/shard_map/dot_general | solution.py:468
  236.4 8.9 %collective-permute-done.24.top = bf16[4,2,64,1024]{3,2,1,0:T(8,128)(2,1)S(1)} collective-permute-done((bf16[4,2,64,1024]{3,2,1,0:T(8,128)(2,1)S(1)}, bf16[4,2,64,1024]{3,2,1,0:T(8,128)(2,1)S(1)}, u32[]{:S(2)}, u32[]{:S(2)}) %collective-permute-start.24) | collective-permute-done | bytes 1048608 | tf_op jit(solution)/shard_map/ppermute | solution.py:25
  253.3 4.9 %convolution_convert_fusion.1 = bf16[1024,2048]{1,0:T(8,128)(2,1)S(1)} fusion(bf16[1024,1024]{1,0:T(8,128)(2,1)S(1)} %copy-done.68, bf16[1024,2048]{1,0:T(8,128)(2,1)S(1)} %copy-done.79), kind=kOutput, calls=%fused_computation.12 | convolution fusion | flops 4297064448 | bytes 10485760 | tf_op jit(solution)/shard_map/dot_general | solution.py:468
  261.4 2.4 multiply_reduce_fusion
  264.0 3.7 fusion.44
  273.1 2.9 convolution_convert_fusion.3
  279.2 6.6 %attend_back.4.refs_0_ = bf16[1024,384]{1,0:T(8,128)(2,1)S(1)} custom-call(bf16[1024,768]{1,0:T(8,128)(2,1)S(1)} %copy-done.9, bf16[1024,512]{1,0:T(8,128)(2,1)S(1)} %pad_maximum_fusion.10.grad_in, f32[2,2,1024]{2,1,0:T(2,128)S(1)} %get-tuple-element.184.log_in, f32[1024,128]{1,0:T(8,128)S(1)} %copy.122.cos_in, f32[1024,128]{1,0:T(8,128)S(1)} %copy.123.sin_in), custom_call_target="tpu_custom_call" | custom-call | flops 1 | bytes 1 | tf_op jit(solution)/shard_map/attend_back/pallas_call | solution.py:596
  285.8 6.8 %attend_back.5.refs_0_ = bf16[1024,384]{1,0:T(8,128)(2,1)S(1)} custom-call(bf16[1024,768]{1,0:T(8,128)(2,1)S(1)} %copy-done.9, bf16[1024,512]{1,0:T(8,128)(2,1)S(1)} %pad_maximum_fusion.10.grad_in, f32[2,2,1024]{2,1,0:T(2,128)S(1)} %get-tuple-element.184.log_in, f32[1024,128]{1,0:T(8,128)S(1)} %copy.122.cos_in, f32[1024,128]{1,0:T(8,128)S(1)} %copy.123.sin_in, ...), custom_call_target="tpu_custom_call" | custom-call | flops 1 | bytes 1 | tf_op jit(solution)/shard_map/attend_back/pallas_call | solution.py:596
  292.6 4.7 %collective-permute-done.28.top_got = bf16[4,64,1024]{2,1,0:T(8,128)(2,1)S(1)} collective-permute-done((bf16[4,64,1024]{2,1,0:T(8,128)(2,1)}, bf16[4,64,1024]{2,1,0:T(8,128)(2,1)S(1)}, u32[]{:S(2)}, u32[]{:S(2)}) %collective-permute-start.28) | collective-permute-done | bytes 524320 | tf_op jit(solution)/shard_map/ppermute | solution.py:29
  297.3 2.8 collective-permute-done.29.low_got
  304.1 6.6 %attend_back.6.refs_0_ = bf16[1024,384]{1,0:T(8,128)(2,1)S(1)} custom-call(bf16[1024,768]{1,0:T(8,128)(2,1)S(1)} %copy-done.11, bf16[1024,512]{1,0:T(8,128)(2,1)S(1)} %pad_maximum_fusion.10.grad_in, f32[2,2,1024]{2,1,0:T(2,128)S(1)} %get-tuple-element.196.log_in, f32[1024,128]{1,0:T(8,128)S(1)} %copy.122.cos_in, f32[1024,128]{1,0:T(8,128)S(1)} %copy.123.sin_in, ...), custom_call_target="tpu_custom_call" | custom-call | flops 1 | bytes 1 | tf_op jit(solution)/shard_map/attend_back/pallas_call | solution.py:596
  313.7 6.8 %attend_back.7 = bf16[1024,384]{1,0:T(8,128)(2,1)S(1)} custom-call(bf16[1024,768]{1,0:T(8,128)(2,1)S(1)} %copy-done.12, bf16[1024,512]{1,0:T(8,128)(2,1)S(1)} %pad_maximum_fusion.10.grad_in, f32[2,2,1024]{2,1,0:T(2,128)S(1)} %get-tuple-element.196.log_in, f32[1024,128]{1,0:T(8,128)S(1)} %copy.122.cos_in, f32[1024,128]{1,0:T(8,128)S(1)} %copy.123.sin_in, ...), custom_call_target="tpu_custom_call" | custom-call | flops 1 | bytes 1 | tf_op jit(solution)/shard_map/attend_back/pallas_call | solution.py:596
  322.1 4.3 convolution_convert_fusion
  333.2 3.4 fusion.52
  351.3 3.3 fusion.15
  357.0 5.2 %collective-permute-start.48 = (f32[64,128]{1,0:T(8,128)S(1)}, f32[64,128]{1,0:T(8,128)S(1)}, u32[]{:S(2)}, u32[]{:S(2)}) collective-permute-start(f32[64,128]{1,0:T(8,128)S(1)} %get-tuple-element.265), channel_id=1, source_target_pairs={{0,16},{8,24},{16,0},{24,8},{1,17},{9,25},{17,1},{25,9},{2,18},{10... | collective-permute-start | bytes 98312 | tf_op jit(solution)/shard_map/ppermute | solution.py:34
  363.6 2.5 collective-permute-done.48
  366.2 4.1 collective-permute-done.49
  371.5 3.5 fusion.14
  380.6 8.7 %collective-permute-done.38.top_got = bf16[4,32,2048]{2,1,0:T(8,128)(2,1)S(1)} collective-permute-done((bf16[4,32,2048]{2,1,0:T(8,128)(2,1)S(1)}, bf16[4,32,2048]{2,1,0:T(8,128)(2,1)S(1)}, u32[]{:S(2)}, u32[]{:S(2)}) %collective-permute-start.38) | collective-permute-done | bytes 524320 | tf_op jit(solution)/shard_map/ppermute | solution.py:29
  404.8 9.0 %collective-permute-done.44 = bf16[256,1024]{1,0:T(8,128)(2,1)} collective-permute-done((bf16[256,1024]{1,0:T(8,128)(2,1)}, bf16[256,1024]{1,0:T(8,128)(2,1)}, u32[]{:S(2)}, u32[]{:S(2)}) %collective-permute-start.44) | collective-permute-done | bytes 524320 | tf_op jit(solution)/shard_map/ppermute | solution.py:25
  413.7 2.7 fusion.21
  417.7 3.0 collective-permute-start.45
  (403 shorter events, 156.8 us)
Async XLA Ops:
  7.2 182.6 %all-gather.2.cloned.1.call-start = ((), (), s32[]{:S(2)}) async-start(), calls=%async_computation.2 | async-start | bytes 4456448 | tf_op jit(solution)/shard_map/all_gather | solution.py:756
  9.3 37.3 %collective-permute-start = (bf16[256,1024]{1,0:T(8,128)(2,1)S(1)}, bf16[256,1024]{1,0:T(8,128)(2,1)S(1)}, u32[]{:S(2)}, u32[]{:S(2)}) collective-permute-start(bf16[256,1024]{1,0:T(8,128)(2,1)S(1)} %get-tuple-element.288), channel_id=1, source_target_pairs={{0,2},{2,0},{1,3},{3,1},{4,6},{6,4},{5,7},{7,5},{8,10},{10,8},{9,1... | collective-permute-start | bytes 1572872 | tf_op jit(solution)/shard_map/ppermute | solution.py:25
  20.1 7.2 %collective-permute-start.2 = (bf16[64,1920]{1,0:T(8,128)(2,1)S(1)}, bf16[64,1920]{1,0:T(8,128)(2,1)S(1)}, u32[]{:S(2)}, u32[]{:S(2)}) collective-permute-start(bf16[64,1920]{1,0:T(8,128)(2,1)S(1)} %bitcast.177), channel_id=1, source_target_pairs={{0,8},{8,16},{16,24},{24,0},{1,9},{9,17},{17,25},{25,1},{2,10},{10... | collective-permute-start | bytes 737288 | tf_op jit(solution)/shard_map/ppermute | solution.py:34
  21.4 20.8 %collective-permute-start.3 = (bf16[64,1920]{1,0:T(8,128)(2,1)S(1)}, bf16[64,1920]{1,0:T(8,128)(2,1)S(1)}, u32[]{:S(2)}, u32[]{:S(2)}) collective-permute-start(bf16[64,1920]{1,0:T(8,128)(2,1)S(1)} %bitcast.178), channel_id=1, source_target_pairs={{0,16},{8,24},{16,0},{24,8},{1,17},{9,25},{17,1},{25,9},{2,18},{10... | collective-permute-start | bytes 737288 | tf_op jit(solution)/shard_map/ppermute | solution.py:34
  22.4 22.3 %collective-permute-start.4 = (bf16[64,1920]{1,0:T(8,128)(2,1)S(1)}, bf16[64,1920]{1,0:T(8,128)(2,1)S(1)}, u32[]{:S(2)}, u32[]{:S(2)}) collective-permute-start(bf16[64,1920]{1,0:T(8,128)(2,1)S(1)} %bitcast.179), channel_id=1, source_target_pairs={{0,24},{8,0},{16,8},{24,16},{1,25},{9,1},{17,9},{25,17},{2,26},{10... | collective-permute-start | bytes 737288 | tf_op jit(solution)/shard_map/ppermute | solution.py:34
  45.3 12.4 %collective-permute-start.7 = (bf16[4,32,1920]{2,1,0:T(8,128)(2,1)S(1)}, bf16[4,32,1920]{2,1,0:T(8,128)(2,1)S(1)}, u32[]{:S(2)}, u32[]{:S(2)}) collective-permute-start(bf16[4,32,1920]{2,1,0:T(8,128)(2,1)S(1)} %get-tuple-element.141.refs_1_), channel_id=1, source_target_pairs={{0,4},{4,0},{1,5},{5,1},{2,6},{6,2},{3,7},{7,3},{8,12},{12,8},{9,1... | collective-permute-start | bytes 1474568 | tf_op jit(solution)/shard_map/ppermute | solution.py:29
  46.6 12.0 %collective-permute-start.6 = (bf16[4,32,1920]{2,1,0:T(8,128)(2,1)S(1)}, bf16[4,32,1920]{2,1,0:T(8,128)(2,1)S(1)}, u32[]{:S(2)}, u32[]{:S(2)}) collective-permute-start(bf16[4,32,1920]{2,1,0:T(8,128)(2,1)S(1)} %get-tuple-element.138.refs_0_), channel_id=1, source_target_pairs={{0,2},{2,0},{1,3},{3,1},{4,6},{6,4},{5,7},{7,5},{8,10},{10,8},{9,1... | collective-permute-start | bytes 1474568 | tf_op jit(solution)/shard_map/ppermute | solution.py:25
  46.9 8.4 %collective-permute-start.8 = (bf16[64,2560]{1,0:T(8,128)(2,1)}, bf16[64,2560]{1,0:T(8,128)(2,1)S(1)}, u32[]{:S(2)}, u32[]{:S(2)}) collective-permute-start(bf16[64,2560]{1,0:T(8,128)(2,1)} %bitcast.12.refs_0_), channel_id=1, source_target_pairs={{0,8},{8,16},{16,24},{24,0},{1,9},{9,17},{17,25},{25,1},{2,10},{10... | collective-permute-start | bytes 983048 | tf_op jit(solution)/shard_map/ppermute | solution.py:34
  59.7 23.8 %collective-permute-start.10 = (bf16[2,4,32,1920]{3,2,1,0:T(8,128)(2,1)}, bf16[2,4,32,1920]{3,2,1,0:T(8,128)(2,1)S(1)}, u32[]{:S(2)}, u32[]{:S(2)}) collective-permute-start(bf16[2,4,32,1920]{3,2,1,0:T(8,128)(2,1)} %pad_maximum_fusion.14), channel_id=1, source_target_pairs={{0,2},{2,0},{1,3},{3,1},{4,6},{6,4},{5,7},{7,5},{8,10},{10,8},{9,1... | collective-permute-start | bytes 2949128 | tf_op jit(solution)/shard_map/ppermute | solution.py:25
  61.1 23.5 %collective-permute-start.9 = (bf16[2,4,32,1920]{3,2,1,0:T(8,128)(2,1)}, bf16[2,4,32,1920]{3,2,1,0:T(8,128)(2,1)S(1)}, u32[]{:S(2)}, u32[]{:S(2)}) collective-permute-start(bf16[2,4,32,1920]{3,2,1,0:T(8,128)(2,1)} %pad_maximum_fusion.13), channel_id=1, source_target_pairs={{0,4},{4,0},{1,5},{5,1},{2,6},{6,2},{3,7},{7,3},{8,12},{12,8},{9,1... | collective-permute-start | bytes 2949128 | tf_op jit(solution)/shard_map/ppermute | solution.py:29
  61.4 27.2 %collective-permute-start.12 = (bf16[64,2560]{1,0:T(8,128)(2,1)}, bf16[64,2560]{1,0:T(8,128)(2,1)}, u32[]{:S(2)}, u32[]{:S(2)}) collective-permute-start(bf16[64,2560]{1,0:T(8,128)(2,1)} %bitcast.12.refs_0_), channel_id=1, source_target_pairs={{0,16},{8,24},{16,0},{24,8},{1,17},{9,25},{17,1},{25,9},{2,18},{10... | collective-permute-start | bytes 983048 | tf_op jit(solution)/shard_map/ppermute | solution.py:34
  61.4 27.6 %collective-permute-start.13 = (bf16[64,2560]{1,0:T(8,128)(2,1)}, bf16[64,2560]{1,0:T(8,128)(2,1)}, u32[]{:S(2)}, u32[]{:S(2)}) collective-permute-start(bf16[64,2560]{1,0:T(8,128)(2,1)} %bitcast.12.refs_0_), channel_id=1, source_target_pairs={{0,24},{8,0},{16,8},{24,16},{1,25},{9,1},{17,9},{25,17},{2,26},{10... | collective-permute-start | bytes 983048 | tf_op jit(solution)/shard_map/ppermute | solution.py:34
  62.6 328.3 %reduce-scatter.5.cloned.1.call-start = ((), (), s32[]{:S(2)}) async-start(), calls=%async_computation.4 | async-start | bytes 1310720 | tf_op jit(solution)/shard_map/reduce_scatter | solution.py:362
  64.9 32.2 %collective-permute-start.5 = (bf16[512,1024]{1,0:T(8,128)(2,1)}, bf16[512,1024]{1,0:T(8,128)(2,1)}, u32[]{:S(2)}, u32[]{:S(2)}) collective-permute-start(bf16[512,1024]{1,0:T(8,128)(2,1)} %pad_maximum_fusion.9), channel_id=1, source_target_pairs={{0,1},{1,0},{2,3},{3,2},{4,5},{5,4},{6,7},{7,6},{8,9},{9,8},{10,11... | collective-permute-start | bytes 3145736 | tf_op jit(solution)/shard_map/ppermute | solution.py:21
  90.7 19.7 %collective-permute-start.14 = (bf16[4,32,2560]{2,1,0:T(8,128)(2,1)S(1)}, bf16[4,32,2560]{2,1,0:T(8,128)(2,1)}, u32[]{:S(2)}, u32[]{:S(2)}) collective-permute-start(bf16[4,32,2560]{2,1,0:T(8,128)(2,1)S(1)} %get-tuple-element.151.refs_0_), channel_id=1, source_target_pairs={{0,2},{2,0},{1,3},{3,1},{4,6},{6,4},{5,7},{7,5},{8,10},{10,8},{9,1... | collective-permute-start | bytes 1966088 | tf_op jit(solution)/shard_map/ppermute | solution.py:25
  91.9 18.5 %collective-permute-start.15 = (bf16[4,32,2560]{2,1,0:T(8,128)(2,1)S(1)}, bf16[4,32,2560]{2,1,0:T(8,128)(2,1)}, u32[]{:S(2)}, u32[]{:S(2)}) collective-permute-start(bf16[4,32,2560]{2,1,0:T(8,128)(2,1)S(1)} %get-tuple-element.152.refs_1_), channel_id=1, source_target_pairs={{0,4},{4,0},{1,5},{5,1},{2,6},{6,2},{3,7},{7,3},{8,12},{12,8},{9,1... | collective-permute-start | bytes 1966088 | tf_op jit(solution)/shard_map/ppermute | solution.py:29
  112.7 38.3 %collective-permute-start.16 = (bf16[2,4,32,2560]{3,2,1,0:T(8,128)(2,1)}, bf16[2,4,32,2560]{3,2,1,0:T(8,128)(2,1)}, u32[]{:S(2)}, u32[]{:S(2)}) collective-permute-start(bf16[2,4,32,2560]{3,2,1,0:T(8,128)(2,1)} %pad_maximum_fusion.6), channel_id=1, source_target_pairs={{0,4},{4,0},{1,5},{5,1},{2,6},{6,2},{3,7},{7,3},{8,12},{12,8},{9,1... | collective-permute-start | bytes 3932168 | tf_op jit(solution)/shard_map/ppermute | solution.py:29
  116.4 42.3 %collective-permute-start.18 = (bf16[2,4,32,2560]{3,2,1,0:T(8,128)(2,1)}, bf16[2,4,32,2560]{3,2,1,0:T(8,128)(2,1)}, u32[]{:S(2)}, u32[]{:S(2)}) collective-permute-start(bf16[2,4,32,2560]{3,2,1,0:T(8,128)(2,1)} %pad_maximum_fusion.7), channel_id=1, source_target_pairs={{0,2},{2,0},{1,3},{3,1},{4,6},{6,4},{5,7},{7,5},{8,10},{10,8},{9,1... | collective-permute-start | bytes 3932168 | tf_op jit(solution)/shard_map/ppermute | solution.py:25
  161.2 7.6 %collective-permute-start.19 = (bf16[16,64,512]{2,1,0:T(8,128)(2,1)S(1)}, bf16[16,64,512]{2,1,0:T(8,128)(2,1)S(1)}, u32[]{:S(2)}, u32[]{:S(2)}) collective-permute-start(bf16[16,64,512]{2,1,0:T(8,128)(2,1)S(1)} %bitcast.171), channel_id=1, source_target_pairs={{0,1},{1,0},{2,3},{3,2},{4,5},{5,4},{6,7},{7,6},{8,9},{9,8},{10,11... | collective-permute-start | bytes 3145736 | tf_op jit(solution)/shard_map/ppermute | solution.py:21
  175.2 14.6 %collective-permute-start.21 = (bf16[256,1152]{1,0:T(8,128)(2,1)S(1)}, bf16[256,1152]{1,0:T(8,128)(2,1)}, u32[]{:S(2)}, u32[]{:S(2)}) collective-permute-start(bf16[256,1152]{1,0:T(8,128)(2,1)S(1)} %copy-done.71), channel_id=1, source_target_pairs={{0,2},{2,0},{1,3},{3,1},{4,6},{6,4},{5,7},{7,5},{8,10},{10,8},{9,1... | collective-permute-start | bytes 1769480 | tf_op jit(solution)/shard_map/ppermute | solution.py:25
  220.4 24.9 %collective-permute-start.24 = (bf16[4,2,64,1024]{3,2,1,0:T(8,128)(2,1)S(1)}, bf16[4,2,64,1024]{3,2,1,0:T(8,128)(2,1)S(1)}, u32[]{:S(2)}, u32[]{:S(2)}) collective-permute-start(bf16[4,2,64,1024]{3,2,1,0:T(8,128)(2,1)S(1)} %get-tuple-element.171), channel_id=1, source_target_pairs={{0,2},{2,0},{1,3},{3,1},{4,6},{6,4},{5,7},{7,5},{8,10},{10,8},{9,1... | collective-permute-start | bytes 3145736 | tf_op jit(solution)/shard_map/ppermute | solution.py:25
  222.0 24.5 %collective-permute-start.25 = (bf16[4,2,64,1024]{3,2,1,0:T(8,128)(2,1)S(1)}, bf16[4,2,64,1024]{3,2,1,0:T(8,128)(2,1)S(1)}, u32[]{:S(2)}, u32[]{:S(2)}) collective-permute-start(bf16[4,2,64,1024]{3,2,1,0:T(8,128)(2,1)S(1)} %get-tuple-element.172), channel_id=1, source_target_pairs={{0,4},{4,0},{1,5},{5,1},{2,6},{6,2},{3,7},{7,3},{8,12},{12,8},{9,1... | collective-permute-start | bytes 3145736 | tf_op jit(solution)/shard_map/ppermute | solution.py:29
  246.4 14.7 %collective-permute-start.26 = (bf16[512,1024]{1,0:T(8,128)(2,1)}, bf16[512,1024]{1,0:T(8,128)(2,1)}, u32[]{:S(2)}, u32[]{:S(2)}) collective-permute-start(bf16[512,1024]{1,0:T(8,128)(2,1)} %slice.201), channel_id=1, source_target_pairs={{0,1},{1,0},{2,3},{3,2},{4,5},{5,4},{6,7},{7,6},{8,9},{9,8},{10,11... | collective-permute-start | bytes 3145736 | tf_op jit(solution)/shard_map/ppermute | solution.py:21
  261.1 49.6 %collective-permute-start.31 = (bf16[4,2,32,2048]{3,2,1,0:T(8,128)(2,1)}, bf16[4,2,32,2048]{3,2,1,0:T(8,128)(2,1)}, u32[]{:S(2)}, u32[]{:S(2)}) collective-permute-start(bf16[4,2,32,2048]{3,2,1,0:T(8,128)(2,1)} %get-tuple-element.194), channel_id=1, source_target_pairs={{0,4},{4,0},{1,5},{5,1},{2,6},{6,2},{3,7},{7,3},{8,12},{12,8},{9,1... | collective-permute-start | bytes 3145736 | tf_op jit(solution)/shard_map/ppermute | solution.py:29
  263.8 46.9 %collective-permute-start.30 = (bf16[4,2,32,2048]{3,2,1,0:T(8,128)(2,1)}, bf16[4,2,32,2048]{3,2,1,0:T(8,128)(2,1)}, u32[]{:S(2)}, u32[]{:S(2)}) collective-permute-start(bf16[4,2,32,2048]{3,2,1,0:T(8,128)(2,1)} %get-tuple-element.193), channel_id=1, source_target_pairs={{0,2},{2,0},{1,3},{3,1},{4,6},{6,4},{5,7},{7,5},{8,10},{10,8},{9,1... | collective-permute-start | bytes 3145736 | tf_op jit(solution)/shard_map/ppermute | solution.py:25
  270.0 7.6 %collective-permute-start.27 = (bf16[512,512]{1,0:T(8,128)(2,1)}, bf16[512,512]{1,0:T(8,128)(2,1)}, u32[]{:S(2)}, u32[]{:S(2)}) collective-permute-start(bf16[512,512]{1,0:T(8,128)(2,1)} %get-tuple-element.181), channel_id=1, source_target_pairs={{0,1},{1,0},{2,3},{3,2},{4,5},{5,4},{6,7},{7,6},{8,9},{9,8},{10,11... | collective-permute-start | bytes 1572872 | tf_op jit(solution)/shard_map/ppermute | solution.py:21
  270.3 27.0 %collective-permute-start.28 = (bf16[4,64,1024]{2,1,0:T(8,128)(2,1)}, bf16[4,64,1024]{2,1,0:T(8,128)(2,1)S(1)}, u32[]{:S(2)}, u32[]{:S(2)}) collective-permute-start(bf16[4,64,1024]{2,1,0:T(8,128)(2,1)} %get-tuple-element.185), channel_id=1, source_target_pairs={{0,4},{4,0},{1,5},{5,1},{2,6},{6,2},{3,7},{7,3},{8,12},{12,8},{9,1... | collective-permute-start | bytes 1572872 | tf_op jit(solution)/shard_map/ppermute | solution.py:29
  271.7 28.4 %collective-permute-start.29 = (bf16[4,64,1024]{2,1,0:T(8,128)(2,1)S(1)}, bf16[4,64,1024]{2,1,0:T(8,128)(2,1)S(1)}, u32[]{:S(2)}, u32[]{:S(2)}) collective-permute-start(bf16[4,64,1024]{2,1,0:T(8,128)(2,1)S(1)} %copy-done.46), channel_id=1, source_target_pairs={{0,2},{2,0},{1,3},{3,1},{4,6},{6,4},{5,7},{7,5},{8,10},{10,8},{9,1... | collective-permute-start | bytes 1572872 | tf_op jit(solution)/shard_map/ppermute | solution.py:25
  301.9 24.6 %collective-permute-start.32 = (bf16[16,32,1024]{2,1,0:T(8,128)(2,1)}, bf16[16,32,1024]{2,1,0:T(8,128)(2,1)}, u32[]{:S(2)}, u32[]{:S(2)}) collective-permute-start(bf16[16,32,1024]{2,1,0:T(8,128)(2,1)} %get-tuple-element.202), channel_id=1, source_target_pairs={{0,1},{1,0},{2,3},{3,2},{4,5},{5,4},{6,7},{7,6},{8,9},{9,8},{10,11... | collective-permute-start | bytes 3145736 | tf_op jit(solution)/shard_map/ppermute | solution.py:21
  320.9 18.5 %collective-permute-start.34 = (bf16[4,32,2048]{2,1,0:T(8,128)(2,1)S(1)}, bf16[4,32,2048]{2,1,0:T(8,128)(2,1)S(1)}, u32[]{:S(2)}, u32[]{:S(2)}) collective-permute-start(bf16[4,32,2048]{2,1,0:T(8,128)(2,1)S(1)} %get-tuple-element.206), channel_id=1, source_target_pairs={{0,4},{4,0},{1,5},{5,1},{2,6},{6,2},{3,7},{7,3},{8,12},{12,8},{9,1... | collective-permute-start | bytes 1572872 | tf_op jit(solution)/shard_map/ppermute | solution.py:29
  329.1 13.3 %collective-permute-start.35 = (bf16[4,32,2048]{2,1,0:T(8,128)(2,1)S(1)}, bf16[4,32,2048]{2,1,0:T(8,128)(2,1)S(1)}, u32[]{:S(2)}, u32[]{:S(2)}) collective-permute-start(bf16[4,32,2048]{2,1,0:T(8,128)(2,1)S(1)} %get-tuple-element.207), channel_id=1, source_target_pairs={{0,2},{2,0},{1,3},{3,1},{4,6},{6,4},{5,7},{7,5},{8,10},{10,8},{9,1... | collective-permute-start | bytes 1572872 | tf_op jit(solution)/shard_map/ppermute | solution.py:25
  343.2 8.1 %collective-permute-start.36 = (bf16[512,1024]{1,0:T(8,128)(2,1)}, bf16[512,1024]{1,0:T(8,128)(2,1)}, u32[]{:S(2)}, u32[]{:S(2)}) collective-permute-start(bf16[512,1024]{1,0:T(8,128)(2,1)} %slice.200), channel_id=1, source_target_pairs={{0,1},{1,0},{2,3},{3,2},{4,5},{5,4},{6,7},{7,6},{8,9},{9,8},{10,11... | collective-permute-start | bytes 3145736 | tf_op jit(solution)/shard_map/ppermute | solution.py:21
  345.6 70.8 %reduce-scatter.3.cloned.1.call-start = ((), (), s32[]{:S(2)}) async-start(), calls=%async_computation.3 | async-start | bytes 1310720 | tf_op jit(solution)/shard_map/reduce_scatter | solution.py:362
  346.1 28.9 %collective-permute-start.33 = (bf16[4,2,32,2048]{3,2,1,0:T(8,128)(2,1)}, bf16[4,2,32,2048]{3,2,1,0:T(8,128)(2,1)S(1)}, u32[]{:S(2)}, u32[]{:S(2)}) collective-permute-start(bf16[4,2,32,2048]{3,2,1,0:T(8,128)(2,1)} %get-tuple-element.204), channel_id=1, source_target_pairs={{0,2},{2,0},{1,3},{3,1},{4,6},{6,4},{5,7},{7,5},{8,10},{10,8},{9,1... | collective-permute-start | bytes 3145736 | tf_op jit(solution)/shard_map/ppermute | solution.py:25
  346.2 28.8 %collective-permute-start.37 = (bf16[4,2,32,2048]{3,2,1,0:T(8,128)(2,1)}, bf16[4,2,32,2048]{3,2,1,0:T(8,128)(2,1)S(1)}, u32[]{:S(2)}, u32[]{:S(2)}) collective-permute-start(bf16[4,2,32,2048]{3,2,1,0:T(8,128)(2,1)} %copy-done.44), channel_id=1, source_target_pairs={{0,4},{4,0},{1,5},{5,1},{2,6},{6,2},{3,7},{7,3},{8,12},{12,8},{9,1... | collective-permute-start | bytes 3145736 | tf_op jit(solution)/shard_map/ppermute | solution.py:29
  356.9 6.7 %collective-permute-start.47 = (f32[64,128]{1,0:T(8,128)S(1)}, f32[64,128]{1,0:T(8,128)S(1)}, u32[]{:S(2)}, u32[]{:S(2)}) collective-permute-start(f32[64,128]{1,0:T(8,128)S(1)} %get-tuple-element.265), channel_id=1, source_target_pairs={{0,8},{8,16},{16,24},{24,0},{1,9},{9,17},{17,25},{25,1},{2,10},{10... | collective-permute-start | bytes 98312 | tf_op jit(solution)/shard_map/ppermute | solution.py:34
  357.0 9.2 %collective-permute-start.48 = (f32[64,128]{1,0:T(8,128)S(1)}, f32[64,128]{1,0:T(8,128)S(1)}, u32[]{:S(2)}, u32[]{:S(2)}) collective-permute-start(f32[64,128]{1,0:T(8,128)S(1)} %get-tuple-element.265), channel_id=1, source_target_pairs={{0,16},{8,24},{16,0},{24,8},{1,17},{9,25},{17,1},{25,9},{2,18},{10... | collective-permute-start | bytes 98312 | tf_op jit(solution)/shard_map/ppermute | solution.py:34
  362.2 8.1 %collective-permute-start.49 = (f32[64,128]{1,0:T(8,128)S(1)}, f32[64,128]{1,0:T(8,128)S(1)}, u32[]{:S(2)}, u32[]{:S(2)}) collective-permute-start(f32[64,128]{1,0:T(8,128)S(1)} %get-tuple-element.265), channel_id=1, source_target_pairs={{0,24},{8,0},{16,8},{24,16},{1,25},{9,1},{17,9},{25,17},{2,26},{10... | collective-permute-start | bytes 98312 | tf_op jit(solution)/shard_map/ppermute | solution.py:34
  370.3 7.1 %collective-permute-start.50 = (f32[4,64,128]{2,1,0:T(8,128)S(1)}, f32[4,64,128]{2,1,0:T(8,128)S(1)}, u32[]{:S(2)}, u32[]{:S(2)}) collective-permute-start(f32[4,64,128]{2,1,0:T(8,128)S(1)} %bitcast_dynamic-update-slice_fusion), channel_id=1, source_target_pairs={{0,2},{2,0},{1,3},{3,1},{4,6},{6,4},{5,7},{7,5},{8,10},{10,8},{9,1... | collective-permute-start | bytes 393224 | tf_op jit(solution)/shard_map/ppermute | solution.py:25
  376.3 12.9 %collective-permute-start.38 = (bf16[4,32,2048]{2,1,0:T(8,128)(2,1)S(1)}, bf16[4,32,2048]{2,1,0:T(8,128)(2,1)S(1)}, u32[]{:S(2)}, u32[]{:S(2)}) collective-permute-start(bf16[4,32,2048]{2,1,0:T(8,128)(2,1)S(1)} %get-tuple-element.220), channel_id=1, source_target_pairs={{0,4},{4,0},{1,5},{5,1},{2,6},{6,2},{3,7},{7,3},{8,12},{12,8},{9,1... | collective-permute-start | bytes 1572872 | tf_op jit(solution)/shard_map/ppermute | solution.py:29
  377.2 12.7 %collective-permute-start.39 = (bf16[4,32,2048]{2,1,0:T(8,128)(2,1)S(1)}, bf16[4,32,2048]{2,1,0:T(8,128)(2,1)S(1)}, u32[]{:S(2)}, u32[]{:S(2)}) collective-permute-start(bf16[4,32,2048]{2,1,0:T(8,128)(2,1)S(1)} %get-tuple-element.221), channel_id=1, source_target_pairs={{0,2},{2,0},{1,3},{3,1},{4,6},{6,4},{5,7},{7,5},{8,10},{10,8},{9,1... | collective-permute-start | bytes 1572872 | tf_op jit(solution)/shard_map/ppermute | solution.py:25
  377.4 17.4 %collective-permute-start.51 = (f32[4,2,64,128]{3,2,1,0:T(8,128)S(1)}, f32[4,2,64,128]{3,2,1,0:T(8,128)S(1)}, u32[]{:S(2)}, u32[]{:S(2)}) collective-permute-start(f32[4,2,64,128]{3,2,1,0:T(8,128)S(1)} %pad_maximum_fusion.19), channel_id=1, source_target_pairs={{0,4},{4,0},{1,5},{5,1},{2,6},{6,2},{3,7},{7,3},{8,12},{12,8},{9,1... | collective-permute-start | bytes 786440 | tf_op jit(solution)/shard_map/ppermute | solution.py:29
  390.7 11.8 %collective-permute-start.43 = (bf16[256,1024]{1,0:T(8,128)(2,1)}, bf16[256,1024]{1,0:T(8,128)(2,1)}, u32[]{:S(2)}, u32[]{:S(2)}) collective-permute-start(bf16[256,1024]{1,0:T(8,128)(2,1)} %slice.155), channel_id=1, source_target_pairs={{0,2},{2,0},{1,3},{3,1},{4,6},{6,4},{5,7},{7,5},{8,10},{10,8},{9,1... | collective-permute-start | bytes 1572872 | tf_op jit(solution)/shard_map/ppermute | solution.py:25
  392.7 21.0 %collective-permute-start.44 = (bf16[256,1024]{1,0:T(8,128)(2,1)}, bf16[256,1024]{1,0:T(8,128)(2,1)}, u32[]{:S(2)}, u32[]{:S(2)}) collective-permute-start(bf16[256,1024]{1,0:T(8,128)(2,1)} %slice.203), channel_id=1, source_target_pairs={{0,2},{2,0},{1,3},{3,1},{4,6},{6,4},{5,7},{7,5},{8,10},{10,8},{9,1... | collective-permute-start | bytes 1572872 | tf_op jit(solution)/shard_map/ppermute | solution.py:25
  398.6 27.6 %collective-permute-start.40 = (bf16[64,2048]{1,0:T(8,128)(2,1)S(1)}, bf16[64,2048]{1,0:T(8,128)(2,1)S(1)}, u32[]{:S(2)}, u32[]{:S(2)}) collective-permute-start(bf16[64,2048]{1,0:T(8,128)(2,1)S(1)} %get-tuple-element.225), channel_id=1, source_target_pairs={{0,8},{8,16},{16,24},{24,0},{1,9},{9,17},{17,25},{25,1},{2,10},{10... | collective-permute-start | bytes 786440 | tf_op jit(solution)/shard_map/ppermute | solution.py:34
  398.7 27.5 %collective-permute-start.41 = (bf16[64,2048]{1,0:T(8,128)(2,1)S(1)}, bf16[64,2048]{1,0:T(8,128)(2,1)}, u32[]{:S(2)}, u32[]{:S(2)}) collective-permute-start(bf16[64,2048]{1,0:T(8,128)(2,1)S(1)} %get-tuple-element.226), channel_id=1, source_target_pairs={{0,16},{8,24},{16,0},{24,8},{1,17},{9,25},{17,1},{25,9},{2,18},{10... | collective-permute-start | bytes 786440 | tf_op jit(solution)/shard_map/ppermute | solution.py:34
  399.3 26.9 %collective-permute-start.42 = (bf16[64,2048]{1,0:T(8,128)(2,1)S(1)}, bf16[64,2048]{1,0:T(8,128)(2,1)}, u32[]{:S(2)}, u32[]{:S(2)}) collective-permute-start(bf16[64,2048]{1,0:T(8,128)(2,1)S(1)} %get-tuple-element.227), channel_id=1, source_target_pairs={{0,24},{8,0},{16,8},{24,16},{1,25},{9,1},{17,9},{25,17},{2,26},{10... | collective-permute-start | bytes 786440 | tf_op jit(solution)/shard_map/ppermute | solution.py:34
  417.7 6.8 %collective-permute-start.45 = (f32[32,16,128]{2,1,0:T(8,128)S(1)}, f32[32,16,128]{2,1,0:T(8,128)S(1)}, u32[]{:S(2)}, u32[]{:S(2)}) collective-permute-start(f32[32,16,128]{2,1,0:T(8,128)S(1)} %dynamic-slice_bitcast_fusion.4), channel_id=1, source_target_pairs={{0,1},{1,0},{2,3},{3,2},{4,5},{5,4},{6,7},{7,6},{8,9},{9,8},{10,11... | collective-permute-start | bytes 786440 | tf_op jit(solution)/shard_map/ppermute | solution.py:21
  (91 other events, 470.3 us)
Sparse Core Ops, SparseCore 0:
  62.7 104.6 all-gather.1
  345.7 30.9 reduce-scatter.4
  379.2 25.4 reduce-scatter.2
